TPU v7x, 512 devices: a whole 4x4x16 slice. The times are simulated.
512 devices in a mesh: gx: 8 (over z_hi, core), gy: 16 (over z_lo, x), gz: 4 (over y).
Axes of the slice: x: 4, y: 4, z: 16 (z_hi: 4, z_lo: 4; z = z_hi * 4 + z_lo), core: 2. Of those that a mesh axis runs over, the one named last changes fastest.
Arguments:
- cr_init: float32 [64, 16, 32, 2048], P(None, 'gz', 'gx', 'gy'), may hold values from 0.1 to 3
- gas: float32 [16, 32, 2048], P('gz', 'gx', 'gy'), may hold values from 0.05 to 3
- diff_coeff: float32 [64], replicated, may hold values from 0.06 to 0.14
- loss_coeff: float32 [64], replicated, may hold values from 0.05 to 0.3
- pi0_table: float32 [96, 64], replicated, may hold values from -0.75 to 0.75
- los_weight: bfloat16 [4, 8, 16, 7, 2048, 128], P('gz', 'gx', 'gy'), may hold values from -0.125 to 0.125
- slot_owner: int32 [4, 8, 16, 7, 1], P('gz', 'gx', 'gy'), may hold values from 0 to 15; in each aligned block of 7 rows (0 to 6, 7 to 13, ..., all dimensions but the last counted through in order) at most 2 rows name the same one
- slot_block: int32 [4, 8, 16, 7], P('gz', 'gx', 'gy'), may hold values from 0 to 3
Outputs:
- cr_final: float32 [64, 16, 32, 2048], P(None, 'gz', 'gx', 'gy')
- sky: float32 [4, 8, 64, 96, 128], P('gz', 'gx', 'gy')
Inputs may be any that keep to these rules, and one draw needn't show every extreme that they name: `slot_owner`: at most 2 of the 7 weight blocks of one device name the same owner, and some device names one owner exactly 2 times.
All inputs are finite; a program needn't handle non-finite values.
Results may differ from a plain program's by a relative error of at most 0.0029.
Values sent between devices are 32-bit elements; how exact they have to be, the bound alone decides.
No kernel may reach another device: no remote copies, remote signals or barrier semaphores. Data moves between devices by JAX's collectives and lax.ppermute only.
A program may use at most 64 MiB of HBM per device.

v0:
```python
import jax
import jax.numpy as jnp
from jax import lax
from jax.sharding import PartitionSpec as P

STEPS = 2
BO = 4


def extended(cells, sides, width):
    for axis, dim in sides:
        count = lax.axis_size(axis)
        ends = count - 1
        head = lax.slice_in_dim(cells, 0, width, axis=dim)
        tail = lax.slice_in_dim(cells, cells.shape[dim] - width, cells.shape[dim], axis=dim)
        cells = jnp.concatenate(
            [
                lax.ppermute(tail, axis, [(i, (i + 1) % count) for i in range(ends)]),
                cells,
                lax.ppermute(head, axis, [((i + 1) % count, i) for i in range(ends)]),
            ],
            axis=dim,
        )
    return cells


def advance(padded, diffusion, losses):
    center = padded[:, 1:-1, 1:-1, 1:-1]
    beside = padded[:, 2:, 1:-1, 1:-1] + padded[:, :-2, 1:-1, 1:-1]
    beside = beside + padded[:, 1:-1, 2:, 1:-1] + padded[:, 1:-1, :-2, 1:-1]
    beside = beside + padded[:, 1:-1, 1:-1, 2:] + padded[:, 1:-1, 1:-1, :-2]
    loss_flux = losses[:, None, None, None] * center
    from_above = jnp.concatenate([loss_flux[1:], jnp.zeros_like(loss_flux[:1])], axis=0)
    return (
        center + diffusion[:, None, None, None] * (beside - 6.0 * center) + from_above - loss_flux
    )


def body(cr_init, gas, diff_coeff, loss_coeff, pi0_table, los_weight, slot_owner, slot_block):
    density = cr_init
    for step_index in range(STEPS):
        padded = extended(density, (("gx", 2), ("gy", 3), ("gz", 1)), 1)
        density = advance(padded, diff_coeff, loss_coeff)
    source = jnp.einsum("ge,ezxy->gzxy", pi0_table, density, precision=lax.Precision.HIGHEST)
    emissivity = (gas[None] * source).astype(jnp.bfloat16)
    flat_cells = emissivity.reshape(emissivity.shape[0], -1)
    weights = los_weight[0, 0, 0]
    contrib = jnp.einsum("gc,scp->sgp", flat_cells, weights, preferred_element_type=jnp.float32)
    gamma_count = contrib.shape[1]
    pixel_count = contrib.shape[2]
    owners = slot_owner[0, 0, 0, :, 0]
    blocks = slot_block[0, 0, 0]
    owner_count = lax.axis_size("gy")
    target = owners * BO + blocks
    select = (target[None, :] == jnp.arange(owner_count * BO)[:, None]).astype(jnp.float32)
    terms = jnp.einsum("rs,sgp->rgp", select, contrib, precision=lax.Precision.HIGHEST)
    sky = lax.psum_scatter(terms, "gy", scatter_dimension=0, tiled=True)
    return (density, sky.reshape(1, 1, BO, gamma_count, pixel_count))


def solution(mesh):
    in_specs = (
        P(None, "gz", "gx", "gy"),
        P("gz", "gx", "gy"),
        P(),
        P(),
        P(),
        P("gz", "gx", "gy", None, None, None),
        P("gz", "gx", "gy", None, None),
        P("gz", "gx", "gy", None),
    )
    out_specs = (P(None, "gz", "gx", "gy"), P("gz", "gx", "gy", None, None))
    return jax.shard_map(body, mesh=mesh, in_specs=in_specs, out_specs=out_specs, check_vma=False)
```

profile of v0, /device:TPU:8, one launch (start us, length us, event | category | flops | bytes accessed | tf_op | source)
XLA Modules:
  0.0 236.1 jit_solution(16487076031144541449)
XLA Ops:
  7.2 0.0 copy-start
  7.2 0.0 reduce-scatter.2.cloned.1.call-start
  7.2 1.4 copy.38
  8.7 0.0 copy-start.3
  8.7 1.8 collective-permute-start
  10.5 1.3 collective-permute-start.1
  11.8 9.1 %collective-permute-done.1 = f32[64,4,1,128]{0,1,3,2:T(4,128)S(1)} collective-permute-done((f32[64,4,1,128]{0,1,3,2:T(4,128)S(1)}, f32[64,4,1,128]{0,1,3,2:T(4,128)S(1)}, u32[]{:S(2)}, u32[]{:S(2)}) %collective-permute-start.1) | collective-permute-done | bytes 131104 | tf_op jit(solution)/shard_map/ppermute | solution.py:20
  20.9 1.3 collective-permute-start.3
  22.2 4.5 %collective-permute-start.2 = (f32[64,4,6,1]{0,1,3,2:T(4,128)S(1)}, f32[64,4,6,1]{0,1,3,2:T(4,128)S(1)}, u32[]{:S(2)}, u32[]{:S(2)}) collective-permute-start(f32[64,4,6,1]{0,1,3,2:T(4,128)S(1)} %get-tuple-element.19), channel_id=1, source_target_pairs={{0,4},{4,8},{8,12},{12,16},{16,20},{20,24},{24,28},{28,32},{32,36}... | collective-permute-start | bytes 18440 | tf_op jit(solution)/shard_map/ppermute | solution.py:18
  26.8 1.4 collective-permute-done.2
  28.1 1.3 pad_maximum_fusion.45
  29.5 0.4 copy.31
  29.9 1.1 copy.33
  31.0 3.5 %collective-permute-start.5 = (f32[64,1,6,130]{3,0,2,1:T(8,128)}, f32[64,1,6,130]{3,0,2,1:T(8,128)S(1)}, u32[]{:S(2)}, u32[]{:S(2)}) collective-permute-start(f32[64,1,6,130]{3,0,2,1:T(8,128)} %copy.33), channel_id=1, source_target_pairs={{0,1},{1,2},{2,3},{4,5},{5,6},{6,7},{8,9},{9,10},{10,11},{12,13},{... | collective-permute-start | bytes 599048 | tf_op jit(solution)/shard_map/ppermute | solution.py:18
  34.4 2.4 %collective-permute-start.4 = (f32[64,1,6,130]{3,0,2,1:T(8,128)S(1)}, f32[64,1,6,130]{3,0,2,1:T(8,128)S(1)}, u32[]{:S(2)}, u32[]{:S(2)}) collective-permute-start(f32[64,1,6,130]{3,0,2,1:T(8,128)S(1)} %copy.31), channel_id=1, source_target_pairs={{1,0},{2,1},{3,2},{5,4},{6,5},{7,6},{9,8},{10,9},{11,10},{13,12},{... | collective-permute-start | bytes 599048 | tf_op jit(solution)/shard_map/ppermute | solution.py:20
  36.8 0.2 broadcast_multiply_fusion.1
  37.0 1.6 slice.118
  38.7 2.2 collective-permute-done.5
  40.8 1.1 copy.34
  41.9 2.2 collective-permute-done.4
  44.1 1.1 copy.32
  45.2 5.5 %broadcast_multiply_fusion = (f32[64,4,4,128]{0,1,3,2:T(4,128)S(1)}, f32[64,4,4,128]{0,1,3,2:T(4,128)S(1)}) fusion(f32[64]{0:T(128)S(1)} %copy-done.3, f32[64,4,4,128]{0,1,3,2:T(4,128)S(1)} %copy.38, f32[63,4,4,128]{0,1,3,2:T(4,128)} %slice.118, f32[64,4,1,128]{0,1,3,2:T(4,128)} %copy-done.1, f32[64,4,1,128]{0,1,3,2:T(4,128)S(1)} %collective-permute-done, ...), kind=kLoop, calls=%fused_computation.63 | loop fusion | flops 4063232 | bytes 2763264 | tf_op jit(solution)/shard_map/mul | solution.py:32
  50.8 16.5 %collective-permute-start.6 = (f32[64,4,1,128]{0,1,3,2:T(4,128)S(1)}, f32[64,4,1,128]{0,1,3,2:T(4,128)S(1)}, u32[]{:S(2)}, u32[]{:S(2)}) collective-permute-start(f32[64,4,1,128]{0,1,3,2:T(4,128)S(1)} %get-tuple-element.20), channel_id=1, source_target_pairs={{0,64},{64,128},{128,192},{192,256},{256,320},{320,384},{384,448},... | collective-permute-start | bytes 393224 | tf_op jit(solution)/shard_map/ppermute | solution.py:18
  67.3 1.3 collective-permute-start.7
  68.6 4.0 %collective-permute-done.7 = f32[64,4,1,128]{0,1,3,2:T(4,128)S(1)} collective-permute-done((f32[64,4,1,128]{0,1,3,2:T(4,128)S(1)}, f32[64,4,1,128]{0,1,3,2:T(4,128)S(1)}, u32[]{:S(2)}, u32[]{:S(2)}) %collective-permute-start.7) | collective-permute-done | bytes 131104 | tf_op jit(solution)/shard_map/ppermute | solution.py:20
  72.6 1.3 collective-permute-start.9
  73.9 4.8 %collective-permute-start.8 = (f32[64,4,6,1]{0,1,3,2:T(4,128)S(1)}, f32[64,4,6,1]{0,1,3,2:T(4,128)S(1)}, u32[]{:S(2)}, u32[]{:S(2)}) collective-permute-start(f32[64,4,6,1]{0,1,3,2:T(4,128)S(1)} %get-tuple-element.17), channel_id=1, source_target_pairs={{0,4},{4,8},{8,12},{12,16},{16,20},{20,24},{24,28},{28,32},{32,36}... | collective-permute-start | bytes 18440 | tf_op jit(solution)/shard_map/ppermute | solution.py:18
  78.8 1.4 collective-permute-done.8
  80.2 2.0 pad_maximum_fusion.40
  82.2 1.9 copy.40
  84.1 1.1 copy.42
  85.2 3.2 %collective-permute-start.11 = (f32[64,1,6,130]{3,0,2,1:T(8,128)}, f32[64,1,6,130]{3,0,2,1:T(8,128)S(1)}, u32[]{:S(2)}, u32[]{:S(2)}) collective-permute-start(f32[64,1,6,130]{3,0,2,1:T(8,128)} %copy.42), channel_id=1, source_target_pairs={{0,1},{1,2},{2,3},{4,5},{5,6},{6,7},{8,9},{9,10},{10,11},{12,13},{... | collective-permute-start | bytes 599048 | tf_op jit(solution)/shard_map/ppermute | solution.py:18
  88.3 2.9 %collective-permute-start.10 = (f32[64,1,6,130]{3,0,2,1:T(8,128)}, f32[64,1,6,130]{3,0,2,1:T(8,128)S(1)}, u32[]{:S(2)}, u32[]{:S(2)}) collective-permute-start(f32[64,1,6,130]{3,0,2,1:T(8,128)} %copy.40), channel_id=1, source_target_pairs={{1,0},{2,1},{3,2},{5,4},{6,5},{7,6},{9,8},{10,9},{11,10},{13,12},{... | collective-permute-start | bytes 599048 | tf_op jit(solution)/shard_map/ppermute | solution.py:20
  91.3 1.6 slice.121
  92.9 2.2 collective-permute-done.11
  95.0 0.5 copy.43
  95.5 2.7 %collective-permute-done.10 = f32[64,1,6,130]{3,0,2,1:T(8,128)S(1)} collective-permute-done((f32[64,1,6,130]{3,0,2,1:T(8,128)}, f32[64,1,6,130]{3,0,2,1:T(8,128)S(1)}, u32[]{:S(2)}, u32[]{:S(2)}) %collective-permute-start.10) | collective-permute-done | bytes 199712 | tf_op jit(solution)/shard_map/ppermute | solution.py:20
  98.2 1.1 copy.41
  99.3 5.4 %fusion.12 = f32[64,4,4,128]{0,1,3,2:T(4,128)S(1)} fusion(f32[64,4,4,128]{0,1,3,2:T(4,128)S(1)} %get-tuple-element.11, f32[64,4,6,1]{0,1,3,2:T(4,128)S(1)} %collective-permute-done.8, f32[64,4,1,128]{0,1,3,2:T(4,128)S(1)} %collective-permute-done.7, f32[64,4,1,128]{0,1,3,2:T(4,128)S(1)} %collective-permute-done.6, ...), kind=kLoop, calls=%fused_computation.12 | loop fusion | flops 3932160 | bytes 2238976 | tf_op jit(solution)/shard_map/sub | solution.py:35
  104.8 1.2 fusion.3
  106.0 0.2 copy.45
  106.2 0.3 reshape.28
  106.5 2.7 %fusion.4 = f32[7,96,128]{2,1,0:T(8,128)S(1)} fusion(bf16[96,2048,1]{1,0,2:T(8,128)(2,1)S(1)} %reshape.28, bf16[1,1,1,7,2048,128]{5,4,3,2,1,0:T(8,128)(2,1)} %param.13), kind=kOutput, calls=%fused_computation.5 | convolution fusion | flops 352321536 | bytes 4407296 | tf_op jit(solution)/shard_map/gc,scp->sgp/dot_general | solution.py:48
  109.3 1.5 fusion.28
  110.8 3.4 %copy.47 = f32[64,96,128]{2,1,0:T(8,128)} copy(f32[64,96,128]{2,0,1:T(8,128)S(1)} %fusion.28) | data formatting | bytes 6291456 | tf_op jit(solution)/shard_map/rs,sgp->rgp/dot_general | solution.py:56
  114.2 0.0 reduce-scatter.2.cloned.1.call-update
  114.3 1.2 copy.48
  115.4 113.8 %reduce-scatter.2.cloned.1.call-done = f32[4,96,128]{2,1,0:T(8,128)} async-done(((f32[64,96,128]{2,1,0:T(8,128)}), f32[4,96,128]{2,1,0:T(8,128)}) %reduce-scatter.2.cloned.1.call-update) | async-done | bytes 196624 | tf_op jit(solution)/shard_map/reduce_scatter | solution.py:57
  (21 shorter events, 0.1 us)
Async XLA Ops:
  7.2 97.6 %copy-start = (f32[96,64]{0,1:T(8,128)S(1)}, f32[96,64]{0,1:T(8,128)}, u32[]{:S(2)}) copy-start(f32[96,64]{0,1:T(8,128)} %param.12) | copy-start | bytes 73732
  7.2 222.0 %reduce-scatter.2.cloned.1.call-start = ((), (), s32[]{:S(2)}) async-start(), calls=%async_computation.1 | async-start | bytes 3342336 | tf_op jit(solution)/shard_map/reduce_scatter | solution.py:57
  8.7 28.2 %copy-start.3 = (f32[64]{0:T(128)S(1)}, f32[64]{0:T(128)}, u32[]{:S(2)}) copy-start(f32[64]{0:T(128)} %param.11) | copy-start | bytes 772
  8.7 3.1 %collective-permute-start = (f32[64,4,1,128]{0,1,3,2:T(4,128)S(1)}, f32[64,4,1,128]{0,1,3,2:T(4,128)S(1)}, u32[]{:S(2)}, u32[]{:S(2)}) collective-permute-start(f32[64,4,1,128]{0,1,3,2:T(4,128)S(1)} %get-tuple-element.22), channel_id=1, source_target_pairs={{0,64},{64,128},{128,192},{192,256},{256,320},{320,384},{384,448},... | collective-permute-start | bytes 393224 | tf_op jit(solution)/shard_map/ppermute | solution.py:18
  10.5 10.4 %collective-permute-start.1 = (f32[64,4,1,128]{0,1,3,2:T(4,128)S(1)}, f32[64,4,1,128]{0,1,3,2:T(4,128)S(1)}, u32[]{:S(2)}, u32[]{:S(2)}) collective-permute-start(f32[64,4,1,128]{0,1,3,2:T(4,128)S(1)} %get-tuple-element.23), channel_id=1, source_target_pairs={{64,0},{128,64},{192,128},{256,192},{320,256},{384,320},{448,384},... | collective-permute-start | bytes 393224 | tf_op jit(solution)/shard_map/ppermute | solution.py:20
  20.9 16.1 %copy-start.1 = (f32[64,4,1,128]{0,1,3,2:T(4,128)}, f32[64,4,1,128]{0,1,3,2:T(4,128)S(1)}, u32[]{:S(2)}) copy-start(f32[64,4,1,128]{0,1,3,2:T(4,128)S(1)} %collective-permute-done.1) | copy-start | bytes 393220
  20.9 5.9 %collective-permute-start.3 = (f32[64,4,6,1]{0,1,3,2:T(4,128)S(1)}, f32[64,4,6,1]{0,1,3,2:T(4,128)S(1)}, u32[]{:S(2)}, u32[]{:S(2)}) collective-permute-start(f32[64,4,6,1]{0,1,3,2:T(4,128)S(1)} %get-tuple-element.18), channel_id=1, source_target_pairs={{4,0},{8,4},{12,8},{16,12},{20,16},{24,20},{28,24},{32,28},{36,32}... | collective-permute-start | bytes 18440 | tf_op jit(solution)/shard_map/ppermute | solution.py:20
  22.2 5.9 %collective-permute-start.2 = (f32[64,4,6,1]{0,1,3,2:T(4,128)S(1)}, f32[64,4,6,1]{0,1,3,2:T(4,128)S(1)}, u32[]{:S(2)}, u32[]{:S(2)}) collective-permute-start(f32[64,4,6,1]{0,1,3,2:T(4,128)S(1)} %get-tuple-element.19), channel_id=1, source_target_pairs={{0,4},{4,8},{8,12},{12,16},{16,20},{20,24},{24,28},{28,32},{32,36}... | collective-permute-start | bytes 18440 | tf_op jit(solution)/shard_map/ppermute | solution.py:18
  29.5 15.7 %copy-start.4 = (f32[64]{0:T(128)S(1)}, f32[64]{0:T(128)}, u32[]{:S(2)}) copy-start(f32[64]{0:T(128)} %param.10) | copy-start | bytes 772
  31.0 9.9 %collective-permute-start.5 = (f32[64,1,6,130]{3,0,2,1:T(8,128)}, f32[64,1,6,130]{3,0,2,1:T(8,128)S(1)}, u32[]{:S(2)}, u32[]{:S(2)}) collective-permute-start(f32[64,1,6,130]{3,0,2,1:T(8,128)} %copy.33), channel_id=1, source_target_pairs={{0,1},{1,2},{2,3},{4,5},{5,6},{6,7},{8,9},{9,10},{10,11},{12,13},{... | collective-permute-start | bytes 599048 | tf_op jit(solution)/shard_map/ppermute | solution.py:18
  34.4 9.7 %collective-permute-start.4 = (f32[64,1,6,130]{3,0,2,1:T(8,128)S(1)}, f32[64,1,6,130]{3,0,2,1:T(8,128)S(1)}, u32[]{:S(2)}, u32[]{:S(2)}) collective-permute-start(f32[64,1,6,130]{3,0,2,1:T(8,128)S(1)} %copy.31), channel_id=1, source_target_pairs={{1,0},{2,1},{3,2},{5,4},{6,5},{7,6},{9,8},{10,9},{11,10},{13,12},{... | collective-permute-start | bytes 599048 | tf_op jit(solution)/shard_map/ppermute | solution.py:20
  50.7 40.5 %copy-start.5 = (s32[1,1,1,7]{3,2,1,0:T(1,128)S(1)}, s32[1,1,1,7]{3,2,1,0:T(1,128)}, u32[]{:S(2)}) copy-start(s32[1,1,1,7]{3,2,1,0:T(1,128)} %param.15) | copy-start | bytes 88
  50.8 40.5 %copy-start.6 = (s32[1,1,1,7,1]{3,4,2,1,0:T(1,128)S(1)}, s32[1,1,1,7,1]{3,4,2,1,0:T(1,128)}, u32[]{:S(2)}) copy-start(s32[1,1,1,7,1]{3,4,2,1,0:T(1,128)} %param.14) | copy-start | bytes 88
  50.8 17.8 %collective-permute-start.6 = (f32[64,4,1,128]{0,1,3,2:T(4,128)S(1)}, f32[64,4,1,128]{0,1,3,2:T(4,128)S(1)}, u32[]{:S(2)}, u32[]{:S(2)}) collective-permute-start(f32[64,4,1,128]{0,1,3,2:T(4,128)S(1)} %get-tuple-element.20), channel_id=1, source_target_pairs={{0,64},{64,128},{128,192},{192,256},{256,320},{320,384},{384,448},... | collective-permute-start | bytes 393224 | tf_op jit(solution)/shard_map/ppermute | solution.py:18
  67.3 5.4 %collective-permute-start.7 = (f32[64,4,1,128]{0,1,3,2:T(4,128)S(1)}, f32[64,4,1,128]{0,1,3,2:T(4,128)S(1)}, u32[]{:S(2)}, u32[]{:S(2)}) collective-permute-start(f32[64,4,1,128]{0,1,3,2:T(4,128)S(1)} %get-tuple-element.21), channel_id=1, source_target_pairs={{64,0},{128,64},{192,128},{256,192},{320,256},{384,320},{448,384},... | collective-permute-start | bytes 393224 | tf_op jit(solution)/shard_map/ppermute | solution.py:20
  72.6 6.1 %collective-permute-start.9 = (f32[64,4,6,1]{0,1,3,2:T(4,128)S(1)}, f32[64,4,6,1]{0,1,3,2:T(4,128)S(1)}, u32[]{:S(2)}, u32[]{:S(2)}) collective-permute-start(f32[64,4,6,1]{0,1,3,2:T(4,128)S(1)} %get-tuple-element.16), channel_id=1, source_target_pairs={{4,0},{8,4},{12,8},{16,12},{20,16},{24,20},{28,24},{32,28},{36,32}... | collective-permute-start | bytes 18440 | tf_op jit(solution)/shard_map/ppermute | solution.py:20
  73.9 6.2 %collective-permute-start.8 = (f32[64,4,6,1]{0,1,3,2:T(4,128)S(1)}, f32[64,4,6,1]{0,1,3,2:T(4,128)S(1)}, u32[]{:S(2)}, u32[]{:S(2)}) collective-permute-start(f32[64,4,6,1]{0,1,3,2:T(4,128)S(1)} %get-tuple-element.17), channel_id=1, source_target_pairs={{0,4},{4,8},{8,12},{12,16},{16,20},{20,24},{24,28},{28,32},{32,36}... | collective-permute-start | bytes 18440 | tf_op jit(solution)/shard_map/ppermute | solution.py:18
  85.2 9.9 %collective-permute-start.11 = (f32[64,1,6,130]{3,0,2,1:T(8,128)}, f32[64,1,6,130]{3,0,2,1:T(8,128)S(1)}, u32[]{:S(2)}, u32[]{:S(2)}) collective-permute-start(f32[64,1,6,130]{3,0,2,1:T(8,128)} %copy.42), channel_id=1, source_target_pairs={{0,1},{1,2},{2,3},{4,5},{5,6},{6,7},{8,9},{9,10},{10,11},{12,13},{... | collective-permute-start | bytes 599048 | tf_op jit(solution)/shard_map/ppermute | solution.py:18
  88.3 9.9 %collective-permute-start.10 = (f32[64,1,6,130]{3,0,2,1:T(8,128)}, f32[64,1,6,130]{3,0,2,1:T(8,128)S(1)}, u32[]{:S(2)}, u32[]{:S(2)}) collective-permute-start(f32[64,1,6,130]{3,0,2,1:T(8,128)} %copy.40), channel_id=1, source_target_pairs={{1,0},{2,1},{3,2},{5,4},{6,5},{7,6},{9,8},{10,9},{11,10},{13,12},{... | collective-permute-start | bytes 599048 | tf_op jit(solution)/shard_map/ppermute | solution.py:20
  91.2 13.5 %copy-start.2 = (f32[4,4,128]{2,1,0:T(4,128)S(1)}, f32[4,4,128]{2,1,0:T(4,128)}, u32[]{:S(2)}) copy-start(f32[4,4,128]{2,1,0:T(4,128)} %param.9) | copy-start | bytes 24580
Sparse Core Ops, SparseCore 0:
  114.4 114.7 reduce-scatter.1
where the time goes:
time: 237 us; the launch traced here: 236 us
  waiting for transfers between devices  139 us (59%)
  starting transfers between devices  44.7 us (19%)
  local copies, waits for them, and re-layouts  18.1 us (8%)
  other arithmetic  14.5 us (6%)
  between operations  14.4 us (6%)
  matrix products  5.5 us (2%)
    reduce_scatter x1, waiting for transfers between devices, body(): sky = lax.psum_scatter(terms, 'gy', scatter_dimension=0, tiled=True)  114 us
    ppermute x6, starting transfers between devices, extended(): lax.ppermute(tail, axis, [(i, (i + 1) % count) for i in range(ends)])  34.2 us
    ppermute x6, waiting for transfers between devices, extended(): lax.ppermute(head, axis, [((i + 1) % count, i) for i in range(ends)])  18.1 us
    ppermute x6, starting transfers between devices, extended(): lax.ppermute(head, axis, [((i + 1) % count, i) for i in range(ends)])  10.4 us
    ppermute x6, waiting for transfers between devices, extended(): lax.ppermute(tail, axis, [(i, (i + 1) % count) for i in range(ends)])  7.08 us
    mul x2, other arithmetic, advance(): loss_flux = losses[:, None, None, None] * center  5.71 us
    sub x1, other arithmetic, advance(): center + diffusion[:, None, None, None] * (beside - 6.0 * center)  5.43 us
  transfers between devices with their start and end apart: 13, of which 9 were waited for; matrix products, arithmetic and copies ran while one was open for 3% of the time, Pallas kernels for 0%

commit v1 on v0

v1 whole, which is shorter than its diff:
```python
import functools

import jax
import jax.numpy as jnp
from jax import lax
from jax.experimental import pallas as pl
from jax.experimental.pallas import tpu as pltpu
from jax.sharding import PartitionSpec as P

NE = 64
NG = 96
PB = 128
CX = 4
CZ = 4
CY = 128
KS = 7
BO = 4
CAP = 2
ZX = CZ * CX
LANE = CAP * NE + 8
VMEM = pl.BlockSpec(memory_space=pltpu.VMEM)
SMEM = pl.BlockSpec(memory_space=pltpu.SMEM)
SMALL = 16 * 1024 * 1024


def even(axis):
    return lax.rem(lax.axis_index(axis), 2) == 0


def lanes(shape=(NE, CY)):
    return lax.broadcasted_iota(jnp.int32, shape, 1)


def native(ref):
    return [ref[pl.ds(zx, NE, stride=ZX), :] for zx in range(ZX)]


def regrouped(ref):
    return [ref[zx * NE:(zx + 1) * NE, :] for zx in range(ZX)]


def put_faces(cells, outs):
    xa, xb, za, zb, ya, yb = outs
    px, py, pz = even("gx"), even("gy"), even("gz")
    for z in range(CZ):
        low, high = cells[z * CX], cells[z * CX + CX - 1]
        xa[z * NE:(z + 1) * NE, :] = jnp.where(px, high, low)
        xb[z * NE:(z + 1) * NE, :] = jnp.where(px, low, high)
    for x in range(CX):
        low, high = cells[x], cells[(CZ - 1) * CX + x]
        za[x * NE:(x + 1) * NE, :] = jnp.where(pz, high, low)
        zb[x * NE:(x + 1) * NE, :] = jnp.where(pz, low, high)
    lane = lanes()
    low = jnp.zeros((NE, CY), jnp.float32)
    high = jnp.zeros((NE, CY), jnp.float32)
    for zx in range(ZX):
        first = cells[zx] if zx == 0 else pltpu.roll(cells[zx], zx, 1)
        low = jnp.where(lane == zx, first, low)
        high = jnp.where(lane == zx, pltpu.roll(cells[zx], zx + 1, 1), high)
    ya[...] = jnp.where(py, high, low)
    yb[...] = jnp.where(py, low, high)


def column(row):
    square = jnp.broadcast_to(row, (NE, NE))
    across = lax.broadcasted_iota(jnp.int32, (NE, NE), 1)
    down = lax.broadcasted_iota(jnp.int32, (NE, NE), 0)
    return jnp.sum(jnp.where(across == down, square, 0.0), axis=1, keepdims=True)


def advance(cells, halos, diff_ref, loss_ref):
    xa, xb, za, zb, ya, yb = halos
    px, py, pz = even("gx"), even("gy"), even("gz")

    def sides(flag, a, b):
        return jnp.where(flag, b, a), jnp.where(flag, a, b)

    diff = jnp.broadcast_to(column(diff_ref[...]), (NE, CY))
    loss = jnp.broadcast_to(column(loss_ref[...]), (NE, CY))
    y_low, y_high = sides(py, ya[...], yb[...])
    lane = lanes()
    last = lax.broadcasted_iota(jnp.int32, (NE, CY), 0) == NE - 1
    out = []
    for z in range(CZ):
        x_low, x_high = sides(px, xa[z * NE:(z + 1) * NE, :], xb[z * NE:(z + 1) * NE, :])
        for x in range(CX):
            zx = z * CX + x
            c = cells[zx]
            if z in (0, CZ - 1):
                z_low, z_high = sides(pz, za[x * NE:(x + 1) * NE, :], zb[x * NE:(x + 1) * NE, :])
            z_up = cells[zx + CX] if z < CZ - 1 else z_high
            z_down = cells[zx - CX] if z > 0 else z_low
            x_up = cells[zx + 1] if x < CX - 1 else x_high
            x_down = cells[zx - 1] if x > 0 else x_low
            low = y_low if zx == 0 else pltpu.roll(y_low, CY - zx, 1)
            y_up = jnp.where(lane == CY - 1, pltpu.roll(y_high, CY - 1 - zx, 1), pltpu.roll(c, CY - 1, 1))
            y_down = jnp.where(lane == 0, low, pltpu.roll(c, 1, 1))
            beside = z_up + z_down + x_up + x_down + y_up + y_down
            flux = loss * c
            above = jnp.where(last, 0.0, pltpu.roll(flux, NE - 1, 0))
            out.append(c + diff * (beside - 6.0 * c) + above - flux)
    return out


def first_faces(cr_ref, *outs):
    put_faces(native(cr_ref), outs)


def middle_step(cr_ref, xa, xb, za, zb, ya, yb, diff_ref, loss_ref, next_ref, *outs):
    cells = advance(native(cr_ref), (xa, xb, za, zb, ya, yb), diff_ref, loss_ref)
    for zx in range(ZX):
        next_ref[zx * NE:(zx + 1) * NE, :] = cells[zx]
    put_faces(cells, outs)


def last_step(owner_ref, block_ref, now_ref, xa, xb, za, zb, ya, yb, diff_ref, loss_ref, gas_ref, weight_ref,
              final_ref, send_ref, parts_ref):
    cells = advance(regrouped(now_ref), (xa, xb, za, zb, ya, yb), diff_ref, loss_ref)
    for zx in range(ZX):
        final_ref[pl.ds(zx, NE, stride=ZX), :] = cells[zx]
        lit = cells[zx] * gas_ref[zx:zx + 1, :]
        upper = lit.astype(jnp.bfloat16)
        parts_ref[0:NE, zx * CY:(zx + 1) * CY] = upper
        parts_ref[NE:2 * NE, zx * CY:(zx + 1) * CY] = (lit - upper.astype(jnp.float32)).astype(jnp.bfloat16)
    send_ref[...] = jnp.zeros_like(send_ref)
    for s in range(KS):
        owner = owner_ref[s]
        place = 0
        for t in range(s):
            place = place + (owner_ref[t] == owner).astype(jnp.int32)
        product = jnp.dot(parts_ref[...], weight_ref[s], preferred_element_type=jnp.float32)
        base = owner * LANE
        at = pl.multiple_of(base + place * NE, 8)
        send_ref[pl.ds(at, NE), :] = product[:NE] + product[NE:]
        mark = base + CAP * NE + place * BO + block_ref[s]
        send_ref[pl.ds(mark, 1), :] = jnp.ones((1, PB), jnp.float32)


def gather_sky(recv_ref, table_ref, sky_ref):
    count = recv_ref.shape[0] // LANE
    total = [jnp.zeros((NE, PB), jnp.float32) for _ in range(BO)]
    for j in range(count):
        for k in range(CAP):
            block = recv_ref[j * LANE + k * NE:j * LANE + (k + 1) * NE, :]
            for b in range(BO):
                row = j * LANE + CAP * NE + k * BO + b
                total[b] = total[b] + block * recv_ref[row:row + 1, :]
    for b in range(BO):
        sky_ref[b * NG:(b + 1) * NG, :] = jnp.dot(
            table_ref[...], total[b], precision=lax.Precision.HIGHEST, preferred_element_type=jnp.float32
        )


def f32(*shape):
    return jax.ShapeDtypeStruct(shape, jnp.float32)


FACES = [f32(CZ * NE, CY)] * 2 + [f32(CX * NE, CY)] * 2 + [f32(NE, CY)] * 2


def call(body, name, outs, in_specs, scratch=()):
    return pl.pallas_call(
        body,
        name=name,
        out_shape=outs,
        in_specs=in_specs,
        out_specs=[VMEM] * len(outs),
        scratch_shapes=list(scratch),
        compiler_params=pltpu.CompilerParams(vmem_limit_bytes=SMALL),
    )


def swap(values, axis, start):
    pairs = []
    for i in range(start, lax.axis_size(axis) - 1, 2):
        pairs += [(i, i + 1), (i + 1, i)]
    return lax.ppermute(values, axis, pairs)


def exchange(faces):
    xa, xb, za, zb, ya, yb = faces
    far = swap(xb, "gx", 1)
    return (swap(xa, "gx", 0), far, swap(za, "gz", 0), swap(zb, "gz", 1), swap(ya, "gy", 0), swap(yb, "gy", 1))


def body(cr_init, gas, diff_coeff, loss_coeff, pi0_table, los_weight, slot_owner, slot_block):
    start = cr_init.reshape(NE * ZX, CY)
    diff, loss = diff_coeff.reshape(1, NE), loss_coeff.reshape(1, NE)
    faces = call(first_faces, "first_faces", FACES, [VMEM])(start)
    now, *faces = call(middle_step, "middle_step", [f32(ZX * NE, CY)] + FACES, [VMEM] * 9)(
        start, *exchange(faces), diff, loss
    )
    owners = lax.axis_size("gy")
    final, send = call(
        last_step,
        "last_step",
        [f32(NE * ZX, CY), f32(owners * LANE, PB)],
        [SMEM] * 2 + [VMEM] * 11,
        [pltpu.VMEM((2 * NE, ZX * CY), jnp.bfloat16)],
    )(
        slot_owner.reshape(KS), slot_block.reshape(KS), now, *exchange(faces), diff, loss,
        gas.reshape(ZX, CY), los_weight.reshape(KS, ZX * CY, PB),
    )
    recv = lax.all_to_all(send.reshape(owners, LANE, PB), "gy", 0, 0, tiled=True)
    (sky,) = call(gather_sky, "gather_sky", [f32(BO * NG, PB)], [VMEM] * 2)(
        recv.reshape(owners * LANE, PB), pi0_table
    )
    return final.reshape(cr_init.shape), sky.reshape(1, 1, BO, NG, PB)


def solution(mesh):
    in_specs = (
        P(None, "gz", "gx", "gy"),
        P("gz", "gx", "gy"),
        P(),
        P(),
        P(),
        P("gz", "gx", "gy", None, None, None),
        P("gz", "gx", "gy", None, None),
        P("gz", "gx", "gy", None),
    )
    out_specs = (P(None, "gz", "gx", "gy"), P("gz", "gx", "gy", None, None))
    return jax.shard_map(body, mesh=mesh, in_specs=in_specs, out_specs=out_specs, check_vma=False)
```

time: 237 us -> 97 us (0.41)
  the two profiles are of different devices: /device:TPU:8 before, /device:TPU:49 now
where the time goes in v1:
time: 97 us; the launch traced here: 96.4 us
  starting transfers between devices  51 us (53%)
  waiting for transfers between devices  34 us (35%)
  Pallas kernels  6.07 us (6%)
  local copies, waits for them, and re-layouts  4.5 us (5%)
    ppermute x12, starting transfers between devices, swap(): return lax.ppermute(values, axis, pairs)  45.4 us
    all_to_all x1, waiting for transfers between devices, body(): lax.all_to_all(send.reshape(owners, LANE, PB), 'gy', 0, 0, tiled=True)  25 us
    ppermute x12, waiting for transfers between devices, swap(): return lax.ppermute(values, axis, pairs)  9.04 us
    all_to_all x1, starting transfers between devices, body(): lax.all_to_all(send.reshape(owners, LANE, PB), 'gy', 0, 0, tiled=True)  5.54 us
    unnamed x19, local copies, waits for them, and re-layouts  4.5 us
    pallas_call x1, Pallas kernels, body(): call(last_step, 'last_step', [f32(NE * ZX, CY), f32(owners * LANE, PB)],...  3.5 us
  transfers between devices with their start and end apart: 13, of which 5 were waited for; matrix products, arithmetic and copies ran while one was open for 0% of the time, Pallas kernels for 0%

profile of v1, /device:TPU:49, one launch (start us, length us, event | category | flops | bytes accessed | tf_op | source)
XLA Modules:
  0.0 96.4 jit_solution(9200957683735139710)
XLA Ops:
  0.6 0.0 copy-start.4
  0.6 0.0 copy-start.6
  0.7 0.0 copy-start.7
  0.7 0.0 copy-start.1
  0.7 1.1 %copy-done.1 = f32[64,4,4,128]{3,2,1,0:T(4,128)S(1)} copy-done((f32[64,4,4,128]{3,2,1,0:T(4,128)S(1)}, f32[64,4,4,128]{3,2,1,0:T(4,128)}, u32[]{:S(2)}) %copy-start.1) | copy-done | bytes 524312
  1.7 0.0 copy-start.2
  1.7 0.4 first_faces.1
  2.1 2.6 %collective-permute-start = (f32[256,128]{1,0:T(8,128)S(1)}, f32[256,128]{1,0:T(8,128)S(1)}, u32[]{:S(2)}, u32[]{:S(2)}) collective-permute-start(f32[256,128]{1,0:T(8,128)S(1)} %get-tuple-element.17), channel_id=1, source_target_pairs={{0,64},{64,0},{128,192},{192,128},{256,320},{320,256},{384,448},{4... | collective-permute-start | bytes 393224 | tf_op jit(solution)/shard_map/ppermute | solution.py:177
  4.7 8.7 %collective-permute-start.1 = (f32[256,128]{1,0:T(8,128)S(1)}, f32[256,128]{1,0:T(8,128)S(1)}, u32[]{:S(2)}, u32[]{:S(2)}) collective-permute-start(f32[256,128]{1,0:T(8,128)S(1)} %get-tuple-element.18), channel_id=1, source_target_pairs={{64,128},{128,64},{192,256},{256,192},{320,384},{384,320},{65,129}... | collective-permute-start | bytes 393224 | tf_op jit(solution)/shard_map/ppermute | solution.py:177
  13.4 2.9 %collective-permute-start.2 = (f32[256,128]{1,0:T(8,128)S(1)}, f32[256,128]{1,0:T(8,128)S(1)}, u32[]{:S(2)}, u32[]{:S(2)}) collective-permute-start(f32[256,128]{1,0:T(8,128)S(1)} %get-tuple-element.19), channel_id=1, source_target_pairs={{0,1},{1,0},{2,3},{3,2},{4,5},{5,4},{6,7},{7,6},{8,9},{9,8},{10,11... | collective-permute-start | bytes 393224 | tf_op jit(solution)/shard_map/ppermute | solution.py:177
  16.3 1.9 %collective-permute-start.3 = (f32[256,128]{1,0:T(8,128)S(1)}, f32[256,128]{1,0:T(8,128)S(1)}, u32[]{:S(2)}, u32[]{:S(2)}) collective-permute-start(f32[256,128]{1,0:T(8,128)S(1)} %get-tuple-element.20), channel_id=1, source_target_pairs={{1,2},{2,1},{5,6},{6,5},{9,10},{10,9},{13,14},{14,13},{17,18},{18,... | collective-permute-start | bytes 393224 | tf_op jit(solution)/shard_map/ppermute | solution.py:177
  18.2 3.1 %collective-permute-start.4 = (f32[64,128]{1,0:T(8,128)S(1)}, f32[64,128]{1,0:T(8,128)S(1)}, u32[]{:S(2)}, u32[]{:S(2)}) collective-permute-start(f32[64,128]{1,0:T(8,128)S(1)} %get-tuple-element.21), channel_id=1, source_target_pairs={{0,4},{4,0},{8,12},{12,8},{16,20},{20,16},{24,28},{28,24},{32,36},... | collective-permute-start | bytes 98312 | tf_op jit(solution)/shard_map/ppermute | solution.py:177
  21.4 1.8 %collective-permute-done.4.ya = f32[64,128]{1,0:T(8,128)S(1)} collective-permute-done((f32[64,128]{1,0:T(8,128)S(1)}, f32[64,128]{1,0:T(8,128)S(1)}, u32[]{:S(2)}, u32[]{:S(2)}) %collective-permute-start.4) | collective-permute-done | bytes 32800 | tf_op jit(solution)/shard_map/ppermute | solution.py:177
  23.2 3.9 %collective-permute-start.5 = (f32[64,128]{1,0:T(8,128)S(1)}, f32[64,128]{1,0:T(8,128)S(1)}, u32[]{:S(2)}, u32[]{:S(2)}) collective-permute-start(f32[64,128]{1,0:T(8,128)S(1)} %get-tuple-element.22), channel_id=1, source_target_pairs={{4,8},{8,4},{12,16},{16,12},{20,24},{24,20},{28,32},{32,28},{36,40... | collective-permute-start | bytes 98312 | tf_op jit(solution)/shard_map/ppermute | solution.py:177
  27.1 2.8 %collective-permute-done.5.yb = f32[64,128]{1,0:T(8,128)S(1)} collective-permute-done((f32[64,128]{1,0:T(8,128)S(1)}, f32[64,128]{1,0:T(8,128)S(1)}, u32[]{:S(2)}, u32[]{:S(2)}) %collective-permute-start.5) | collective-permute-done | bytes 32800 | tf_op jit(solution)/shard_map/ppermute | solution.py:177
  30.0 0.0 collective-permute-done.xa
  30.0 0.0 collective-permute-done.1.xb
  30.0 0.0 collective-permute-done.2.za
  30.0 0.0 collective-permute-done.3.zb
  30.0 0.0 copy-start.3
  30.0 0.6 copy-done.3
  30.6 0.0 copy-start.5
  30.6 0.7 copy-done.5
  31.3 0.9 middle_step.1
  32.2 1.9 %collective-permute-start.6 = (f32[256,128]{1,0:T(8,128)S(1)}, f32[256,128]{1,0:T(8,128)S(1)}, u32[]{:S(2)}, u32[]{:S(2)}) collective-permute-start(f32[256,128]{1,0:T(8,128)S(1)} %get-tuple-element.24), channel_id=1, source_target_pairs={{0,64},{64,0},{128,192},{192,128},{256,320},{320,256},{384,448},{4... | collective-permute-start | bytes 393224 | tf_op jit(solution)/shard_map/ppermute | solution.py:177
  34.2 8.0 %collective-permute-start.7 = (f32[256,128]{1,0:T(8,128)S(1)}, f32[256,128]{1,0:T(8,128)S(1)}, u32[]{:S(2)}, u32[]{:S(2)}) collective-permute-start(f32[256,128]{1,0:T(8,128)S(1)} %get-tuple-element.25), channel_id=1, source_target_pairs={{64,128},{128,64},{192,256},{256,192},{320,384},{384,320},{65,129}... | collective-permute-start | bytes 393224 | tf_op jit(solution)/shard_map/ppermute | solution.py:177
  42.2 1.9 %collective-permute-start.8 = (f32[256,128]{1,0:T(8,128)S(1)}, f32[256,128]{1,0:T(8,128)S(1)}, u32[]{:S(2)}, u32[]{:S(2)}) collective-permute-start(f32[256,128]{1,0:T(8,128)S(1)} %get-tuple-element.26), channel_id=1, source_target_pairs={{0,1},{1,0},{2,3},{3,2},{4,5},{5,4},{6,7},{7,6},{8,9},{9,8},{10,11... | collective-permute-start | bytes 393224 | tf_op jit(solution)/shard_map/ppermute | solution.py:177
  44.1 3.4 %collective-permute-start.9 = (f32[256,128]{1,0:T(8,128)S(1)}, f32[256,128]{1,0:T(8,128)S(1)}, u32[]{:S(2)}, u32[]{:S(2)}) collective-permute-start(f32[256,128]{1,0:T(8,128)S(1)} %get-tuple-element.27), channel_id=1, source_target_pairs={{1,2},{2,1},{5,6},{6,5},{9,10},{10,9},{13,14},{14,13},{17,18},{18,... | collective-permute-start | bytes 393224 | tf_op jit(solution)/shard_map/ppermute | solution.py:177
  47.5 1.9 %collective-permute-start.10 = (f32[64,128]{1,0:T(8,128)S(1)}, f32[64,128]{1,0:T(8,128)S(1)}, u32[]{:S(2)}, u32[]{:S(2)}) collective-permute-start(f32[64,128]{1,0:T(8,128)S(1)} %get-tuple-element.28), channel_id=1, source_target_pairs={{0,4},{4,0},{8,12},{12,8},{16,20},{20,16},{24,28},{28,24},{32,36},... | collective-permute-start | bytes 98312 | tf_op jit(solution)/shard_map/ppermute | solution.py:177
  49.4 2.7 %collective-permute-done.10.ya = f32[64,128]{1,0:T(8,128)S(1)} collective-permute-done((f32[64,128]{1,0:T(8,128)S(1)}, f32[64,128]{1,0:T(8,128)S(1)}, u32[]{:S(2)}, u32[]{:S(2)}) %collective-permute-start.10) | collective-permute-done | bytes 32800 | tf_op jit(solution)/shard_map/ppermute | solution.py:177
  52.2 5.1 %collective-permute-start.11 = (f32[64,128]{1,0:T(8,128)S(1)}, f32[64,128]{1,0:T(8,128)S(1)}, u32[]{:S(2)}, u32[]{:S(2)}) collective-permute-start(f32[64,128]{1,0:T(8,128)S(1)} %get-tuple-element.29), channel_id=1, source_target_pairs={{4,8},{8,4},{12,16},{16,12},{20,24},{24,20},{28,32},{32,28},{36,40... | collective-permute-start | bytes 98312 | tf_op jit(solution)/shard_map/ppermute | solution.py:177
  57.3 1.6 %collective-permute-done.11.yb = f32[64,128]{1,0:T(8,128)S(1)} collective-permute-done((f32[64,128]{1,0:T(8,128)S(1)}, f32[64,128]{1,0:T(8,128)S(1)}, u32[]{:S(2)}, u32[]{:S(2)}) %collective-permute-start.11) | collective-permute-done | bytes 32800 | tf_op jit(solution)/shard_map/ppermute | solution.py:177
  58.9 0.0 collective-permute-done.6.xa
  58.9 0.0 collective-permute-done.7.xb
  58.9 0.0 collective-permute-done.8.za
  58.9 0.0 collective-permute-done.9.zb
  58.9 0.0 copy-done.4
  58.9 0.0 copy-done.6
  59.0 0.0 copy-done.7
  59.0 0.0 copy-done.2
  59.0 0.0 copy-start
  59.0 2.0 %copy-done = bf16[1,1,1,7,2048,128]{5,4,3,2,1,0:T(8,128)(2,1)S(1)} copy-done((bf16[1,1,1,7,2048,128]{5,4,3,2,1,0:T(8,128)(2,1)S(1)}, bf16[1,1,1,7,2048,128]{5,4,3,2,1,0:T(8,128)(2,1)}, u32[]{:S(2)}) %copy-start) | copy-done | bytes 3670040
  61.0 3.5 %last_step.1 = (f32[1024,128]{1,0:T(8,128)}, f32[2176,128]{1,0:T(8,128)}) custom-call(s32[7]{0:T(128)S(1)} %bitcast.20, s32[7]{0:T(128)S(1)} %bitcast.21, f32[1024,128]{1,0:T(8,128)S(1)} %get-tuple-element.23.now_ref, f32[256,128]{1,0:T(8,128)S(1)} %collective-permute-done.6.xa, f32[256,128]{1,0:T(8,128)S(1)} %collective-permute-done.7.xb, ...), custom_call_target="tpu_custom_call" | custom-call | tf_op jit(solution)/shard_map/last_step/pallas_call | solution.py:194
  64.5 5.5 %all-to-all-start = ((f32[16,136,128]{2,1,0:T(8,128)}), f32[16,136,128]{2,1,0:T(8,128)S(1)}, u32[]{:S(2)}, u32[]{:S(2)}) async-start(f32[16,136,128]{2,1,0:T(8,128)} %bitcast.8), calls=%async_computation | async-start | bytes 2228224 | tf_op jit(solution)/shard_map/all_to_all | solution.py:204
  70.1 0.0 copy-done.8
  70.1 0.1 copy.10.table_ref
  70.2 25.0 %all-to-all-done = f32[16,136,128]{2,1,0:T(8,128)S(1)} async-done(((f32[16,136,128]{2,1,0:T(8,128)}), f32[16,136,128]{2,1,0:T(8,128)S(1)}, u32[]{:S(2)}, u32[]{:S(2)}) %all-to-all-start) | async-done | bytes 1114144 | tf_op jit(solution)/shard_map/all_to_all | solution.py:204
  95.1 1.3 %gather_sky.1 = f32[384,128]{1,0:T(8,128)} custom-call(f32[2176,128]{1,0:T(8,128)S(1)} %bitcast.11, f32[96,64]{1,0:T(8,128)S(1)} %copy.10.table_ref), custom_call_target="tpu_custom_call" | custom-call | tf_op jit(solution)/shard_map/gather_sky/pallas_call | solution.py:205
  (1 shorter events, 0.0 us)
Async XLA Ops:
  0.6 58.3 %copy-start.4 = (f32[64]{0:T(128)S(1)}, f32[64]{0:T(128)}, u32[]{:S(2)}) copy-start(f32[64]{0:T(128)} %param.10) | copy-start | bytes 772
  0.6 58.3 %copy-start.6 = (s32[1,1,1,7,1]{3,4,2,1,0:T(1,128)S(1)}, s32[1,1,1,7,1]{3,4,2,1,0:T(1,128)}, u32[]{:S(2)}) copy-start(s32[1,1,1,7,1]{3,4,2,1,0:T(1,128)} %param.14) | copy-start | bytes 88
  0.7 58.3 %copy-start.7 = (s32[1,1,1,7]{3,2,1,0:T(1,128)S(1)}, s32[1,1,1,7]{3,2,1,0:T(1,128)}, u32[]{:S(2)}) copy-start(s32[1,1,1,7]{3,2,1,0:T(1,128)} %param.15) | copy-start | bytes 88
  0.7 1.1 %copy-start.1 = (f32[64,4,4,128]{3,2,1,0:T(4,128)S(1)}, f32[64,4,4,128]{3,2,1,0:T(4,128)}, u32[]{:S(2)}) copy-start(f32[64,4,4,128]{3,2,1,0:T(4,128)} %param.8) | copy-start | bytes 1572868
  1.7 57.2 %copy-start.2 = (f32[4,4,128]{2,1,0:T(4,128)S(1)}, f32[4,4,128]{2,1,0:T(4,128)}, u32[]{:S(2)}) copy-start(f32[4,4,128]{2,1,0:T(4,128)} %param.9) | copy-start | bytes 24580
  2.1 27.9 %collective-permute-start = (f32[256,128]{1,0:T(8,128)S(1)}, f32[256,128]{1,0:T(8,128)S(1)}, u32[]{:S(2)}, u32[]{:S(2)}) collective-permute-start(f32[256,128]{1,0:T(8,128)S(1)} %get-tuple-element.17), channel_id=1, source_target_pairs={{0,64},{64,0},{128,192},{192,128},{256,320},{320,256},{384,448},{4... | collective-permute-start | bytes 393224 | tf_op jit(solution)/shard_map/ppermute | solution.py:177
  4.7 25.3 %collective-permute-start.1 = (f32[256,128]{1,0:T(8,128)S(1)}, f32[256,128]{1,0:T(8,128)S(1)}, u32[]{:S(2)}, u32[]{:S(2)}) collective-permute-start(f32[256,128]{1,0:T(8,128)S(1)} %get-tuple-element.18), channel_id=1, source_target_pairs={{64,128},{128,64},{192,256},{256,192},{320,384},{384,320},{65,129}... | collective-permute-start | bytes 393224 | tf_op jit(solution)/shard_map/ppermute | solution.py:177
  13.4 16.6 %collective-permute-start.2 = (f32[256,128]{1,0:T(8,128)S(1)}, f32[256,128]{1,0:T(8,128)S(1)}, u32[]{:S(2)}, u32[]{:S(2)}) collective-permute-start(f32[256,128]{1,0:T(8,128)S(1)} %get-tuple-element.19), channel_id=1, source_target_pairs={{0,1},{1,0},{2,3},{3,2},{4,5},{5,4},{6,7},{7,6},{8,9},{9,8},{10,11... | collective-permute-start | bytes 393224 | tf_op jit(solution)/shard_map/ppermute | solution.py:177
  16.3 13.7 %collective-permute-start.3 = (f32[256,128]{1,0:T(8,128)S(1)}, f32[256,128]{1,0:T(8,128)S(1)}, u32[]{:S(2)}, u32[]{:S(2)}) collective-permute-start(f32[256,128]{1,0:T(8,128)S(1)} %get-tuple-element.20), channel_id=1, source_target_pairs={{1,2},{2,1},{5,6},{6,5},{9,10},{10,9},{13,14},{14,13},{17,18},{18,... | collective-permute-start | bytes 393224 | tf_op jit(solution)/shard_map/ppermute | solution.py:177
  18.2 5.0 %collective-permute-start.4 = (f32[64,128]{1,0:T(8,128)S(1)}, f32[64,128]{1,0:T(8,128)S(1)}, u32[]{:S(2)}, u32[]{:S(2)}) collective-permute-start(f32[64,128]{1,0:T(8,128)S(1)} %get-tuple-element.21), channel_id=1, source_target_pairs={{0,4},{4,0},{8,12},{12,8},{16,20},{20,16},{24,28},{28,24},{32,36},... | collective-permute-start | bytes 98312 | tf_op jit(solution)/shard_map/ppermute | solution.py:177
  23.2 6.8 %collective-permute-start.5 = (f32[64,128]{1,0:T(8,128)S(1)}, f32[64,128]{1,0:T(8,128)S(1)}, u32[]{:S(2)}, u32[]{:S(2)}) collective-permute-start(f32[64,128]{1,0:T(8,128)S(1)} %get-tuple-element.22), channel_id=1, source_target_pairs={{4,8},{8,4},{12,16},{16,12},{20,24},{24,20},{28,32},{32,28},{36,40... | collective-permute-start | bytes 98312 | tf_op jit(solution)/shard_map/ppermute | solution.py:177
  30.0 0.7 copy-start.3
  30.6 0.7 copy-start.5
  32.2 26.7 %collective-permute-start.6 = (f32[256,128]{1,0:T(8,128)S(1)}, f32[256,128]{1,0:T(8,128)S(1)}, u32[]{:S(2)}, u32[]{:S(2)}) collective-permute-start(f32[256,128]{1,0:T(8,128)S(1)} %get-tuple-element.24), channel_id=1, source_target_pairs={{0,64},{64,0},{128,192},{192,128},{256,320},{320,256},{384,448},{4... | collective-permute-start | bytes 393224 | tf_op jit(solution)/shard_map/ppermute | solution.py:177
  34.2 24.7 %collective-permute-start.7 = (f32[256,128]{1,0:T(8,128)S(1)}, f32[256,128]{1,0:T(8,128)S(1)}, u32[]{:S(2)}, u32[]{:S(2)}) collective-permute-start(f32[256,128]{1,0:T(8,128)S(1)} %get-tuple-element.25), channel_id=1, source_target_pairs={{64,128},{128,64},{192,256},{256,192},{320,384},{384,320},{65,129}... | collective-permute-start | bytes 393224 | tf_op jit(solution)/shard_map/ppermute | solution.py:177
  42.2 16.7 %collective-permute-start.8 = (f32[256,128]{1,0:T(8,128)S(1)}, f32[256,128]{1,0:T(8,128)S(1)}, u32[]{:S(2)}, u32[]{:S(2)}) collective-permute-start(f32[256,128]{1,0:T(8,128)S(1)} %get-tuple-element.26), channel_id=1, source_target_pairs={{0,1},{1,0},{2,3},{3,2},{4,5},{5,4},{6,7},{7,6},{8,9},{9,8},{10,11... | collective-permute-start | bytes 393224 | tf_op jit(solution)/shard_map/ppermute | solution.py:177
  44.1 14.8 %collective-permute-start.9 = (f32[256,128]{1,0:T(8,128)S(1)}, f32[256,128]{1,0:T(8,128)S(1)}, u32[]{:S(2)}, u32[]{:S(2)}) collective-permute-start(f32[256,128]{1,0:T(8,128)S(1)} %get-tuple-element.27), channel_id=1, source_target_pairs={{1,2},{2,1},{5,6},{6,5},{9,10},{10,9},{13,14},{14,13},{17,18},{18,... | collective-permute-start | bytes 393224 | tf_op jit(solution)/shard_map/ppermute | solution.py:177
  47.5 4.7 %collective-permute-start.10 = (f32[64,128]{1,0:T(8,128)S(1)}, f32[64,128]{1,0:T(8,128)S(1)}, u32[]{:S(2)}, u32[]{:S(2)}) collective-permute-start(f32[64,128]{1,0:T(8,128)S(1)} %get-tuple-element.28), channel_id=1, source_target_pairs={{0,4},{4,0},{8,12},{12,8},{16,20},{20,16},{24,28},{28,24},{32,36},... | collective-permute-start | bytes 98312 | tf_op jit(solution)/shard_map/ppermute | solution.py:177
  52.2 6.8 %collective-permute-start.11 = (f32[64,128]{1,0:T(8,128)S(1)}, f32[64,128]{1,0:T(8,128)S(1)}, u32[]{:S(2)}, u32[]{:S(2)}) collective-permute-start(f32[64,128]{1,0:T(8,128)S(1)} %get-tuple-element.29), channel_id=1, source_target_pairs={{4,8},{8,4},{12,16},{16,12},{20,24},{24,20},{28,32},{32,28},{36,40... | collective-permute-start | bytes 98312 | tf_op jit(solution)/shard_map/ppermute | solution.py:177
  59.0 2.0 %copy-start = (bf16[1,1,1,7,2048,128]{5,4,3,2,1,0:T(8,128)(2,1)S(1)}, bf16[1,1,1,7,2048,128]{5,4,3,2,1,0:T(8,128)(2,1)}, u32[]{:S(2)}) copy-start(bf16[1,1,1,7,2048,128]{5,4,3,2,1,0:T(8,128)(2,1)} %param.13) | copy-start | bytes 11010052
  64.5 5.5 %copy-start.8 = (f32[96,64]{0,1:T(8,128)S(1)}, f32[96,64]{0,1:T(8,128)}, u32[]{:S(2)}) copy-start(f32[96,64]{0,1:T(8,128)} %param.12) | copy-start | bytes 73732
  64.5 30.6 %all-to-all-start = ((f32[16,136,128]{2,1,0:T(8,128)}), f32[16,136,128]{2,1,0:T(8,128)S(1)}, u32[]{:S(2)}, u32[]{:S(2)}) async-start(f32[16,136,128]{2,1,0:T(8,128)} %bitcast.8), calls=%async_computation | async-start | bytes 2228224 | tf_op jit(solution)/shard_map/all_to_all | solution.py:204

commit v2 on v1

v2 whole, which is shorter than its diff:
```python
import jax
import jax.numpy as jnp
from jax import lax
from jax.experimental import pallas as pl
from jax.experimental.pallas import tpu as pltpu
from jax.sharding import PartitionSpec as P

NE = 64
NG = 96
PB = 128
CX = 4
CZ = 4
CY = 128
KS = 7
BO = 4
CAP = 2
ZX = CZ * CX
LANE = CAP * NE + 8
VMEM = pl.BlockSpec(memory_space=pltpu.VMEM)
SMEM = pl.BlockSpec(memory_space=pltpu.SMEM)
HBM = pl.BlockSpec(memory_space=pltpu.MemorySpace.HBM)
SMALL = 16 * 1024 * 1024
LARGE = 50 * 1024 * 1024


def even(axis):
    return lax.rem(lax.axis_index(axis), 2) == 0


def tile(ref, row):
    return ref[row * NE:(row + 1) * NE, :]


def native(ref):
    return [ref[pl.ds(zx, NE, stride=ZX), :] for zx in range(ZX)]


def lanes():
    return lax.broadcasted_iota(jnp.int32, (NE, CY), 1)


def moved(values, shift):
    return values if shift % CY == 0 else pltpu.roll(values, shift % CY, 1)


def gather_columns(entries):
    lane = lanes()
    packed = jnp.zeros((NE, CY), jnp.float32)
    for to, values, at in entries:
        packed = jnp.where(lane == to, moved(values, to - at), packed)
    return packed


def first_faces(cr_ref, xa, xb, za, zb):
    cells = native(cr_ref)
    px, pz = even("gx"), even("gz")
    for depth in range(2):
        for i in range(4):
            row = (depth * 4 + i) * NE
            low, high = cells[i * CX + depth], cells[i * CX + CX - 1 - depth]
            xa[row:row + NE, :] = jnp.where(px, high, low)
            xb[row:row + NE, :] = jnp.where(px, low, high)
            low, high = cells[depth * CX + i], cells[(CZ - 1 - depth) * CX + i]
            za[row:row + NE, :] = jnp.where(pz, high, low)
            zb[row:row + NE, :] = jnp.where(pz, low, high)


def halo_rows(flag, a_ref, b_ref, count):
    pairs = [(tile(a_ref, i), tile(b_ref, i)) for i in range(count)]
    return [jnp.where(flag, b, a) for a, b in pairs], [jnp.where(flag, a, b) for a, b in pairs]


def edge_faces(cr_ref, xa, xb, za, zb, ya_out, yb_out, ea_out, eb_out):
    cells = native(cr_ref)
    px, py, pz = even("gx"), even("gy"), even("gz")
    x_low, x_high = halo_rows(px, xa, xb, CZ)
    z_low, z_high = halo_rows(pz, za, zb, CX)
    packs = []
    for near in (0, CY - 1):
        deep = 1 if near == 0 else CY - 2
        entries = []
        for zx in range(ZX):
            entries.append((zx, cells[zx], near))
            entries.append((ZX + zx, cells[zx], deep))
        for i in range(4):
            entries.append((2 * ZX + i * CX, x_low[i], near))
            entries.append((2 * ZX + i * CX + CX - 1, x_high[i], near))
            entries.append((3 * ZX + i, z_low[i], near))
            entries.append((3 * ZX + (CZ - 1) * CX + i, z_high[i], near))
        packs.append(gather_columns(entries))
    low, high = packs
    ya_out[...] = jnp.where(py, high, low)
    yb_out[...] = jnp.where(py, low, high)
    for i, rows in enumerate((x_low, x_high)):
        ea_out[i * NE:(i + 1) * NE, :] = jnp.where(pz, rows[CZ - 1], rows[0])
        eb_out[i * NE:(i + 1) * NE, :] = jnp.where(pz, rows[0], rows[CZ - 1])


def column(row):
    square = jnp.broadcast_to(row, (NE, NE))
    across = lax.broadcasted_iota(jnp.int32, (NE, NE), 1)
    down = lax.broadcasted_iota(jnp.int32, (NE, NE), 0)
    return jnp.sum(jnp.where(across == down, square, 0.0), axis=1, keepdims=True)


def two_steps(cr_ref, halos, diff_ref, loss_ref):
    xa, xb, za, zb, ya, yb, ea, eb = halos
    px, py, pz = even("gx"), even("gy"), even("gz")
    lane = lanes()
    top = lax.broadcasted_iota(jnp.int32, (NE, CY), 0) == NE - 1
    diff = jnp.broadcast_to(column(diff_ref[...]), (NE, CY))
    loss = jnp.broadcast_to(column(loss_ref[...]), (NE, CY))
    inside = {}
    for axis in ("gx", "gy", "gz"):
        at = lax.axis_index(axis)
        inside[axis] = (at > 0, at < lax.axis_size(axis) - 1)

    def update(c, z_up, z_down, x_up, x_down, y_up, y_down):
        beside = z_up + z_down + x_up + x_down + y_up + y_down
        flux = loss * c
        above = jnp.where(top, 0.0, pltpu.roll(flux, NE - 1, 0))
        return c + diff * (beside - 6.0 * c) + above - flux

    def beside_y(c, low, low_lane, high, high_lane):
        y_up = jnp.where(lane == CY - 1, moved(high, CY - 1 - high_lane), pltpu.roll(c, CY - 1, 1))
        y_down = jnp.where(lane == 0, moved(low, -low_lane), pltpu.roll(c, 1, 1))
        return y_up, y_down

    cells = native(cr_ref)
    x_low, x_high = halo_rows(px, xa, xb, 2 * CZ)
    z_low, z_high = halo_rows(pz, za, zb, 2 * CX)
    e_low, e_high = halo_rows(pz, ea, eb, 2)
    (y_low,), (y_high,) = halo_rows(py, ya, yb, 1)

    def at(z, x):
        if 0 <= z < CZ and 0 <= x < CX:
            return cells[z * CX + x]
        if 0 <= z < CZ:
            return x_low[(-1 - x) * CZ + z] if x < 0 else x_high[(x - CX) * CZ + z]
        if 0 <= x < CX:
            return z_low[(-1 - z) * CX + x] if z < 0 else z_high[(z - CZ) * CX + x]
        return (e_low if z < 0 else e_high)[0 if x < 0 else 1]

    def y_lane(z, x):
        if 0 <= z < CZ and 0 <= x < CX:
            return z * CX + x
        if 0 <= z < CZ:
            return 2 * ZX + z * CX + (0 if x < 0 else CX - 1)
        return 3 * ZX + (0 if z < 0 else (CZ - 1) * CX) + x

    def first(z, x):
        c, place = at(z, x), y_lane(z, x)
        new = update(c, at(z + 1, x), at(z - 1, x), at(z, x + 1), at(z, x - 1), *beside_y(c, y_low, place, y_high, place))
        if z in (-1, CZ):
            return jnp.where(inside["gz"][0 if z < 0 else 1], new, 0.0)
        if x in (-1, CX):
            return jnp.where(inside["gx"][0 if x < 0 else 1], new, 0.0)
        return new

    def first_y(pack, own, upper):
        cx, cz = lax.rem(lane, CX), lax.div(lane, CX)
        deep, x_edge, z_edge = moved(pack, -ZX), moved(pack, -2 * ZX), moved(pack, -3 * ZX)
        z_up = jnp.where(cz == CZ - 1, z_edge, moved(pack, -CX))
        z_down = jnp.where(cz == 0, z_edge, moved(pack, CX))
        x_up = jnp.where(cx == CX - 1, x_edge, moved(pack, -1))
        x_down = jnp.where(cx == 0, x_edge, moved(pack, 1))
        new = update(pack, z_up, z_down, x_up, x_down, *((deep, own) if upper else (own, deep)))
        return jnp.where(inside["gy"][1 if upper else 0], new, 0.0)

    own_low = gather_columns([(zx, cells[zx], 0) for zx in range(ZX)])
    own_high = gather_columns([(zx, cells[zx], CY - 1) for zx in range(ZX)])
    next_y_low = first_y(y_low, own_low, False)
    next_y_high = first_y(y_high, own_high, True)
    ring = [(z, x) for z in range(CZ) for x in (-1, CX)] + [(z, x) for z in (-1, CZ) for x in range(CX)]
    now = {zx: first(*zx) for zx in [(z, x) for z in range(CZ) for x in range(CX)] + ring}
    out = []
    for z in range(CZ):
        for x in range(CX):
            c, place = now[z, x], z * CX + x
            out.append(update(c, now[z + 1, x], now[z - 1, x], now[z, x + 1], now[z, x - 1],
                              *beside_y(c, next_y_low, place, next_y_high, place)))
    return out


def project(owner_ref, block_ref, cr_ref, xa, xb, za, zb, ya, yb, ea, eb, diff_ref, loss_ref, gas_ref, weight_hbm,
            final_ref, send_ref, parts_ref, weight_ref, sems):
    copies = [pltpu.make_async_copy(weight_hbm.at[s], weight_ref.at[s], sems.at[s]) for s in range(KS)]
    for copy in copies:
        copy.start()
    cells = two_steps(cr_ref, (xa, xb, za, zb, ya, yb, ea, eb), diff_ref, loss_ref)
    for zx in range(ZX):
        final_ref[pl.ds(zx, NE, stride=ZX), :] = cells[zx]
        lit = cells[zx] * gas_ref[zx:zx + 1, :]
        upper = lit.astype(jnp.bfloat16)
        parts_ref[0:NE, zx * CY:(zx + 1) * CY] = upper
        parts_ref[NE:2 * NE, zx * CY:(zx + 1) * CY] = (lit - upper.astype(jnp.float32)).astype(jnp.bfloat16)
    send_ref[...] = jnp.zeros_like(send_ref)
    for s in range(KS):
        owner = owner_ref[s]
        place = 0
        for t in range(s):
            place = place + (owner_ref[t] == owner).astype(jnp.int32)
        copies[s].wait()
        product = jnp.dot(parts_ref[...], weight_ref[s], preferred_element_type=jnp.float32)
        base = owner * LANE
        send_ref[pl.ds(pl.multiple_of(base + place * NE, 8), NE), :] = product[:NE] + product[NE:]
        mark = base + CAP * NE + place * BO + block_ref[s]
        send_ref[pl.ds(mark, 1), :] = jnp.ones((1, PB), jnp.float32)


def gather_sky(recv_ref, table_ref, sky_ref):
    count = recv_ref.shape[0] // LANE
    total = [jnp.zeros((NE, PB), jnp.float32) for _ in range(BO)]
    for j in range(count):
        for k in range(CAP):
            block = recv_ref[j * LANE + k * NE:j * LANE + (k + 1) * NE, :]
            for b in range(BO):
                row = j * LANE + CAP * NE + k * BO + b
                total[b] = total[b] + block * recv_ref[row:row + 1, :]
    for b in range(BO):
        sky_ref[b * NG:(b + 1) * NG, :] = jnp.dot(
            table_ref[...], total[b], precision=lax.Precision.HIGHEST, preferred_element_type=jnp.float32
        )


def f32(*shape):
    return jax.ShapeDtypeStruct(shape, jnp.float32)


def call(body, name, outs, in_specs, scratch=(), limit=SMALL):
    return pl.pallas_call(
        body,
        name=name,
        out_shape=outs,
        in_specs=in_specs,
        out_specs=[VMEM] * len(outs),
        scratch_shapes=list(scratch),
        compiler_params=pltpu.CompilerParams(vmem_limit_bytes=limit),
    )


def swap(values, axis, start):
    pairs = []
    for i in range(start, lax.axis_size(axis) - 1, 2):
        pairs += [(i, i + 1), (i + 1, i)]
    return lax.ppermute(values, axis, pairs)


def body(cr_init, gas, diff_coeff, loss_coeff, pi0_table, los_weight, slot_owner, slot_block):
    start = cr_init.reshape(NE * ZX, CY)
    diff, loss = diff_coeff.reshape(1, NE), loss_coeff.reshape(1, NE)
    xa, xb, za, zb = call(first_faces, "first_faces", [f32(2 * 4 * NE, CY)] * 4, [VMEM])(start)
    xb = swap(xb, "gx", 1)
    xa = swap(xa, "gx", 0)
    za = swap(za, "gz", 0)
    zb = swap(zb, "gz", 1)
    ya, yb, ea, eb = call(edge_faces, "edge_faces", [f32(NE, CY)] * 2 + [f32(2 * NE, CY)] * 2, [VMEM] * 5)(
        start, xa, xb, za, zb
    )
    yb = swap(yb, "gy", 1)
    ya = swap(ya, "gy", 0)
    ea = swap(ea, "gz", 0)
    eb = swap(eb, "gz", 1)
    owners = lax.axis_size("gy")
    final, send = call(
        project,
        "project",
        [f32(NE * ZX, CY), f32(owners * LANE, PB)],
        [SMEM] * 2 + [VMEM] * 12 + [HBM],
        [
            pltpu.VMEM((2 * NE, ZX * CY), jnp.bfloat16),
            pltpu.VMEM((KS, ZX * CY, PB), jnp.bfloat16),
            pltpu.SemaphoreType.DMA((KS,)),
        ],
        LARGE,
    )(
        slot_owner.reshape(KS), slot_block.reshape(KS), start, xa, xb, za, zb, ya, yb, ea, eb, diff, loss,
        gas.reshape(ZX, CY), los_weight.reshape(KS, ZX * CY, PB),
    )
    recv = lax.all_to_all(send.reshape(owners, LANE, PB), "gy", 0, 0, tiled=True)
    (sky,) = call(gather_sky, "gather_sky", [f32(BO * NG, PB)], [VMEM] * 2)(
        recv.reshape(owners * LANE, PB), pi0_table
    )
    return final.reshape(cr_init.shape), sky.reshape(1, 1, BO, NG, PB)


def solution(mesh):
    in_specs = (
        P(None, "gz", "gx", "gy"),
        P("gz", "gx", "gy"),
        P(),
        P(),
        P(),
        P("gz", "gx", "gy", None, None, None),
        P("gz", "gx", "gy", None, None),
        P("gz", "gx", "gy", None),
    )
    out_specs = (P(None, "gz", "gx", "gy"), P("gz", "gx", "gy", None, None))
    return jax.shard_map(body, mesh=mesh, in_specs=in_specs, out_specs=out_specs, check_vma=False)
```

time: 97 us -> 82.3 us (0.85)
  the two profiles are of different devices: /device:TPU:49 before, /device:TPU:328 now
where the time goes in v2:
time: 82.3 us; the launch traced here: 81.9 us
  waiting for transfers between devices  38.2 us (46%)
  starting transfers between devices  32.3 us (39%)
  Pallas kernels  9.37 us (11%)
  local copies, waits for them, and re-layouts  1.16 us (1%)
    all_to_all x1, waiting for transfers between devices, body(): lax.all_to_all(send.reshape(owners, LANE, PB), 'gy', 0, 0, tiled=True)  26 us
    ppermute x8, starting transfers between devices, swap(): return lax.ppermute(values, axis, pairs)  23.5 us
    ppermute x8, waiting for transfers between devices, swap(): return lax.ppermute(values, axis, pairs)  12.2 us
    all_to_all x1, starting transfers between devices, body(): lax.all_to_all(send.reshape(owners, LANE, PB), 'gy', 0, 0, tiled=True)  8.83 us
    pallas_call x1, Pallas kernels, body(): call(project, 'project', [f32(NE * ZX, CY), f32(owners * LANE, PB)], [SME...  6.97 us
  transfers between devices with their start and end apart: 9, of which 4 were waited for; matrix products, arithmetic and copies ran while one was open for 0% of the time, Pallas kernels for 0%

profile of v2, /device:TPU:328, one launch (start us, length us, event | category | flops | bytes accessed | tf_op | source)
XLA Modules:
  0.0 81.9 jit_solution(16355459452443675952)
XLA Ops:
  0.6 0.0 copy-start.3
  0.6 0.0 copy-start.4
  0.7 0.0 copy-start.5
  0.7 0.0 copy-start
  0.7 1.1 %copy-done = f32[64,4,4,128]{3,2,1,0:T(4,128)S(1)} copy-done((f32[64,4,4,128]{3,2,1,0:T(4,128)S(1)}, f32[64,4,4,128]{3,2,1,0:T(4,128)}, u32[]{:S(2)}) %copy-start) | copy-done | bytes 524312
  1.7 0.0 copy-start.1
  1.7 0.0 copy-start.2
  1.7 0.0 copy-start.6
  1.7 0.2 first_faces.1
  1.9 1.9 %collective-permute-start = (f32[512,128]{1,0:T(8,128)S(1)}, f32[512,128]{1,0:T(8,128)S(1)}, u32[]{:S(2)}, u32[]{:S(2)}) collective-permute-start(f32[512,128]{1,0:T(8,128)S(1)} %get-tuple-element.12), channel_id=1, source_target_pairs={{0,64},{64,0},{128,192},{192,128},{256,320},{320,256},{384,448},{4... | collective-permute-start | bytes 786440 | tf_op jit(solution)/shard_map/ppermute | solution.py:246
  3.8 2.6 %collective-permute-start.1 = (f32[512,128]{1,0:T(8,128)S(1)}, f32[512,128]{1,0:T(8,128)S(1)}, u32[]{:S(2)}, u32[]{:S(2)}) collective-permute-start(f32[512,128]{1,0:T(8,128)S(1)} %get-tuple-element.13), channel_id=1, source_target_pairs={{64,128},{128,64},{192,256},{256,192},{320,384},{384,320},{65,129}... | collective-permute-start | bytes 786440 | tf_op jit(solution)/shard_map/ppermute | solution.py:246
  6.4 2.4 %collective-permute-start.2 = (f32[512,128]{1,0:T(8,128)S(1)}, f32[512,128]{1,0:T(8,128)S(1)}, u32[]{:S(2)}, u32[]{:S(2)}) collective-permute-start(f32[512,128]{1,0:T(8,128)S(1)} %get-tuple-element.14), channel_id=1, source_target_pairs={{0,1},{1,0},{2,3},{3,2},{4,5},{5,4},{6,7},{7,6},{8,9},{9,8},{10,11... | collective-permute-start | bytes 786440 | tf_op jit(solution)/shard_map/ppermute | solution.py:246
  8.8 4.3 %collective-permute-start.3 = (f32[512,128]{1,0:T(8,128)S(1)}, f32[512,128]{1,0:T(8,128)S(1)}, u32[]{:S(2)}, u32[]{:S(2)}) collective-permute-start(f32[512,128]{1,0:T(8,128)S(1)} %get-tuple-element.15), channel_id=1, source_target_pairs={{1,2},{2,1},{5,6},{6,5},{9,10},{10,9},{13,14},{14,13},{17,18},{18,... | collective-permute-start | bytes 786440 | tf_op jit(solution)/shard_map/ppermute | solution.py:246
  13.1 0.0 collective-permute-done.xa
  13.1 6.6 %collective-permute-done.1.xb = f32[512,128]{1,0:T(8,128)S(1)} collective-permute-done((f32[512,128]{1,0:T(8,128)S(1)}, f32[512,128]{1,0:T(8,128)S(1)}, u32[]{:S(2)}, u32[]{:S(2)}) %collective-permute-start.1) | collective-permute-done | bytes 262176 | tf_op jit(solution)/shard_map/ppermute | solution.py:246
  19.7 0.0 collective-permute-done.2.za
  19.7 0.0 collective-permute-done.3.zb
  19.7 1.0 %edge_faces.1 = (f32[64,128]{1,0:T(8,128)S(1)}, f32[64,128]{1,0:T(8,128)S(1)}, f32[128,128]{1,0:T(8,128)S(1)}, f32[128,128]{1,0:T(8,128)S(1)}) custom-call(f32[1024,128]{1,0:T(8,128)S(1)} %bitcast.12, f32[512,128]{1,0:T(8,128)S(1)} %collective-permute-done.xa, f32[512,128]{1,0:T(8,128)S(1)} %collective-permute-done.1.xb, ...), custom_call_target="tpu_custom_call" | custom-call | tf_op jit(solution)/shard_map/edge_faces/pallas_call | solution.py:257
  20.6 2.4 %collective-permute-start.6 = (f32[128,128]{1,0:T(8,128)S(1)}, f32[128,128]{1,0:T(8,128)S(1)}, u32[]{:S(2)}, u32[]{:S(2)}) collective-permute-start(f32[128,128]{1,0:T(8,128)S(1)} %get-tuple-element.18), channel_id=1, source_target_pairs={{0,1},{1,0},{2,3},{3,2},{4,5},{5,4},{6,7},{7,6},{8,9},{9,8},{10,11... | collective-permute-start | bytes 196616 | tf_op jit(solution)/shard_map/ppermute | solution.py:246
  23.0 4.3 %collective-permute-start.7 = (f32[128,128]{1,0:T(8,128)S(1)}, f32[128,128]{1,0:T(8,128)S(1)}, u32[]{:S(2)}, u32[]{:S(2)}) collective-permute-start(f32[128,128]{1,0:T(8,128)S(1)} %get-tuple-element.19), channel_id=1, source_target_pairs={{1,2},{2,1},{5,6},{6,5},{9,10},{10,9},{13,14},{14,13},{17,18},{18,... | collective-permute-start | bytes 196616 | tf_op jit(solution)/shard_map/ppermute | solution.py:246
  27.3 3.4 %collective-permute-start.4 = (f32[64,128]{1,0:T(8,128)S(1)}, f32[64,128]{1,0:T(8,128)S(1)}, u32[]{:S(2)}, u32[]{:S(2)}) collective-permute-start(f32[64,128]{1,0:T(8,128)S(1)} %get-tuple-element.16), channel_id=1, source_target_pairs={{0,4},{4,0},{8,12},{12,8},{16,20},{20,16},{24,28},{28,24},{32,36},... | collective-permute-start | bytes 98312 | tf_op jit(solution)/shard_map/ppermute | solution.py:246
  30.7 2.3 %collective-permute-start.5 = (f32[64,128]{1,0:T(8,128)S(1)}, f32[64,128]{1,0:T(8,128)S(1)}, u32[]{:S(2)}, u32[]{:S(2)}) collective-permute-start(f32[64,128]{1,0:T(8,128)S(1)} %get-tuple-element.17), channel_id=1, source_target_pairs={{4,8},{8,4},{12,16},{16,12},{20,24},{24,20},{28,32},{32,28},{36,40... | collective-permute-start | bytes 98312 | tf_op jit(solution)/shard_map/ppermute | solution.py:246
  33.0 0.1 collective-permute-done.4.ya
  33.1 5.5 %collective-permute-done.5.yb = f32[64,128]{1,0:T(8,128)S(1)} collective-permute-done((f32[64,128]{1,0:T(8,128)S(1)}, f32[64,128]{1,0:T(8,128)S(1)}, u32[]{:S(2)}, u32[]{:S(2)}) %collective-permute-start.5) | collective-permute-done | bytes 32800 | tf_op jit(solution)/shard_map/ppermute | solution.py:246
  38.6 0.0 collective-permute-done.6.ea
  38.6 0.0 collective-permute-done.7.eb
  38.7 0.0 copy-done.3
  38.7 0.0 copy-done.4
  38.7 0.0 copy-done.5
  38.7 0.0 copy-done.1
  38.7 0.0 copy-done.2
  38.7 0.0 copy-done.6
  38.7 7.0 %project.1 = (f32[1024,128]{1,0:T(8,128)}, f32[2176,128]{1,0:T(8,128)}) custom-call(s32[7]{0:T(128)S(1)} %bitcast.16, s32[7]{0:T(128)S(1)} %bitcast.17, f32[1024,128]{1,0:T(8,128)S(1)} %bitcast.13, f32[512,128]{1,0:T(8,128)S(1)} %collective-permute-done.xa, f32[512,128]{1,0:T(8,128)S(1)} %collective-permute-done.1.xb, ...), custom_call_target="tpu_custom_call" | custom-call | tf_op jit(solution)/shard_map/project/pallas_call | solution.py:265
  45.7 0.0 copy-start.7
  45.7 8.8 %all-to-all-start = ((f32[16,136,128]{2,1,0:T(8,128)}), f32[16,136,128]{2,1,0:T(8,128)S(1)}, u32[]{:S(2)}, u32[]{:S(2)}) async-start(f32[16,136,128]{2,1,0:T(8,128)} %bitcast.8), calls=%async_computation | async-start | bytes 2228224 | tf_op jit(solution)/shard_map/all_to_all | solution.py:280
  54.5 0.0 copy-done.7
  54.5 0.1 copy.10.table_ref
  54.6 26.0 %all-to-all-done = f32[16,136,128]{2,1,0:T(8,128)S(1)} async-done(((f32[16,136,128]{2,1,0:T(8,128)}), f32[16,136,128]{2,1,0:T(8,128)S(1)}, u32[]{:S(2)}, u32[]{:S(2)}) %all-to-all-start) | async-done | bytes 1114144 | tf_op jit(solution)/shard_map/all_to_all | solution.py:280
  80.6 1.3 %gather_sky.1 = f32[384,128]{1,0:T(8,128)} custom-call(f32[2176,128]{1,0:T(8,128)S(1)} %bitcast.14, f32[96,64]{1,0:T(8,128)S(1)} %copy.10.table_ref), custom_call_target="tpu_custom_call" | custom-call | tf_op jit(solution)/shard_map/gather_sky/pallas_call | solution.py:281
Async XLA Ops:
  0.6 38.0 %copy-start.3 = (s32[1,1,1,7,1]{3,4,2,1,0:T(1,128)S(1)}, s32[1,1,1,7,1]{3,4,2,1,0:T(1,128)}, u32[]{:S(2)}) copy-start(s32[1,1,1,7,1]{3,4,2,1,0:T(1,128)} %param.14) | copy-start | bytes 88
  0.6 38.0 %copy-start.4 = (s32[1,1,1,7]{3,2,1,0:T(1,128)S(1)}, s32[1,1,1,7]{3,2,1,0:T(1,128)}, u32[]{:S(2)}) copy-start(s32[1,1,1,7]{3,2,1,0:T(1,128)} %param.15) | copy-start | bytes 88
  0.7 38.0 %copy-start.5 = (f32[64]{0:T(128)S(1)}, f32[64]{0:T(128)}, u32[]{:S(2)}) copy-start(f32[64]{0:T(128)} %param.10) | copy-start | bytes 772
  0.7 1.1 %copy-start = (f32[64,4,4,128]{3,2,1,0:T(4,128)S(1)}, f32[64,4,4,128]{3,2,1,0:T(4,128)}, u32[]{:S(2)}) copy-start(f32[64,4,4,128]{3,2,1,0:T(4,128)} %param.8) | copy-start | bytes 1572868
  1.7 37.0 %copy-start.1 = (f32[64,4,4,128]{3,2,1,0:T(4,128)S(1)}, f32[64,4,4,128]{3,2,1,0:T(4,128)}, u32[]{:S(2)}) copy-start(f32[64,4,4,128]{3,2,1,0:T(4,128)} %param.8) | copy-start | bytes 1572868
  1.7 37.0 %copy-start.2 = (f32[4,4,128]{2,1,0:T(4,128)S(1)}, f32[4,4,128]{2,1,0:T(4,128)}, u32[]{:S(2)}) copy-start(f32[4,4,128]{2,1,0:T(4,128)} %param.9) | copy-start | bytes 24580
  1.7 37.0 %copy-start.6 = (f32[64]{0:T(128)S(1)}, f32[64]{0:T(128)}, u32[]{:S(2)}) copy-start(f32[64]{0:T(128)} %param.11) | copy-start | bytes 772
  1.9 11.2 %collective-permute-start = (f32[512,128]{1,0:T(8,128)S(1)}, f32[512,128]{1,0:T(8,128)S(1)}, u32[]{:S(2)}, u32[]{:S(2)}) collective-permute-start(f32[512,128]{1,0:T(8,128)S(1)} %get-tuple-element.12), channel_id=1, source_target_pairs={{0,64},{64,0},{128,192},{192,128},{256,320},{320,256},{384,448},{4... | collective-permute-start | bytes 786440 | tf_op jit(solution)/shard_map/ppermute | solution.py:246
  3.8 15.8 %collective-permute-start.1 = (f32[512,128]{1,0:T(8,128)S(1)}, f32[512,128]{1,0:T(8,128)S(1)}, u32[]{:S(2)}, u32[]{:S(2)}) collective-permute-start(f32[512,128]{1,0:T(8,128)S(1)} %get-tuple-element.13), channel_id=1, source_target_pairs={{64,128},{128,64},{192,256},{256,192},{320,384},{384,320},{65,129}... | collective-permute-start | bytes 786440 | tf_op jit(solution)/shard_map/ppermute | solution.py:246
  6.4 13.3 %collective-permute-start.2 = (f32[512,128]{1,0:T(8,128)S(1)}, f32[512,128]{1,0:T(8,128)S(1)}, u32[]{:S(2)}, u32[]{:S(2)}) collective-permute-start(f32[512,128]{1,0:T(8,128)S(1)} %get-tuple-element.14), channel_id=1, source_target_pairs={{0,1},{1,0},{2,3},{3,2},{4,5},{5,4},{6,7},{7,6},{8,9},{9,8},{10,11... | collective-permute-start | bytes 786440 | tf_op jit(solution)/shard_map/ppermute | solution.py:246
  8.8 10.9 %collective-permute-start.3 = (f32[512,128]{1,0:T(8,128)S(1)}, f32[512,128]{1,0:T(8,128)S(1)}, u32[]{:S(2)}, u32[]{:S(2)}) collective-permute-start(f32[512,128]{1,0:T(8,128)S(1)} %get-tuple-element.15), channel_id=1, source_target_pairs={{1,2},{2,1},{5,6},{6,5},{9,10},{10,9},{13,14},{14,13},{17,18},{18,... | collective-permute-start | bytes 786440 | tf_op jit(solution)/shard_map/ppermute | solution.py:246
  20.6 18.0 %collective-permute-start.6 = (f32[128,128]{1,0:T(8,128)S(1)}, f32[128,128]{1,0:T(8,128)S(1)}, u32[]{:S(2)}, u32[]{:S(2)}) collective-permute-start(f32[128,128]{1,0:T(8,128)S(1)} %get-tuple-element.18), channel_id=1, source_target_pairs={{0,1},{1,0},{2,3},{3,2},{4,5},{5,4},{6,7},{7,6},{8,9},{9,8},{10,11... | collective-permute-start | bytes 196616 | tf_op jit(solution)/shard_map/ppermute | solution.py:246
  23.0 15.7 %collective-permute-start.7 = (f32[128,128]{1,0:T(8,128)S(1)}, f32[128,128]{1,0:T(8,128)S(1)}, u32[]{:S(2)}, u32[]{:S(2)}) collective-permute-start(f32[128,128]{1,0:T(8,128)S(1)} %get-tuple-element.19), channel_id=1, source_target_pairs={{1,2},{2,1},{5,6},{6,5},{9,10},{10,9},{13,14},{14,13},{17,18},{18,... | collective-permute-start | bytes 196616 | tf_op jit(solution)/shard_map/ppermute | solution.py:246
  27.3 5.8 %collective-permute-start.4 = (f32[64,128]{1,0:T(8,128)S(1)}, f32[64,128]{1,0:T(8,128)S(1)}, u32[]{:S(2)}, u32[]{:S(2)}) collective-permute-start(f32[64,128]{1,0:T(8,128)S(1)} %get-tuple-element.16), channel_id=1, source_target_pairs={{0,4},{4,0},{8,12},{12,8},{16,20},{20,16},{24,28},{28,24},{32,36},... | collective-permute-start | bytes 98312 | tf_op jit(solution)/shard_map/ppermute | solution.py:246
  30.7 7.9 %collective-permute-start.5 = (f32[64,128]{1,0:T(8,128)S(1)}, f32[64,128]{1,0:T(8,128)S(1)}, u32[]{:S(2)}, u32[]{:S(2)}) collective-permute-start(f32[64,128]{1,0:T(8,128)S(1)} %get-tuple-element.17), channel_id=1, source_target_pairs={{4,8},{8,4},{12,16},{16,12},{20,24},{24,20},{28,32},{32,28},{36,40... | collective-permute-start | bytes 98312 | tf_op jit(solution)/shard_map/ppermute | solution.py:246
  45.7 8.8 %copy-start.7 = (f32[96,64]{0,1:T(8,128)S(1)}, f32[96,64]{0,1:T(8,128)}, u32[]{:S(2)}) copy-start(f32[96,64]{0,1:T(8,128)} %param.12) | copy-start | bytes 73732
  45.7 34.9 %all-to-all-start = ((f32[16,136,128]{2,1,0:T(8,128)}), f32[16,136,128]{2,1,0:T(8,128)S(1)}, u32[]{:S(2)}, u32[]{:S(2)}) async-start(f32[16,136,128]{2,1,0:T(8,128)} %bitcast.8), calls=%async_computation | async-start | bytes 2228224 | tf_op jit(solution)/shard_map/all_to_all | solution.py:280

commit v3 on v2

v3 whole, which is shorter than its diff:
```python
import jax
import jax.numpy as jnp
from jax import lax
from jax.experimental import pallas as pl
from jax.experimental.pallas import tpu as pltpu
from jax.sharding import PartitionSpec as P

NE = 64
NG = 96
PB = 128
CX = 4
CZ = 4
CY = 128
KS = 7
BO = 4
CAP = 2
ZX = CZ * CX
LANE = CAP * NE + 8
VMEM = pl.BlockSpec(memory_space=pltpu.VMEM)
ANY = pl.BlockSpec(memory_space=pl.ANY)
SMALL = 16 * 1024 * 1024


def even(axis):
    return lax.rem(lax.axis_index(axis), 2) == 0


def tile(ref, row):
    return ref[row * NE:(row + 1) * NE, :]


def native(ref):
    return [ref[pl.ds(zx, NE, stride=ZX), :] for zx in range(ZX)]


def lanes():
    return lax.broadcasted_iota(jnp.int32, (NE, CY), 1)


def moved(values, shift):
    return values if shift % CY == 0 else pltpu.roll(values, shift % CY, 1)


def gather_columns(packed, entries):
    lane = lanes()
    for to, values, at in entries:
        packed = jnp.where(lane == to, moved(values, to - at), packed)
    return packed


def first_faces(cr_ref, xa, xb, za, zb):
    cells = native(cr_ref)
    px, pz = even("gx"), even("gz")
    for depth in range(2):
        for i in range(4):
            row = (depth * 4 + i) * NE
            low, high = cells[i * CX + depth], cells[i * CX + CX - 1 - depth]
            xa[row:row + NE, :] = jnp.where(px, high, low)
            xb[row:row + NE, :] = jnp.where(px, low, high)
            low, high = cells[depth * CX + i], cells[(CZ - 1 - depth) * CX + i]
            za[row:row + NE, :] = jnp.where(pz, high, low)
            zb[row:row + NE, :] = jnp.where(pz, low, high)


def halo_rows(flag, a_ref, b_ref, count):
    pairs = [(tile(a_ref, i), tile(b_ref, i)) for i in range(count)]
    return [jnp.where(flag, b, a) for a, b in pairs], [jnp.where(flag, a, b) for a, b in pairs]


def place_of(owner_ref, s):
    place = 0
    for t in range(s):
        place = place + (owner_ref[t] == owner_ref[s]).astype(jnp.int32)
    return place


def blank_lanes(owner_any, block_any, send_ref, owner_ref, block_ref, sem):
    fetches = [
        pltpu.make_async_copy(owner_any, owner_ref, sem.at[0]), pltpu.make_async_copy(block_any, block_ref, sem.at[1])
    ]
    for fetch in fetches:
        fetch.start()
    send_ref[...] = jnp.zeros_like(send_ref)
    for fetch in fetches:
        fetch.wait()
    for s in range(KS):
        row = owner_ref[s] * LANE + CAP * NE + place_of(owner_ref, s) * BO + block_ref[s]
        send_ref[pl.ds(row, 1), :] = jnp.ones((1, PB), jnp.float32)


def own_columns(cr_ref, blank_any, low_ref, high_ref):
    del blank_any
    cells = native(cr_ref)
    for ref, near, deep in ((low_ref, 0, 1), (high_ref, CY - 1, CY - 2)):
        entries = [(4 * zx, cells[zx], near) for zx in range(ZX)] + [(4 * zx + 1, cells[zx], deep) for zx in range(ZX)]
        ref[...] = gather_columns(jnp.zeros((NE, CY), jnp.float32), entries)


def edge_faces(xa, xb, za, zb, low_ref, high_ref, ya_out, yb_out, ea_out, eb_out):
    px, py, pz = even("gx"), even("gy"), even("gz")
    x_low, x_high = halo_rows(px, xa, xb, CZ)
    z_low, z_high = halo_rows(pz, za, zb, CX)
    packs = []
    for ref, near in ((low_ref, 0), (high_ref, CY - 1)):
        entries = []
        for i in range(4):
            entries.append((4 * (i * CX) + 2, x_low[i], near))
            entries.append((4 * (i * CX + CX - 1) + 2, x_high[i], near))
            entries.append((4 * i + 3, z_low[i], near))
            entries.append((4 * ((CZ - 1) * CX + i) + 3, z_high[i], near))
        packs.append(gather_columns(ref[...], entries))
    low, high = packs
    ya_out[...] = jnp.where(py, high, low)
    yb_out[...] = jnp.where(py, low, high)
    for i, rows in enumerate((x_low, x_high)):
        ea_out[i * NE:(i + 1) * NE, :] = jnp.where(pz, rows[CZ - 1], rows[0])
        eb_out[i * NE:(i + 1) * NE, :] = jnp.where(pz, rows[0], rows[CZ - 1])


def column(row):
    square = jnp.broadcast_to(row, (NE, NE))
    across = lax.broadcasted_iota(jnp.int32, (NE, NE), 1)
    down = lax.broadcasted_iota(jnp.int32, (NE, NE), 0)
    return jnp.sum(jnp.where(across == down, square, 0.0), axis=1, keepdims=True)


def coefficients(diff_ref, loss_ref):
    return [jnp.broadcast_to(column(ref[...]), (NE, CY)) for ref in (diff_ref, loss_ref)]


def inside(axis):
    at = lax.axis_index(axis)
    return at > 0, at < lax.axis_size(axis) - 1


def stepper(diff, loss):
    top = lax.broadcasted_iota(jnp.int32, (NE, CY), 0) == NE - 1

    def update(c, beside):
        flux = loss * c
        above = jnp.where(top, 0.0, pltpu.roll(flux, NE - 1, 0))
        return c + diff * (beside - 6.0 * c) + above - flux

    return update


def inner_steps(cr_ref, xa, xb, za, zb, diff_ref, loss_ref, inner_ref):
    px, pz = even("gx"), even("gz")
    lane = lanes()
    diff, loss = coefficients(diff_ref, loss_ref)
    update = stepper(diff, loss)
    cells = native(cr_ref)
    x_low, x_high = halo_rows(px, xa, xb, 2 * CZ)
    z_low, z_high = halo_rows(pz, za, zb, 2 * CX)

    def along_y(c):
        return jnp.where(lane == CY - 1, 0.0, pltpu.roll(c, CY - 1, 1)) + jnp.where(lane == 0, 0.0, pltpu.roll(c, 1, 1))

    def at(z, x):
        if 0 <= z < CZ and 0 <= x < CX:
            return cells[z * CX + x]
        if 0 <= z < CZ:
            return x_low[(-1 - x) * CZ + z] if x < 0 else x_high[(x - CX) * CZ + z]
        if 0 <= x < CX:
            return z_low[(-1 - z) * CX + x] if z < 0 else z_high[(z - CZ) * CX + x]
        return None

    def around(get, z, x):
        found = [get(z + 1, x), get(z - 1, x), get(z, x + 1), get(z, x - 1)]
        found = [values for values in found if values is not None]
        return sum(found[1:], found[0])

    now = {}
    for z in range(-1, CZ + 1):
        for x in range(-1, CX + 1):
            if at(z, x) is None:
                continue
            new = around(at, z, x)
            if 0 <= z < CZ and 0 <= x < CX:
                now[z, x] = update(at(z, x), new + along_y(at(z, x)))
            else:
                axis, upper = ("gx", x > 0) if 0 <= z < CZ else ("gz", z > 0)
                now[z, x] = jnp.where(inside(axis)[1 if upper else 0], update(at(z, x), new), 0.0)
    for z in range(CZ):
        for x in range(CX):
            c = now[z, x]
            halos = [at(*there) for there in ((z + 1, x), (z - 1, x), (z, x + 1), (z, x - 1))
                     if not (0 <= there[0] < CZ and 0 <= there[1] < CX)]
            mixed = c + diff * sum(halos[1:], halos[0]) if halos else c
            row = (z * CX + x) * NE
            inner_ref[row:row + NE, :] = update(c, around(lambda *there: now[there], z, x) + along_y(mixed))


def y_corrections(pack, own, diff, loss, update, here):
    place = lax.div(lanes(), 4)
    cx, cz = lax.rem(place, CX), lax.div(place, CX)
    deep, x_edge, z_edge = moved(pack, -1), moved(pack, -2), moved(pack, -3)

    def around(values, x_halo, z_halo):
        return (
            jnp.where(cz == CZ - 1, z_halo, moved(values, -4 * CX)) + jnp.where(cz == 0, z_halo, moved(values, 4 * CX))
            + jnp.where(cx == CX - 1, x_halo, moved(values, -4)) + jnp.where(cx == 0, x_halo, moved(values, 4))
        )

    beyond = jnp.where(here, update(pack, around(pack, x_edge, z_edge) + deep + own), 0.0)
    first = diff * pack
    outer = update(first, around(first, diff * x_edge, diff * z_edge) + beyond)
    return outer, diff * first


def project(owner_any, lanes_any, inner_ref, low_ref, high_ref, ya, yb, ea, eb, diff_ref, loss_ref, gas_ref, weight_ref,
            cells_ref, send_any, parts_ref, blocks_ref, owner_ref, sem, owner_sem):
    del lanes_any
    fetch = pltpu.make_async_copy(owner_any, owner_ref, owner_sem)
    fetch.start()
    py, pz = even("gy"), even("gz")
    lane = lanes()
    diff, loss = coefficients(diff_ref, loss_ref)
    update = stepper(diff, loss)
    e_low, e_high = halo_rows(pz, ea, eb, 2)
    (y_low,), (y_high,) = halo_rows(py, ya, yb, 1)
    below, beyond = inside("gy")
    outer_low, next_low = y_corrections(y_low, low_ref[...], diff, loss, update, below)
    outer_high, next_high = y_corrections(y_high, high_ref[...], diff, loss, update, beyond)
    kind = lax.rem(lane, 4)
    mixed = jnp.where(kind == 0, outer_low, moved(next_low, 1))
    mixed = jnp.where(kind == 3, moved(outer_high, -1), mixed)
    mixed = jnp.where(kind == 2, moved(next_high, -2), mixed)
    rim = (lane < 2) | (lane >= CY - 2)
    corners = {0: e_low[0], CX - 1: e_low[1], (CZ - 1) * CX: e_high[0], ZX - 1: e_high[1]}
    for zx in range(ZX):
        cell = tile(inner_ref, zx) + jnp.where(rim, moved(mixed, -4 * zx), 0.0)
        if zx in corners:
            cell = cell + 2.0 * diff * diff * corners[zx]
        cells_ref[zx * NE:(zx + 1) * NE, :] = cell
        lit = cell * gas_ref[zx:zx + 1, :]
        upper = lit.astype(jnp.bfloat16)
        parts_ref[0:NE, zx * CY:(zx + 1) * CY] = upper
        parts_ref[NE:2 * NE, zx * CY:(zx + 1) * CY] = (lit - upper.astype(jnp.float32)).astype(jnp.bfloat16)
    weights = jnp.concatenate([weight_ref[s] for s in range(KS)], axis=1)
    product = jnp.dot(parts_ref[...], weights, preferred_element_type=jnp.float32)
    product = product[:NE] + product[NE:]
    for s in range(KS):
        blocks_ref[s * NE:(s + 1) * NE, :] = product[:, s * PB:(s + 1) * PB]
    fetch.wait()
    copies = []
    for s in range(KS):
        row = pl.multiple_of(owner_ref[s] * LANE + place_of(owner_ref, s) * NE, 8)
        copies.append(pltpu.make_async_copy(blocks_ref.at[pl.ds(s * NE, NE)], send_any.at[pl.ds(row, NE)], sem.at[s]))
        copies[s].start()
    for copy in copies:
        copy.wait()


def finish_density(cells_ref, final_ref):
    for zx in range(ZX):
        final_ref[pl.ds(zx, NE, stride=ZX), :] = tile(cells_ref, zx)


def gather_sky(recv_ref, table_ref, sky_ref):
    count = recv_ref.shape[0] // LANE
    total = [jnp.zeros((NE, PB), jnp.float32) for _ in range(BO)]
    for j in range(count):
        for k in range(CAP):
            block = recv_ref[j * LANE + k * NE:j * LANE + (k + 1) * NE, :]
            for b in range(BO):
                row = j * LANE + CAP * NE + k * BO + b
                total[b] = total[b] + block * recv_ref[row:row + 1, :]
    for b in range(BO):
        sky_ref[b * NG:(b + 1) * NG, :] = jnp.dot(
            table_ref[...], total[b], precision=lax.Precision.HIGHEST, preferred_element_type=jnp.float32
        )


def f32(*shape):
    return jax.ShapeDtypeStruct(shape, jnp.float32)


def cost(us):
    return pl.CostEstimate(flops=0, transcendentals=0, bytes_accessed=us * 3000000)


def call(body, name, outs, in_specs, us, out_specs=None, scratch=(), aliases=None):
    return pl.pallas_call(
        body,
        name=name,
        out_shape=outs,
        in_specs=in_specs,
        out_specs=out_specs or [VMEM] * len(outs),
        scratch_shapes=list(scratch),
        input_output_aliases=aliases or {},
        cost_estimate=cost(us),
        compiler_params=pltpu.CompilerParams(vmem_limit_bytes=SMALL),
    )


def swap(values, axis, start):
    pairs = []
    for i in range(start, lax.axis_size(axis) - 1, 2):
        pairs += [(i, i + 1), (i + 1, i)]
    return lax.ppermute(values, axis, pairs)


def body(cr_init, gas, diff_coeff, loss_coeff, pi0_table, los_weight, slot_owner, slot_block):
    start = cr_init.reshape(NE * ZX, CY)
    diff, loss = diff_coeff.reshape(1, NE), loss_coeff.reshape(1, NE)
    column_pack, edge_rows = f32(NE, CY), f32(2 * NE, CY)
    xa, xb, za, zb = call(first_faces, "first_faces", [f32(2 * 4 * NE, CY)] * 4, [VMEM], 1)(start)
    xb = swap(xb, "gx", 1)
    xa = swap(xa, "gx", 0)
    za = swap(za, "gz", 0)
    zb = swap(zb, "gz", 1)
    owner, owners = slot_owner.reshape(KS), lax.axis_size("gy")
    (blank,) = call(
        blank_lanes,
        "blank_lanes",
        [f32(owners * LANE, PB)],
        [ANY] * 2,
        1,
        scratch=[pltpu.SMEM((KS,), jnp.int32), pltpu.SMEM((KS,), jnp.int32), pltpu.SemaphoreType.DMA((2,))],
    )(owner, slot_block.reshape(KS))
    low, high = call(own_columns, "own_columns", [column_pack] * 2, [VMEM, ANY], 1)(start, blank)
    ya, yb, ea, eb = call(edge_faces, "edge_faces", [column_pack] * 2 + [edge_rows] * 2, [VMEM] * 6, 1)(
        xa, xb, za, zb, low, high
    )
    yb = swap(yb, "gy", 1)
    ya = swap(ya, "gy", 0)
    ea = swap(ea, "gz", 0)
    eb = swap(eb, "gz", 1)
    (inner,) = call(inner_steps, "inner_steps", [f32(ZX * NE, CY)], [VMEM] * 7, 2)(start, xa, xb, za, zb, diff, loss)
    cells, send = call(
        project,
        "project",
        [f32(ZX * NE, CY), f32(owners * LANE, PB)],
        [ANY] * 2 + [VMEM] * 11,
        2,
        out_specs=[VMEM, ANY],
        scratch=[
            pltpu.VMEM((2 * NE, ZX * CY), jnp.bfloat16),
            pltpu.VMEM((KS * NE, PB), jnp.float32),
            pltpu.SMEM((KS,), jnp.int32),
            pltpu.SemaphoreType.DMA((KS,)),
            pltpu.SemaphoreType.DMA,
        ],
        aliases={1: 1},
    )(
        owner, blank, inner, low, high, ya, yb, ea, eb, diff, loss,
        gas.reshape(ZX, CY), los_weight.reshape(KS, ZX * CY, PB),
    )
    (final,) = call(finish_density, "finish_density", [f32(NE * ZX, CY)], [VMEM], 2)(cells)
    recv = lax.all_to_all(send.reshape(owners, LANE, PB), "gy", 0, 0, tiled=True)
    (sky,) = call(gather_sky, "gather_sky", [f32(BO * NG, PB)], [VMEM] * 2, 1)(
        recv.reshape(owners * LANE, PB), pi0_table
    )
    return final.reshape(cr_init.shape), sky.reshape(1, 1, BO, NG, PB)


def solution(mesh):
    in_specs = (
        P(None, "gz", "gx", "gy"),
        P("gz", "gx", "gy"),
        P(),
        P(),
        P(),
        P("gz", "gx", "gy", None, None, None),
        P("gz", "gx", "gy", None, None),
        P("gz", "gx", "gy", None),
    )
    out_specs = (P(None, "gz", "gx", "gy"), P("gz", "gx", "gy", None, None))
    return jax.shard_map(body, mesh=mesh, in_specs=in_specs, out_specs=out_specs, check_vma=False)
```

time: 82.3 us -> 76.8 us (0.933)
  waiting for transfers between devices: 38.2 us -> 32.5 us
  local copies, waits for them, and re-layouts: 1.16 us -> 2.46 us
  Pallas kernels: 9.37 us -> 8.12 us
    ppermute x8, waiting for transfers between devices: 12.2 us -> 7.54 us  [swap(): return lax.ppermute(values, axis, pairs)]
    unnamed x17 -> x21, local copies, waits for them, and re-layouts: 1.16 us -> 2.46 us
    pallas_call x4 -> x8, Pallas kernels: 9.37 us -> 8.12 us  [the longest x1 2 us: body(): call(project, 'project', [f32(ZX * NE, CY), f32(owners * LANE, PB)], [ANY...]
    all_to_all x1, waiting for transfers between devices: 26 us -> 24.9 us  [body(): lax.all_to_all(send.reshape(owners, LANE, PB), 'gy', 0, 0, tiled=True)]
  transfers between devices with their start and end apart: 9 -> 9, of which waited for: 4 -> 3; matrix products, arithmetic and copies ran while one was open for 0% -> 0% of each run, Pallas kernels for 0% -> 6%
where the time goes in v3:
time: 76.8 us; the launch traced here: 76.2 us
  waiting for transfers between devices  32.5 us (42%)
  starting transfers between devices  32.3 us (42%)
  Pallas kernels  8.12 us (11%)
  local copies, waits for them, and re-layouts  2.46 us (3%)
  between operations  0.85 us (1%)
    all_to_all x1, waiting for transfers between devices, body(): lax.all_to_all(send.reshape(owners, LANE, PB), 'gy', 0, 0, tiled=True)  24.9 us
    ppermute x8, starting transfers between devices, swap(): return lax.ppermute(values, axis, pairs)  23.5 us
    all_to_all x1, starting transfers between devices, body(): lax.all_to_all(send.reshape(owners, LANE, PB), 'gy', 0, 0, tiled=True)  8.84 us
    ppermute x8, waiting for transfers between devices, swap(): return lax.ppermute(values, axis, pairs)  7.54 us
    unnamed x21, local copies, waits for them, and re-layouts  2.46 us
    pallas_call x1, Pallas kernels, body(): call(project, 'project', [f32(ZX * NE, CY), f32(owners * LANE, PB)], [ANY...  2 us
    pallas_call x1, Pallas kernels, body(): call(blank_lanes, 'blank_lanes', [f32(owners * LANE, PB)], [ANY] * 2, 1,...  1.63 us
  transfers between devices with their start and end apart: 9, of which 3 were waited for; matrix products, arithmetic and copies ran while one was open for 0% of the time, Pallas kernels for 6%

profile of v3, /device:TPU:328, one launch (start us, length us, event | category | flops | bytes accessed | tf_op | source)
XLA Modules:
  0.0 76.2 jit_solution(3284796450745951400)
XLA Ops:
  0.6 0.0 copy-start
  0.6 1.0 %copy-done = f32[64,4,4,128]{3,2,1,0:T(4,128)S(1)} copy-done((f32[64,4,4,128]{3,2,1,0:T(4,128)S(1)}, f32[64,4,4,128]{3,2,1,0:T(4,128)}, u32[]{:S(2)}) %copy-start) | copy-done | bytes 524312
  1.7 0.0 copy-start.1
  1.7 0.2 first_faces.1
  1.9 1.9 %collective-permute-start = (f32[512,128]{1,0:T(8,128)S(1)}, f32[512,128]{1,0:T(8,128)S(1)}, u32[]{:S(2)}, u32[]{:S(2)}) collective-permute-start(f32[512,128]{1,0:T(8,128)S(1)} %get-tuple-element.14), channel_id=1, source_target_pairs={{0,64},{64,0},{128,192},{192,128},{256,320},{320,256},{384,448},{4... | collective-permute-start | bytes 786440 | tf_op jit(solution)/shard_map/ppermute | solution.py:301
  3.8 2.6 %collective-permute-start.1 = (f32[512,128]{1,0:T(8,128)S(1)}, f32[512,128]{1,0:T(8,128)S(1)}, u32[]{:S(2)}, u32[]{:S(2)}) collective-permute-start(f32[512,128]{1,0:T(8,128)S(1)} %get-tuple-element.15), channel_id=1, source_target_pairs={{64,128},{128,64},{192,256},{256,192},{320,384},{384,320},{65,129}... | collective-permute-start | bytes 786440 | tf_op jit(solution)/shard_map/ppermute | solution.py:301
  6.3 2.4 %collective-permute-start.2 = (f32[512,128]{1,0:T(8,128)S(1)}, f32[512,128]{1,0:T(8,128)S(1)}, u32[]{:S(2)}, u32[]{:S(2)}) collective-permute-start(f32[512,128]{1,0:T(8,128)S(1)} %get-tuple-element.16), channel_id=1, source_target_pairs={{0,1},{1,0},{2,3},{3,2},{4,5},{5,4},{6,7},{7,6},{8,9},{9,8},{10,11... | collective-permute-start | bytes 786440 | tf_op jit(solution)/shard_map/ppermute | solution.py:301
  8.7 4.3 %collective-permute-start.3 = (f32[512,128]{1,0:T(8,128)S(1)}, f32[512,128]{1,0:T(8,128)S(1)}, u32[]{:S(2)}, u32[]{:S(2)}) collective-permute-start(f32[512,128]{1,0:T(8,128)S(1)} %get-tuple-element.17), channel_id=1, source_target_pairs={{1,2},{2,1},{5,6},{6,5},{9,10},{10,9},{13,14},{14,13},{17,18},{18,... | collective-permute-start | bytes 786440 | tf_op jit(solution)/shard_map/ppermute | solution.py:301
  13.0 0.0 copy-start.4
  13.1 0.6 copy-done.4
  13.7 0.0 copy-start.8
  13.7 0.7 copy-done.8
  14.4 0.0 copy-start.6
  14.4 0.0 copy-start.7
  14.4 1.6 %blank_lanes.1.blank_any.lanes_any = f32[2176,128]{1,0:T(8,128)} custom-call(s32[7]{0:T(128)S(1)} %bitcast.17, s32[7]{0:T(128)S(1)} %bitcast.23), custom_call_target="tpu_custom_call" | custom-call | bytes 3000000 | tf_op jit(solution)/shard_map/blank_lanes/pallas_call | solution.py:314
  16.0 0.0 copy-done.1
  16.0 0.0 copy-start.2
  16.0 0.6 own_columns.1
  16.6 0.0 collective-permute-done.xa
  16.6 3.0 %collective-permute-done.1.xb = f32[512,128]{1,0:T(8,128)S(1)} collective-permute-done((f32[512,128]{1,0:T(8,128)S(1)}, f32[512,128]{1,0:T(8,128)S(1)}, u32[]{:S(2)}, u32[]{:S(2)}) %collective-permute-start.1) | collective-permute-done | bytes 262176 | tf_op jit(solution)/shard_map/ppermute | solution.py:301
  19.6 0.0 collective-permute-done.2.za
  19.6 0.0 collective-permute-done.3.zb
  19.6 0.3 edge_faces.1
  20.0 0.0 copy-start.3
  20.0 0.0 copy-start.5
  20.0 2.4 %collective-permute-start.6 = (f32[128,128]{1,0:T(8,128)S(1)}, f32[128,128]{1,0:T(8,128)S(1)}, u32[]{:S(2)}, u32[]{:S(2)}) collective-permute-start(f32[128,128]{1,0:T(8,128)S(1)} %get-tuple-element.22), channel_id=1, source_target_pairs={{0,1},{1,0},{2,3},{3,2},{4,5},{5,4},{6,7},{7,6},{8,9},{9,8},{10,11... | collective-permute-start | bytes 196616 | tf_op jit(solution)/shard_map/ppermute | solution.py:301
  22.4 4.3 %collective-permute-start.7 = (f32[128,128]{1,0:T(8,128)S(1)}, f32[128,128]{1,0:T(8,128)S(1)}, u32[]{:S(2)}, u32[]{:S(2)}) collective-permute-start(f32[128,128]{1,0:T(8,128)S(1)} %get-tuple-element.23), channel_id=1, source_target_pairs={{1,2},{2,1},{5,6},{6,5},{9,10},{10,9},{13,14},{14,13},{17,18},{18,... | collective-permute-start | bytes 196616 | tf_op jit(solution)/shard_map/ppermute | solution.py:301
  26.7 3.4 %collective-permute-start.4 = (f32[64,128]{1,0:T(8,128)S(1)}, f32[64,128]{1,0:T(8,128)S(1)}, u32[]{:S(2)}, u32[]{:S(2)}) collective-permute-start(f32[64,128]{1,0:T(8,128)S(1)} %get-tuple-element.20), channel_id=1, source_target_pairs={{0,4},{4,0},{8,12},{12,8},{16,20},{20,16},{24,28},{28,24},{32,36},... | collective-permute-start | bytes 98312 | tf_op jit(solution)/shard_map/ppermute | solution.py:301
  30.1 2.3 %collective-permute-start.5 = (f32[64,128]{1,0:T(8,128)S(1)}, f32[64,128]{1,0:T(8,128)S(1)}, u32[]{:S(2)}, u32[]{:S(2)}) collective-permute-start(f32[64,128]{1,0:T(8,128)S(1)} %get-tuple-element.21), channel_id=1, source_target_pairs={{4,8},{8,4},{12,16},{16,12},{20,24},{24,20},{28,32},{32,28},{36,40... | collective-permute-start | bytes 98312 | tf_op jit(solution)/shard_map/ppermute | solution.py:301
  32.4 0.0 copy-done.6
  32.4 0.0 copy-done.7
  32.4 1.1 %inner_steps.1.inner_ref = f32[1024,128]{1,0:T(8,128)S(1)} custom-call(f32[1024,128]{1,0:T(8,128)S(1)} %bitcast.13, f32[512,128]{1,0:T(8,128)S(1)} %collective-permute-done.xa, f32[512,128]{1,0:T(8,128)S(1)} %collective-permute-done.1.xb, f32[512,128]{1,0:T(8,128)S(1)} %collective-permute-done.2.za, f32[512,128]{1,0:T(8,128)S(1)} %collective-permute-done.3.zb, ...), custom_call_target="tpu_custom_call" | custom-call | bytes 6000000 | tf_op jit(solution)/shard_map/inner_steps/pallas_call | solution.py:330
  33.5 0.0 collective-permute-done.4.ya
  33.5 4.5 %collective-permute-done.5.yb = f32[64,128]{1,0:T(8,128)S(1)} collective-permute-done((f32[64,128]{1,0:T(8,128)S(1)}, f32[64,128]{1,0:T(8,128)S(1)}, u32[]{:S(2)}, u32[]{:S(2)}) %collective-permute-start.5) | collective-permute-done | bytes 32800 | tf_op jit(solution)/shard_map/ppermute | solution.py:301
  38.0 0.0 collective-permute-done.6.ea
  38.0 0.0 collective-permute-done.7.eb
  38.0 0.0 copy-done.2
  38.0 0.0 copy-done.3
  38.0 0.0 copy-done.5
  38.0 2.0 %project.1 = (f32[1024,128]{1,0:T(8,128)S(1)}, f32[2176,128]{1,0:T(8,128)}) custom-call(s32[7]{0:T(128)S(1)} %bitcast.18, f32[2176,128]{1,0:T(8,128)} %blank_lanes.1.blank_any.lanes_any, f32[1024,128]{1,0:T(8,128)S(1)} %inner_steps.1.inner_ref, f32[64,128]{1,0:T(8,128)S(1)} %get-tuple-element.18.low_ref, ...), custom_call_target="tpu_custom_call", output_to_operand_aliasing={{1}: (1, {})} | custom-call | bytes 6000000 | tf_op jit(solution)/shard_map/project/pallas_call | solution.py:331
  40.0 0.0 copy-start.9
  40.1 8.8 %all-to-all-start = ((f32[16,136,128]{2,1,0:T(8,128)}), f32[16,136,128]{2,1,0:T(8,128)S(1)}, u32[]{:S(2)}, u32[]{:S(2)}) async-start(f32[16,136,128]{2,1,0:T(8,128)} %bitcast.8), calls=%async_computation | async-start | bytes 2228224 | tf_op jit(solution)/shard_map/all_to_all | solution.py:351
  48.9 0.0 copy-done.9
  48.9 0.1 copy.11.table_ref
  49.0 1.0 %finish_density.1 = f32[1024,128]{1,0:T(8,128)} custom-call(f32[1024,128]{1,0:T(8,128)S(1)} %get-tuple-element.24.cells_ref), custom_call_target="tpu_custom_call" | custom-call | bytes 6000000 | tf_op jit(solution)/shard_map/finish_density/pallas_call | solution.py:350
  50.0 24.9 %all-to-all-done = f32[16,136,128]{2,1,0:T(8,128)S(1)} async-done(((f32[16,136,128]{2,1,0:T(8,128)}), f32[16,136,128]{2,1,0:T(8,128)S(1)}, u32[]{:S(2)}, u32[]{:S(2)}) %all-to-all-start) | async-done | bytes 1114144 | tf_op jit(solution)/shard_map/all_to_all | solution.py:351
  75.0 1.3 %gather_sky.1 = f32[384,128]{1,0:T(8,128)} custom-call(f32[2176,128]{1,0:T(8,128)S(1)} %bitcast.14, f32[96,64]{1,0:T(8,128)S(1)} %copy.11.table_ref), custom_call_target="tpu_custom_call" | custom-call | bytes 3000000 | tf_op jit(solution)/shard_map/gather_sky/pallas_call | solution.py:352
Async XLA Ops:
  0.6 1.0 %copy-start = (f32[64,4,4,128]{3,2,1,0:T(4,128)S(1)}, f32[64,4,4,128]{3,2,1,0:T(4,128)}, u32[]{:S(2)}) copy-start(f32[64,4,4,128]{3,2,1,0:T(4,128)} %param.8) | copy-start | bytes 1572868
  1.7 14.3 %copy-start.1 = (f32[64,4,4,128]{3,2,1,0:T(4,128)S(1)}, f32[64,4,4,128]{3,2,1,0:T(4,128)}, u32[]{:S(2)}) copy-start(f32[64,4,4,128]{3,2,1,0:T(4,128)} %param.8) | copy-start | bytes 1572868
  1.9 14.7 %collective-permute-start = (f32[512,128]{1,0:T(8,128)S(1)}, f32[512,128]{1,0:T(8,128)S(1)}, u32[]{:S(2)}, u32[]{:S(2)}) collective-permute-start(f32[512,128]{1,0:T(8,128)S(1)} %get-tuple-element.14), channel_id=1, source_target_pairs={{0,64},{64,0},{128,192},{192,128},{256,320},{320,256},{384,448},{4... | collective-permute-start | bytes 786440 | tf_op jit(solution)/shard_map/ppermute | solution.py:301
  3.8 15.8 %collective-permute-start.1 = (f32[512,128]{1,0:T(8,128)S(1)}, f32[512,128]{1,0:T(8,128)S(1)}, u32[]{:S(2)}, u32[]{:S(2)}) collective-permute-start(f32[512,128]{1,0:T(8,128)S(1)} %get-tuple-element.15), channel_id=1, source_target_pairs={{64,128},{128,64},{192,256},{256,192},{320,384},{384,320},{65,129}... | collective-permute-start | bytes 786440 | tf_op jit(solution)/shard_map/ppermute | solution.py:301
  6.3 13.3 %collective-permute-start.2 = (f32[512,128]{1,0:T(8,128)S(1)}, f32[512,128]{1,0:T(8,128)S(1)}, u32[]{:S(2)}, u32[]{:S(2)}) collective-permute-start(f32[512,128]{1,0:T(8,128)S(1)} %get-tuple-element.16), channel_id=1, source_target_pairs={{0,1},{1,0},{2,3},{3,2},{4,5},{5,4},{6,7},{7,6},{8,9},{9,8},{10,11... | collective-permute-start | bytes 786440 | tf_op jit(solution)/shard_map/ppermute | solution.py:301
  8.7 10.9 %collective-permute-start.3 = (f32[512,128]{1,0:T(8,128)S(1)}, f32[512,128]{1,0:T(8,128)S(1)}, u32[]{:S(2)}, u32[]{:S(2)}) collective-permute-start(f32[512,128]{1,0:T(8,128)S(1)} %get-tuple-element.17), channel_id=1, source_target_pairs={{1,2},{2,1},{5,6},{6,5},{9,10},{10,9},{13,14},{14,13},{17,18},{18,... | collective-permute-start | bytes 786440 | tf_op jit(solution)/shard_map/ppermute | solution.py:301
  13.0 0.7 copy-start.4
  13.7 0.7 copy-start.8
  14.4 18.0 %copy-start.6 = (f32[64]{0:T(128)S(1)}, f32[64]{0:T(128)}, u32[]{:S(2)}) copy-start(f32[64]{0:T(128)} %param.10) | copy-start | bytes 772
  14.4 18.0 %copy-start.7 = (f32[64]{0:T(128)S(1)}, f32[64]{0:T(128)}, u32[]{:S(2)}) copy-start(f32[64]{0:T(128)} %param.11) | copy-start | bytes 772
  16.0 22.0 %copy-start.2 = (bf16[1,1,1,7,2048,128]{5,4,3,2,1,0:T(8,128)(2,1)S(1)}, bf16[1,1,1,7,2048,128]{5,4,3,2,1,0:T(8,128)(2,1)}, u32[]{:S(2)}) copy-start(bf16[1,1,1,7,2048,128]{5,4,3,2,1,0:T(8,128)(2,1)} %param.13) | copy-start | bytes 11010052
  20.0 18.1 %copy-start.3 = (f32[4,4,128]{2,1,0:T(4,128)S(1)}, f32[4,4,128]{2,1,0:T(4,128)}, u32[]{:S(2)}) copy-start(f32[4,4,128]{2,1,0:T(4,128)} %param.9) | copy-start | bytes 24580
  20.0 18.1 %copy-start.5 = (s32[1,1,1,7,1]{3,4,2,1,0:T(1,128)S(1)}, s32[1,1,1,7,1]{3,4,2,1,0:T(1,128)}, u32[]{:S(2)}) copy-start(s32[1,1,1,7,1]{3,4,2,1,0:T(1,128)} %param.14) | copy-start | bytes 88
  20.0 18.0 %collective-permute-start.6 = (f32[128,128]{1,0:T(8,128)S(1)}, f32[128,128]{1,0:T(8,128)S(1)}, u32[]{:S(2)}, u32[]{:S(2)}) collective-permute-start(f32[128,128]{1,0:T(8,128)S(1)} %get-tuple-element.22), channel_id=1, source_target_pairs={{0,1},{1,0},{2,3},{3,2},{4,5},{5,4},{6,7},{7,6},{8,9},{9,8},{10,11... | collective-permute-start | bytes 196616 | tf_op jit(solution)/shard_map/ppermute | solution.py:301
  22.4 15.7 %collective-permute-start.7 = (f32[128,128]{1,0:T(8,128)S(1)}, f32[128,128]{1,0:T(8,128)S(1)}, u32[]{:S(2)}, u32[]{:S(2)}) collective-permute-start(f32[128,128]{1,0:T(8,128)S(1)} %get-tuple-element.23), channel_id=1, source_target_pairs={{1,2},{2,1},{5,6},{6,5},{9,10},{10,9},{13,14},{14,13},{17,18},{18,... | collective-permute-start | bytes 196616 | tf_op jit(solution)/shard_map/ppermute | solution.py:301
  26.7 6.8 %collective-permute-start.4 = (f32[64,128]{1,0:T(8,128)S(1)}, f32[64,128]{1,0:T(8,128)S(1)}, u32[]{:S(2)}, u32[]{:S(2)}) collective-permute-start(f32[64,128]{1,0:T(8,128)S(1)} %get-tuple-element.20), channel_id=1, source_target_pairs={{0,4},{4,0},{8,12},{12,8},{16,20},{20,16},{24,28},{28,24},{32,36},... | collective-permute-start | bytes 98312 | tf_op jit(solution)/shard_map/ppermute | solution.py:301
  30.1 7.9 %collective-permute-start.5 = (f32[64,128]{1,0:T(8,128)S(1)}, f32[64,128]{1,0:T(8,128)S(1)}, u32[]{:S(2)}, u32[]{:S(2)}) collective-permute-start(f32[64,128]{1,0:T(8,128)S(1)} %get-tuple-element.21), channel_id=1, source_target_pairs={{4,8},{8,4},{12,16},{16,12},{20,24},{24,20},{28,32},{32,28},{36,40... | collective-permute-start | bytes 98312 | tf_op jit(solution)/shard_map/ppermute | solution.py:301
  40.0 8.9 %copy-start.9 = (f32[96,64]{0,1:T(8,128)S(1)}, f32[96,64]{0,1:T(8,128)}, u32[]{:S(2)}) copy-start(f32[96,64]{0,1:T(8,128)} %param.12) | copy-start | bytes 73732
  40.1 34.9 %all-to-all-start = ((f32[16,136,128]{2,1,0:T(8,128)}), f32[16,136,128]{2,1,0:T(8,128)S(1)}, u32[]{:S(2)}, u32[]{:S(2)}) async-start(f32[16,136,128]{2,1,0:T(8,128)} %bitcast.8), calls=%async_computation | async-start | bytes 2228224 | tf_op jit(solution)/shard_map/all_to_all | solution.py:351

commit v4 on v3

--- a/solution.py
+++ b/solution.py
@@ -110,8 +110,10 @@
             entries.append((4 * ((CZ - 1) * CX + i) + 3, z_high[i], near))
         packs.append(gather_columns(ref[...], entries))
     low, high = packs
-    ya_out[...] = jnp.where(py, high, low)
-    yb_out[...] = jnp.where(py, low, high)
+    ya_out[0:NE, :] = jnp.where(py, high, low)
+    yb_out[0:NE, :] = jnp.where(py, low, high)
+    for ref in (ya_out, yb_out):
+        ref[NE:2 * NE, :] = jnp.zeros((NE, CY), jnp.float32)
     for i, rows in enumerate((x_low, x_high)):
         ea_out[i * NE:(i + 1) * NE, :] = jnp.where(pz, rows[CZ - 1], rows[0])
         eb_out[i * NE:(i + 1) * NE, :] = jnp.where(pz, rows[0], rows[CZ - 1])
@@ -320,7 +322,7 @@
         scratch=[pltpu.SMEM((KS,), jnp.int32), pltpu.SMEM((KS,), jnp.int32), pltpu.SemaphoreType.DMA((2,))],
     )(owner, slot_block.reshape(KS))
     low, high = call(own_columns, "own_columns", [column_pack] * 2, [VMEM, ANY], 1)(start, blank)
-    ya, yb, ea, eb = call(edge_faces, "edge_faces", [column_pack] * 2 + [edge_rows] * 2, [VMEM] * 6, 1)(
+    ya, yb, ea, eb = call(edge_faces, "edge_faces", [edge_rows] * 4, [VMEM] * 6, 1)(
         xa, xb, za, zb, low, high
     )
     yb = swap(yb, "gy", 1)

time: 76.8 us -> 74.9 us (0.975)
  the two profiles are of different devices: /device:TPU:328 before, /device:TPU:336 now
where the time goes in v4:
time: 74.9 us; the launch traced here: 74.4 us
  waiting for transfers between devices  33.1 us (44%)
  starting transfers between devices  29.8 us (40%)
  Pallas kernels  8.11 us (11%)
  local copies, waits for them, and re-layouts  2.46 us (3%)
  between operations  0.84 us (1%)
    all_to_all x1, waiting for transfers between devices, body(): lax.all_to_all(send.reshape(owners, LANE, PB), 'gy', 0, 0, tiled=True)  25 us
    ppermute x8, starting transfers between devices, swap(): return lax.ppermute(values, axis, pairs)  19.9 us
    all_to_all x1, starting transfers between devices, body(): lax.all_to_all(send.reshape(owners, LANE, PB), 'gy', 0, 0, tiled=True)  9.92 us
    ppermute x8, waiting for transfers between devices, swap(): return lax.ppermute(values, axis, pairs)  8.15 us
    unnamed x21, local copies, waits for them, and re-layouts  2.46 us
    pallas_call x1, Pallas kernels, body(): call(project, 'project', [f32(ZX * NE, CY), f32(owners * LANE, PB)], [ANY...  1.98 us
    pallas_call x1, Pallas kernels, body(): call(blank_lanes, 'blank_lanes', [f32(owners * LANE, PB)], [ANY] * 2, 1,...  1.63 us
  transfers between devices with their start and end apart: 9, of which 6 were waited for; matrix products, arithmetic and copies ran while one was open for 0% of the time, Pallas kernels for 6%

profile of v4, /device:TPU:336, one launch (start us, length us, event | category | flops | bytes accessed | tf_op | source)
XLA Modules:
  0.0 74.4 jit_solution(8322326916802460816)
XLA Ops:
  0.6 0.0 copy-start
  0.6 1.0 %copy-done = f32[64,4,4,128]{3,2,1,0:T(4,128)S(1)} copy-done((f32[64,4,4,128]{3,2,1,0:T(4,128)S(1)}, f32[64,4,4,128]{3,2,1,0:T(4,128)}, u32[]{:S(2)}) %copy-start) | copy-done | bytes 524312
  1.7 0.0 copy-start.1
  1.7 0.2 first_faces.1
  1.9 1.9 %collective-permute-start = (f32[512,128]{1,0:T(8,128)S(1)}, f32[512,128]{1,0:T(8,128)S(1)}, u32[]{:S(2)}, u32[]{:S(2)}) collective-permute-start(f32[512,128]{1,0:T(8,128)S(1)} %get-tuple-element.14), channel_id=1, source_target_pairs={{0,64},{64,0},{128,192},{192,128},{256,320},{320,256},{384,448},{4... | collective-permute-start | bytes 786440 | tf_op jit(solution)/shard_map/ppermute | solution.py:303
  3.8 2.6 %collective-permute-start.1 = (f32[512,128]{1,0:T(8,128)S(1)}, f32[512,128]{1,0:T(8,128)S(1)}, u32[]{:S(2)}, u32[]{:S(2)}) collective-permute-start(f32[512,128]{1,0:T(8,128)S(1)} %get-tuple-element.15), channel_id=1, source_target_pairs={{64,128},{128,64},{192,256},{256,192},{320,384},{384,320},{65,129}... | collective-permute-start | bytes 786440 | tf_op jit(solution)/shard_map/ppermute | solution.py:303
  6.3 3.2 %collective-permute-start.2 = (f32[512,128]{1,0:T(8,128)S(1)}, f32[512,128]{1,0:T(8,128)S(1)}, u32[]{:S(2)}, u32[]{:S(2)}) collective-permute-start(f32[512,128]{1,0:T(8,128)S(1)} %get-tuple-element.16), channel_id=1, source_target_pairs={{0,1},{1,0},{2,3},{3,2},{4,5},{5,4},{6,7},{7,6},{8,9},{9,8},{10,11... | collective-permute-start | bytes 786440 | tf_op jit(solution)/shard_map/ppermute | solution.py:303
  9.5 1.9 %collective-permute-start.3 = (f32[512,128]{1,0:T(8,128)S(1)}, f32[512,128]{1,0:T(8,128)S(1)}, u32[]{:S(2)}, u32[]{:S(2)}) collective-permute-start(f32[512,128]{1,0:T(8,128)S(1)} %get-tuple-element.17), channel_id=1, source_target_pairs={{1,2},{2,1},{5,6},{6,5},{9,10},{10,9},{13,14},{14,13},{17,18},{18,... | collective-permute-start | bytes 786440 | tf_op jit(solution)/shard_map/ppermute | solution.py:303
  11.5 0.0 copy-start.4
  11.5 0.6 copy-done.4
  12.1 0.0 copy-start.8
  12.1 0.7 copy-done.8
  12.8 0.0 copy-start.6
  12.8 0.0 copy-start.7
  12.8 1.6 %blank_lanes.1.blank_any.lanes_any = f32[2176,128]{1,0:T(8,128)} custom-call(s32[7]{0:T(128)S(1)} %bitcast.17, s32[7]{0:T(128)S(1)} %bitcast.23), custom_call_target="tpu_custom_call" | custom-call | bytes 3000000 | tf_op jit(solution)/shard_map/blank_lanes/pallas_call | solution.py:316
  14.4 0.0 copy-done.1
  14.4 0.0 copy-start.2
  14.5 0.6 own_columns.1
  15.0 0.0 collective-permute-done.xa
  15.0 4.6 %collective-permute-done.1.xb = f32[512,128]{1,0:T(8,128)S(1)} collective-permute-done((f32[512,128]{1,0:T(8,128)S(1)}, f32[512,128]{1,0:T(8,128)S(1)}, u32[]{:S(2)}, u32[]{:S(2)}) %collective-permute-start.1) | collective-permute-done | bytes 262176 | tf_op jit(solution)/shard_map/ppermute | solution.py:303
  19.6 0.0 collective-permute-done.2.za
  19.6 0.5 collective-permute-done.3.zb
  20.1 0.3 edge_faces.1
  20.4 0.0 copy-start.3
  20.4 0.0 copy-start.5
  20.5 3.4 %collective-permute-start.4 = (f32[128,128]{1,0:T(8,128)S(1)}, f32[128,128]{1,0:T(8,128)S(1)}, u32[]{:S(2)}, u32[]{:S(2)}) collective-permute-start(f32[128,128]{1,0:T(8,128)S(1)} %get-tuple-element.20), channel_id=1, source_target_pairs={{0,4},{4,0},{8,12},{12,8},{16,20},{20,16},{24,28},{28,24},{32,36},... | collective-permute-start | bytes 196616 | tf_op jit(solution)/shard_map/ppermute | solution.py:303
  23.9 3.1 %collective-permute-start.5 = (f32[128,128]{1,0:T(8,128)S(1)}, f32[128,128]{1,0:T(8,128)S(1)}, u32[]{:S(2)}, u32[]{:S(2)}) collective-permute-start(f32[128,128]{1,0:T(8,128)S(1)} %get-tuple-element.21), channel_id=1, source_target_pairs={{4,8},{8,4},{12,16},{16,12},{20,24},{24,20},{28,32},{32,28},{36,40... | collective-permute-start | bytes 196616 | tf_op jit(solution)/shard_map/ppermute | solution.py:303
  27.0 1.9 %collective-permute-start.6 = (f32[128,128]{1,0:T(8,128)S(1)}, f32[128,128]{1,0:T(8,128)S(1)}, u32[]{:S(2)}, u32[]{:S(2)}) collective-permute-start(f32[128,128]{1,0:T(8,128)S(1)} %get-tuple-element.22), channel_id=1, source_target_pairs={{0,1},{1,0},{2,3},{3,2},{4,5},{5,4},{6,7},{7,6},{8,9},{9,8},{10,11... | collective-permute-start | bytes 196616 | tf_op jit(solution)/shard_map/ppermute | solution.py:303
  28.9 1.9 %collective-permute-start.7 = (f32[128,128]{1,0:T(8,128)S(1)}, f32[128,128]{1,0:T(8,128)S(1)}, u32[]{:S(2)}, u32[]{:S(2)}) collective-permute-start(f32[128,128]{1,0:T(8,128)S(1)} %get-tuple-element.23), channel_id=1, source_target_pairs={{1,2},{2,1},{5,6},{6,5},{9,10},{10,9},{13,14},{14,13},{17,18},{18,... | collective-permute-start | bytes 196616 | tf_op jit(solution)/shard_map/ppermute | solution.py:303
  30.8 0.0 copy-done.6
  30.8 0.0 copy-done.7
  30.8 1.1 %inner_steps.1.inner_ref = f32[1024,128]{1,0:T(8,128)S(1)} custom-call(f32[1024,128]{1,0:T(8,128)S(1)} %bitcast.13, f32[512,128]{1,0:T(8,128)S(1)} %collective-permute-done.xa, f32[512,128]{1,0:T(8,128)S(1)} %collective-permute-done.1.xb, f32[512,128]{1,0:T(8,128)S(1)} %collective-permute-done.2.za, f32[512,128]{1,0:T(8,128)S(1)} %collective-permute-done.3.zb, ...), custom_call_target="tpu_custom_call" | custom-call | bytes 6000000 | tf_op jit(solution)/shard_map/inner_steps/pallas_call | solution.py:332
  31.9 0.0 collective-permute-done.4.ya
  31.9 0.2 collective-permute-done.5.yb
  32.1 1.0 %collective-permute-done.6.ea = f32[128,128]{1,0:T(8,128)S(1)} collective-permute-done((f32[128,128]{1,0:T(8,128)S(1)}, f32[128,128]{1,0:T(8,128)S(1)}, u32[]{:S(2)}, u32[]{:S(2)}) %collective-permute-start.6) | collective-permute-done | bytes 65568 | tf_op jit(solution)/shard_map/ppermute | solution.py:303
  33.1 1.9 %collective-permute-done.7.eb = f32[128,128]{1,0:T(8,128)S(1)} collective-permute-done((f32[128,128]{1,0:T(8,128)S(1)}, f32[128,128]{1,0:T(8,128)S(1)}, u32[]{:S(2)}, u32[]{:S(2)}) %collective-permute-start.7) | collective-permute-done | bytes 65568 | tf_op jit(solution)/shard_map/ppermute | solution.py:303
  35.0 0.0 copy-done.2
  35.0 0.0 copy-done.3
  35.0 0.0 copy-done.5
  35.1 2.0 %project.1 = (f32[1024,128]{1,0:T(8,128)S(1)}, f32[2176,128]{1,0:T(8,128)}) custom-call(s32[7]{0:T(128)S(1)} %bitcast.18, f32[2176,128]{1,0:T(8,128)} %blank_lanes.1.blank_any.lanes_any, f32[1024,128]{1,0:T(8,128)S(1)} %inner_steps.1.inner_ref, f32[64,128]{1,0:T(8,128)S(1)} %get-tuple-element.18.low_ref, ...), custom_call_target="tpu_custom_call", output_to_operand_aliasing={{1}: (1, {})} | custom-call | bytes 6000000 | tf_op jit(solution)/shard_map/project/pallas_call | solution.py:333
  37.0 0.0 copy-start.9
  37.1 9.9 %all-to-all-start = ((f32[16,136,128]{2,1,0:T(8,128)}), f32[16,136,128]{2,1,0:T(8,128)S(1)}, u32[]{:S(2)}, u32[]{:S(2)}) async-start(f32[16,136,128]{2,1,0:T(8,128)} %bitcast.8), calls=%async_computation | async-start | bytes 2228224 | tf_op jit(solution)/shard_map/all_to_all | solution.py:353
  47.0 0.0 copy-done.9
  47.0 0.1 copy.11.table_ref
  47.1 1.0 %finish_density.1 = f32[1024,128]{1,0:T(8,128)} custom-call(f32[1024,128]{1,0:T(8,128)S(1)} %get-tuple-element.24.cells_ref), custom_call_target="tpu_custom_call" | custom-call | bytes 6000000 | tf_op jit(solution)/shard_map/finish_density/pallas_call | solution.py:352
  48.1 25.0 %all-to-all-done = f32[16,136,128]{2,1,0:T(8,128)S(1)} async-done(((f32[16,136,128]{2,1,0:T(8,128)}), f32[16,136,128]{2,1,0:T(8,128)S(1)}, u32[]{:S(2)}, u32[]{:S(2)}) %all-to-all-start) | async-done | bytes 1114144 | tf_op jit(solution)/shard_map/all_to_all | solution.py:353
  73.1 1.3 %gather_sky.1 = f32[384,128]{1,0:T(8,128)} custom-call(f32[2176,128]{1,0:T(8,128)S(1)} %bitcast.14, f32[96,64]{1,0:T(8,128)S(1)} %copy.11.table_ref), custom_call_target="tpu_custom_call" | custom-call | bytes 3000000 | tf_op jit(solution)/shard_map/gather_sky/pallas_call | solution.py:354
Async XLA Ops:
  0.6 1.0 %copy-start = (f32[64,4,4,128]{3,2,1,0:T(4,128)S(1)}, f32[64,4,4,128]{3,2,1,0:T(4,128)}, u32[]{:S(2)}) copy-start(f32[64,4,4,128]{3,2,1,0:T(4,128)} %param.8) | copy-start | bytes 1572868
  1.7 12.8 %copy-start.1 = (f32[64,4,4,128]{3,2,1,0:T(4,128)S(1)}, f32[64,4,4,128]{3,2,1,0:T(4,128)}, u32[]{:S(2)}) copy-start(f32[64,4,4,128]{3,2,1,0:T(4,128)} %param.8) | copy-start | bytes 1572868
  1.9 13.2 %collective-permute-start = (f32[512,128]{1,0:T(8,128)S(1)}, f32[512,128]{1,0:T(8,128)S(1)}, u32[]{:S(2)}, u32[]{:S(2)}) collective-permute-start(f32[512,128]{1,0:T(8,128)S(1)} %get-tuple-element.14), channel_id=1, source_target_pairs={{0,64},{64,0},{128,192},{192,128},{256,320},{320,256},{384,448},{4... | collective-permute-start | bytes 786440 | tf_op jit(solution)/shard_map/ppermute | solution.py:303
  3.8 15.8 %collective-permute-start.1 = (f32[512,128]{1,0:T(8,128)S(1)}, f32[512,128]{1,0:T(8,128)S(1)}, u32[]{:S(2)}, u32[]{:S(2)}) collective-permute-start(f32[512,128]{1,0:T(8,128)S(1)} %get-tuple-element.15), channel_id=1, source_target_pairs={{64,128},{128,64},{192,256},{256,192},{320,384},{384,320},{65,129}... | collective-permute-start | bytes 786440 | tf_op jit(solution)/shard_map/ppermute | solution.py:303
  6.3 13.3 %collective-permute-start.2 = (f32[512,128]{1,0:T(8,128)S(1)}, f32[512,128]{1,0:T(8,128)S(1)}, u32[]{:S(2)}, u32[]{:S(2)}) collective-permute-start(f32[512,128]{1,0:T(8,128)S(1)} %get-tuple-element.16), channel_id=1, source_target_pairs={{0,1},{1,0},{2,3},{3,2},{4,5},{5,4},{6,7},{7,6},{8,9},{9,8},{10,11... | collective-permute-start | bytes 786440 | tf_op jit(solution)/shard_map/ppermute | solution.py:303
  9.5 10.5 %collective-permute-start.3 = (f32[512,128]{1,0:T(8,128)S(1)}, f32[512,128]{1,0:T(8,128)S(1)}, u32[]{:S(2)}, u32[]{:S(2)}) collective-permute-start(f32[512,128]{1,0:T(8,128)S(1)} %get-tuple-element.17), channel_id=1, source_target_pairs={{1,2},{2,1},{5,6},{6,5},{9,10},{10,9},{13,14},{14,13},{17,18},{18,... | collective-permute-start | bytes 786440 | tf_op jit(solution)/shard_map/ppermute | solution.py:303
  11.5 0.7 copy-start.4
  12.1 0.7 copy-start.8
  12.8 18.0 %copy-start.6 = (f32[64]{0:T(128)S(1)}, f32[64]{0:T(128)}, u32[]{:S(2)}) copy-start(f32[64]{0:T(128)} %param.10) | copy-start | bytes 772
  12.8 18.0 %copy-start.7 = (f32[64]{0:T(128)S(1)}, f32[64]{0:T(128)}, u32[]{:S(2)}) copy-start(f32[64]{0:T(128)} %param.11) | copy-start | bytes 772
  14.4 20.6 %copy-start.2 = (bf16[1,1,1,7,2048,128]{5,4,3,2,1,0:T(8,128)(2,1)S(1)}, bf16[1,1,1,7,2048,128]{5,4,3,2,1,0:T(8,128)(2,1)}, u32[]{:S(2)}) copy-start(bf16[1,1,1,7,2048,128]{5,4,3,2,1,0:T(8,128)(2,1)} %param.13) | copy-start | bytes 11010052
  20.4 14.6 %copy-start.3 = (f32[4,4,128]{2,1,0:T(4,128)S(1)}, f32[4,4,128]{2,1,0:T(4,128)}, u32[]{:S(2)}) copy-start(f32[4,4,128]{2,1,0:T(4,128)} %param.9) | copy-start | bytes 24580
  20.4 14.6 %copy-start.5 = (s32[1,1,1,7,1]{3,4,2,1,0:T(1,128)S(1)}, s32[1,1,1,7,1]{3,4,2,1,0:T(1,128)}, u32[]{:S(2)}) copy-start(s32[1,1,1,7,1]{3,4,2,1,0:T(1,128)} %param.14) | copy-start | bytes 88
  20.5 11.5 %collective-permute-start.4 = (f32[128,128]{1,0:T(8,128)S(1)}, f32[128,128]{1,0:T(8,128)S(1)}, u32[]{:S(2)}, u32[]{:S(2)}) collective-permute-start(f32[128,128]{1,0:T(8,128)S(1)} %get-tuple-element.20), channel_id=1, source_target_pairs={{0,4},{4,0},{8,12},{12,8},{16,20},{20,16},{24,28},{28,24},{32,36},... | collective-permute-start | bytes 196616 | tf_op jit(solution)/shard_map/ppermute | solution.py:303
  23.9 8.3 %collective-permute-start.5 = (f32[128,128]{1,0:T(8,128)S(1)}, f32[128,128]{1,0:T(8,128)S(1)}, u32[]{:S(2)}, u32[]{:S(2)}) collective-permute-start(f32[128,128]{1,0:T(8,128)S(1)} %get-tuple-element.21), channel_id=1, source_target_pairs={{4,8},{8,4},{12,16},{16,12},{20,24},{24,20},{28,32},{32,28},{36,40... | collective-permute-start | bytes 196616 | tf_op jit(solution)/shard_map/ppermute | solution.py:303
  27.0 6.2 %collective-permute-start.6 = (f32[128,128]{1,0:T(8,128)S(1)}, f32[128,128]{1,0:T(8,128)S(1)}, u32[]{:S(2)}, u32[]{:S(2)}) collective-permute-start(f32[128,128]{1,0:T(8,128)S(1)} %get-tuple-element.22), channel_id=1, source_target_pairs={{0,1},{1,0},{2,3},{3,2},{4,5},{5,4},{6,7},{7,6},{8,9},{9,8},{10,11... | collective-permute-start | bytes 196616 | tf_op jit(solution)/shard_map/ppermute | solution.py:303
  28.9 6.2 %collective-permute-start.7 = (f32[128,128]{1,0:T(8,128)S(1)}, f32[128,128]{1,0:T(8,128)S(1)}, u32[]{:S(2)}, u32[]{:S(2)}) collective-permute-start(f32[128,128]{1,0:T(8,128)S(1)} %get-tuple-element.23), channel_id=1, source_target_pairs={{1,2},{2,1},{5,6},{6,5},{9,10},{10,9},{13,14},{14,13},{17,18},{18,... | collective-permute-start | bytes 196616 | tf_op jit(solution)/shard_map/ppermute | solution.py:303
  37.0 9.9 %copy-start.9 = (f32[96,64]{0,1:T(8,128)S(1)}, f32[96,64]{0,1:T(8,128)}, u32[]{:S(2)}) copy-start(f32[96,64]{0,1:T(8,128)} %param.12) | copy-start | bytes 73732
  37.1 36.0 %all-to-all-start = ((f32[16,136,128]{2,1,0:T(8,128)}), f32[16,136,128]{2,1,0:T(8,128)S(1)}, u32[]{:S(2)}, u32[]{:S(2)}) async-start(f32[16,136,128]{2,1,0:T(8,128)} %bitcast.8), calls=%async_computation | async-start | bytes 2228224 | tf_op jit(solution)/shard_map/all_to_all | solution.py:353

commit v5 on v4

--- a/solution.py
+++ b/solution.py
@@ -15,7 +15,7 @@
 BO = 4
 CAP = 2
 ZX = CZ * CX
-LANE = CAP * NE + 8
+LANE = CAP * NE + 1
 VMEM = pl.BlockSpec(memory_space=pltpu.VMEM)
 ANY = pl.BlockSpec(memory_space=pl.ANY)
 SMALL = 16 * 1024 * 1024
@@ -83,9 +83,11 @@
     send_ref[...] = jnp.zeros_like(send_ref)
     for fetch in fetches:
         fetch.wait()
+    half = lax.broadcasted_iota(jnp.int32, (1, PB), 1) // (PB // CAP)
     for s in range(KS):
-        row = owner_ref[s] * LANE + CAP * NE + place_of(owner_ref, s) * BO + block_ref[s]
-        send_ref[pl.ds(row, 1), :] = jnp.ones((1, PB), jnp.float32)
+        row = pl.ds(owner_ref[s] * LANE + CAP * NE, 1)
+        feeds = jnp.broadcast_to(block_ref[s], (1, PB)).astype(jnp.float32)
+        send_ref[row, :] = jnp.where(half == place_of(owner_ref, s), feeds, send_ref[row, :])
 
 
 def own_columns(cr_ref, blank_any, low_ref, high_ref):
@@ -243,11 +245,11 @@
     product = jnp.dot(parts_ref[...], weights, preferred_element_type=jnp.float32)
     product = product[:NE] + product[NE:]
     for s in range(KS):
-        blocks_ref[s * NE:(s + 1) * NE, :] = product[:, s * PB:(s + 1) * PB]
+        blocks_ref[s * NE:(s + 1) * NE, 0, :] = product[:, s * PB:(s + 1) * PB]
     fetch.wait()
     copies = []
     for s in range(KS):
-        row = pl.multiple_of(owner_ref[s] * LANE + place_of(owner_ref, s) * NE, 8)
+        row = owner_ref[s] * LANE + place_of(owner_ref, s) * NE
         copies.append(pltpu.make_async_copy(blocks_ref.at[pl.ds(s * NE, NE)], send_any.at[pl.ds(row, NE)], sem.at[s]))
         copies[s].start()
     for copy in copies:
@@ -262,12 +264,16 @@
 def gather_sky(recv_ref, table_ref, sky_ref):
     count = recv_ref.shape[0] // LANE
     total = [jnp.zeros((NE, PB), jnp.float32) for _ in range(BO)]
-    for j in range(count):
-        for k in range(CAP):
-            block = recv_ref[j * LANE + k * NE:j * LANE + (k + 1) * NE, :]
-            for b in range(BO):
-                row = j * LANE + CAP * NE + k * BO + b
-                total[b] = total[b] + block * recv_ref[row:row + 1, :]
+    feeds = recv_ref[pl.ds(CAP * NE, count, stride=LANE), :]
+    first = lax.broadcasted_iota(jnp.int32, (count, PB), 1) < PB // 2
+    turned = pltpu.roll(feeds, PB // 2, 1)
+    feeds = [jnp.where(first, feeds, turned), jnp.where(first, turned, feeds)]
+    for b in range(BO):
+        chosen = [jnp.where(rows == b, 1.0, 0.0) for rows in feeds]
+        for j in range(count):
+            for k in range(CAP):
+                block = recv_ref[j * LANE + k * NE:j * LANE + (k + 1) * NE, :]
+                total[b] = total[b] + block * chosen[k][j:j + 1, :]
     for b in range(BO):
         sky_ref[b * NG:(b + 1) * NG, :] = jnp.dot(
             table_ref[...], total[b], precision=lax.Precision.HIGHEST, preferred_element_type=jnp.float32
@@ -333,24 +339,24 @@
     cells, send = call(
         project,
         "project",
-        [f32(ZX * NE, CY), f32(owners * LANE, PB)],
+        [f32(ZX * NE, CY), f32(owners * LANE, 1, PB)],
         [ANY] * 2 + [VMEM] * 11,
         2,
         out_specs=[VMEM, ANY],
         scratch=[
             pltpu.VMEM((2 * NE, ZX * CY), jnp.bfloat16),
-            pltpu.VMEM((KS * NE, PB), jnp.float32),
+            pltpu.VMEM((KS * NE, 1, PB), jnp.float32),
             pltpu.SMEM((KS,), jnp.int32),
             pltpu.SemaphoreType.DMA((KS,)),
             pltpu.SemaphoreType.DMA,
         ],
         aliases={1: 1},
     )(
-        owner, blank, inner, low, high, ya, yb, ea, eb, diff, loss,
+        owner, blank.reshape(owners * LANE, 1, PB), inner, low, high, ya, yb, ea, eb, diff, loss,
         gas.reshape(ZX, CY), los_weight.reshape(KS, ZX * CY, PB),
     )
     (final,) = call(finish_density, "finish_density", [f32(NE * ZX, CY)], [VMEM], 2)(cells)
-    recv = lax.all_to_all(send.reshape(owners, LANE, PB), "gy", 0, 0, tiled=True)
+    recv = lax.all_to_all(send.reshape(owners, 1, LANE * PB), "gy", 0, 0, tiled=True)
     (sky,) = call(gather_sky, "gather_sky", [f32(BO * NG, PB)], [VMEM] * 2, 1)(
         recv.reshape(owners * LANE, PB), pi0_table
     )

time: 74.9 us -> 73.8 us (0.985)
  waiting for transfers between devices: 33.1 us -> 31.8 us
    all_to_all x1, waiting for transfers between devices: 25 us -> 23.7 us  [body(): lax.all_to_all(send.reshape(owners, 1, LANE * PB), 'gy', 0, 0, tiled=True)]
where the time goes in v5:
time: 73.8 us; the launch traced here: 73.2 us
  waiting for transfers between devices  31.8 us (43%)
  starting transfers between devices  29.9 us (41%)
  Pallas kernels  8.24 us (11%)
  local copies, waits for them, and re-layouts  2.46 us (3%)
  between operations  0.84 us (1%)
    all_to_all x1, waiting for transfers between devices, body(): lax.all_to_all(send.reshape(owners, 1, LANE * PB), 'gy', 0, 0, tiled=True)  23.7 us
    ppermute x8, starting transfers between devices, swap(): return lax.ppermute(values, axis, pairs)  19.9 us
    all_to_all x1, starting transfers between devices, body(): lax.all_to_all(send.reshape(owners, 1, LANE * PB), 'gy', 0, 0, tiled=True)  9.95 us
    ppermute x8, waiting for transfers between devices, swap(): return lax.ppermute(values, axis, pairs)  8.18 us
    unnamed x21, local copies, waits for them, and re-layouts  2.46 us
    pallas_call x1, Pallas kernels, body(): call(project, 'project', [f32(ZX * NE, CY), f32(owners * LANE, 1, PB)], [...  2.06 us
    pallas_call x1, Pallas kernels, body(): call(blank_lanes, 'blank_lanes', [f32(owners * LANE, PB)], [ANY] * 2, 1,...  1.59 us
  transfers between devices with their start and end apart: 9, of which 6 were waited for; matrix products, arithmetic and copies ran while one was open for 0% of the time, Pallas kernels for 6%

profile of v5, /device:TPU:336, one launch (start us, length us, event | category | flops | bytes accessed | tf_op | source)
XLA Modules:
  0.0 73.2 jit_solution(15913166550754801122)
XLA Ops:
  0.6 0.0 copy-start
  0.6 1.0 %copy-done = f32[64,4,4,128]{3,2,1,0:T(4,128)S(1)} copy-done((f32[64,4,4,128]{3,2,1,0:T(4,128)S(1)}, f32[64,4,4,128]{3,2,1,0:T(4,128)}, u32[]{:S(2)}) %copy-start) | copy-done | bytes 524312
  1.7 0.0 copy-start.1
  1.7 0.2 first_faces.1
  1.9 1.9 %collective-permute-start = (f32[512,128]{1,0:T(8,128)S(1)}, f32[512,128]{1,0:T(8,128)S(1)}, u32[]{:S(2)}, u32[]{:S(2)}) collective-permute-start(f32[512,128]{1,0:T(8,128)S(1)} %get-tuple-element.14), channel_id=1, source_target_pairs={{0,64},{64,0},{128,192},{192,128},{256,320},{320,256},{384,448},{4... | collective-permute-start | bytes 786440 | tf_op jit(solution)/shard_map/ppermute | solution.py:309
  3.8 2.6 %collective-permute-start.1 = (f32[512,128]{1,0:T(8,128)S(1)}, f32[512,128]{1,0:T(8,128)S(1)}, u32[]{:S(2)}, u32[]{:S(2)}) collective-permute-start(f32[512,128]{1,0:T(8,128)S(1)} %get-tuple-element.15), channel_id=1, source_target_pairs={{64,128},{128,64},{192,256},{256,192},{320,384},{384,320},{65,129}... | collective-permute-start | bytes 786440 | tf_op jit(solution)/shard_map/ppermute | solution.py:309
  6.3 3.2 %collective-permute-start.2 = (f32[512,128]{1,0:T(8,128)S(1)}, f32[512,128]{1,0:T(8,128)S(1)}, u32[]{:S(2)}, u32[]{:S(2)}) collective-permute-start(f32[512,128]{1,0:T(8,128)S(1)} %get-tuple-element.16), channel_id=1, source_target_pairs={{0,1},{1,0},{2,3},{3,2},{4,5},{5,4},{6,7},{7,6},{8,9},{9,8},{10,11... | collective-permute-start | bytes 786440 | tf_op jit(solution)/shard_map/ppermute | solution.py:309
  9.5 1.9 %collective-permute-start.3 = (f32[512,128]{1,0:T(8,128)S(1)}, f32[512,128]{1,0:T(8,128)S(1)}, u32[]{:S(2)}, u32[]{:S(2)}) collective-permute-start(f32[512,128]{1,0:T(8,128)S(1)} %get-tuple-element.17), channel_id=1, source_target_pairs={{1,2},{2,1},{5,6},{6,5},{9,10},{10,9},{13,14},{14,13},{17,18},{18,... | collective-permute-start | bytes 786440 | tf_op jit(solution)/shard_map/ppermute | solution.py:309
  11.5 0.0 copy-start.4
  11.5 0.6 copy-done.4
  12.1 0.0 copy-start.8
  12.1 0.7 copy-done.8
  12.8 0.0 copy-start.6
  12.8 0.0 copy-start.7
  12.8 1.6 %blank_lanes.1.blank_any = f32[2064,128]{1,0:T(8,128)} custom-call(s32[7]{0:T(128)S(1)} %bitcast.18, s32[7]{0:T(128)S(1)} %bitcast.24), custom_call_target="tpu_custom_call" | custom-call | bytes 3000000 | tf_op jit(solution)/shard_map/blank_lanes/pallas_call | solution.py:322
  14.4 0.0 copy-done.1
  14.4 0.0 copy-start.2
  14.4 0.6 own_columns.1
  15.0 0.0 collective-permute-done.xa
  15.0 4.6 %collective-permute-done.1.xb = f32[512,128]{1,0:T(8,128)S(1)} collective-permute-done((f32[512,128]{1,0:T(8,128)S(1)}, f32[512,128]{1,0:T(8,128)S(1)}, u32[]{:S(2)}, u32[]{:S(2)}) %collective-permute-start.1) | collective-permute-done | bytes 262176 | tf_op jit(solution)/shard_map/ppermute | solution.py:309
  19.6 0.0 collective-permute-done.2.za
  19.6 0.5 collective-permute-done.3.zb
  20.1 0.3 edge_faces.1
  20.4 0.0 copy-start.3
  20.4 0.0 copy-start.5
  20.5 3.4 %collective-permute-start.4 = (f32[128,128]{1,0:T(8,128)S(1)}, f32[128,128]{1,0:T(8,128)S(1)}, u32[]{:S(2)}, u32[]{:S(2)}) collective-permute-start(f32[128,128]{1,0:T(8,128)S(1)} %get-tuple-element.20), channel_id=1, source_target_pairs={{0,4},{4,0},{8,12},{12,8},{16,20},{20,16},{24,28},{28,24},{32,36},... | collective-permute-start | bytes 196616 | tf_op jit(solution)/shard_map/ppermute | solution.py:309
  23.9 3.1 %collective-permute-start.5 = (f32[128,128]{1,0:T(8,128)S(1)}, f32[128,128]{1,0:T(8,128)S(1)}, u32[]{:S(2)}, u32[]{:S(2)}) collective-permute-start(f32[128,128]{1,0:T(8,128)S(1)} %get-tuple-element.21), channel_id=1, source_target_pairs={{4,8},{8,4},{12,16},{16,12},{20,24},{24,20},{28,32},{32,28},{36,40... | collective-permute-start | bytes 196616 | tf_op jit(solution)/shard_map/ppermute | solution.py:309
  27.0 1.9 %collective-permute-start.6 = (f32[128,128]{1,0:T(8,128)S(1)}, f32[128,128]{1,0:T(8,128)S(1)}, u32[]{:S(2)}, u32[]{:S(2)}) collective-permute-start(f32[128,128]{1,0:T(8,128)S(1)} %get-tuple-element.22), channel_id=1, source_target_pairs={{0,1},{1,0},{2,3},{3,2},{4,5},{5,4},{6,7},{7,6},{8,9},{9,8},{10,11... | collective-permute-start | bytes 196616 | tf_op jit(solution)/shard_map/ppermute | solution.py:309
  28.9 1.9 %collective-permute-start.7 = (f32[128,128]{1,0:T(8,128)S(1)}, f32[128,128]{1,0:T(8,128)S(1)}, u32[]{:S(2)}, u32[]{:S(2)}) collective-permute-start(f32[128,128]{1,0:T(8,128)S(1)} %get-tuple-element.23), channel_id=1, source_target_pairs={{1,2},{2,1},{5,6},{6,5},{9,10},{10,9},{13,14},{14,13},{17,18},{18,... | collective-permute-start | bytes 196616 | tf_op jit(solution)/shard_map/ppermute | solution.py:309
  30.8 0.0 copy-done.6
  30.8 0.0 copy-done.7
  30.8 1.1 %inner_steps.1.inner_ref = f32[1024,128]{1,0:T(8,128)S(1)} custom-call(f32[1024,128]{1,0:T(8,128)S(1)} %bitcast.14, f32[512,128]{1,0:T(8,128)S(1)} %collective-permute-done.xa, f32[512,128]{1,0:T(8,128)S(1)} %collective-permute-done.1.xb, f32[512,128]{1,0:T(8,128)S(1)} %collective-permute-done.2.za, f32[512,128]{1,0:T(8,128)S(1)} %collective-permute-done.3.zb, ...), custom_call_target="tpu_custom_call" | custom-call | bytes 6000000 | tf_op jit(solution)/shard_map/inner_steps/pallas_call | solution.py:338
  31.9 0.0 collective-permute-done.4.ya
  32.0 0.2 collective-permute-done.5.yb
  32.1 1.0 %collective-permute-done.6.ea = f32[128,128]{1,0:T(8,128)S(1)} collective-permute-done((f32[128,128]{1,0:T(8,128)S(1)}, f32[128,128]{1,0:T(8,128)S(1)}, u32[]{:S(2)}, u32[]{:S(2)}) %collective-permute-start.6) | collective-permute-done | bytes 65568 | tf_op jit(solution)/shard_map/ppermute | solution.py:309
  33.1 1.9 %collective-permute-done.7.eb = f32[128,128]{1,0:T(8,128)S(1)} collective-permute-done((f32[128,128]{1,0:T(8,128)S(1)}, f32[128,128]{1,0:T(8,128)S(1)}, u32[]{:S(2)}, u32[]{:S(2)}) %collective-permute-start.7) | collective-permute-done | bytes 65568 | tf_op jit(solution)/shard_map/ppermute | solution.py:309
  35.0 0.0 copy-done.2
  35.0 0.0 copy-done.3
  35.0 0.0 copy-done.5
  35.1 2.1 %project.1 = (f32[1024,128]{1,0:T(8,128)S(1)}, f32[2064,1,128]{2,1,0:T(1,128)}) custom-call(s32[7]{0:T(128)S(1)} %bitcast.19, f32[2064,1,128]{2,1,0:T(1,128)} %bitcast.2.lanes_any, f32[1024,128]{1,0:T(8,128)S(1)} %inner_steps.1.inner_ref, f32[64,128]{1,0:T(8,128)S(1)} %get-tuple-element.18.low_ref, ...), custom_call_target="tpu_custom_call", output_to_operand_aliasing={{1}: (1, {})} | custom-call | bytes 6000000 | tf_op jit(solution)/shard_map/project/pallas_call | solution.py:339
  37.1 0.0 copy-start.9
  37.1 9.9 %all-to-all-start = ((f32[16,1,16512]{2,1,0:T(1,128)}), f32[16,1,16512]{2,1,0:T(1,128)S(1)}, u32[]{:S(2)}, u32[]{:S(2)}) async-start(f32[16,1,16512]{2,1,0:T(1,128)} %bitcast.9), calls=%async_computation | async-start | bytes 2113536 | tf_op jit(solution)/shard_map/all_to_all | solution.py:359
  47.1 0.0 copy-done.9
  47.1 0.1 copy.13.table_ref
  47.2 1.0 %finish_density.1 = f32[1024,128]{1,0:T(8,128)} custom-call(f32[1024,128]{1,0:T(8,128)S(1)} %get-tuple-element.24.cells_ref), custom_call_target="tpu_custom_call" | custom-call | bytes 6000000 | tf_op jit(solution)/shard_map/finish_density/pallas_call | solution.py:358
  48.2 23.7 %all-to-all-done = f32[16,1,16512]{2,1,0:T(1,128)S(1)} async-done(((f32[16,1,16512]{2,1,0:T(1,128)}), f32[16,1,16512]{2,1,0:T(1,128)S(1)}, u32[]{:S(2)}, u32[]{:S(2)}) %all-to-all-start) | async-done | bytes 1056800 | tf_op jit(solution)/shard_map/all_to_all | solution.py:359
  71.9 1.3 %gather_sky.1 = f32[384,128]{1,0:T(8,128)} custom-call(f32[2064,128]{1,0:T(8,128)S(1)} %bitcast.15, f32[96,64]{1,0:T(8,128)S(1)} %copy.13.table_ref), custom_call_target="tpu_custom_call" | custom-call | bytes 3000000 | tf_op jit(solution)/shard_map/gather_sky/pallas_call | solution.py:360
Async XLA Ops:
  0.6 1.0 %copy-start = (f32[64,4,4,128]{3,2,1,0:T(4,128)S(1)}, f32[64,4,4,128]{3,2,1,0:T(4,128)}, u32[]{:S(2)}) copy-start(f32[64,4,4,128]{3,2,1,0:T(4,128)} %param.8) | copy-start | bytes 1572868
  1.7 12.7 %copy-start.1 = (f32[64,4,4,128]{3,2,1,0:T(4,128)S(1)}, f32[64,4,4,128]{3,2,1,0:T(4,128)}, u32[]{:S(2)}) copy-start(f32[64,4,4,128]{3,2,1,0:T(4,128)} %param.8) | copy-start | bytes 1572868
  1.9 13.1 %collective-permute-start = (f32[512,128]{1,0:T(8,128)S(1)}, f32[512,128]{1,0:T(8,128)S(1)}, u32[]{:S(2)}, u32[]{:S(2)}) collective-permute-start(f32[512,128]{1,0:T(8,128)S(1)} %get-tuple-element.14), channel_id=1, source_target_pairs={{0,64},{64,0},{128,192},{192,128},{256,320},{320,256},{384,448},{4... | collective-permute-start | bytes 786440 | tf_op jit(solution)/shard_map/ppermute | solution.py:309
  3.8 15.8 %collective-permute-start.1 = (f32[512,128]{1,0:T(8,128)S(1)}, f32[512,128]{1,0:T(8,128)S(1)}, u32[]{:S(2)}, u32[]{:S(2)}) collective-permute-start(f32[512,128]{1,0:T(8,128)S(1)} %get-tuple-element.15), channel_id=1, source_target_pairs={{64,128},{128,64},{192,256},{256,192},{320,384},{384,320},{65,129}... | collective-permute-start | bytes 786440 | tf_op jit(solution)/shard_map/ppermute | solution.py:309
  6.3 13.3 %collective-permute-start.2 = (f32[512,128]{1,0:T(8,128)S(1)}, f32[512,128]{1,0:T(8,128)S(1)}, u32[]{:S(2)}, u32[]{:S(2)}) collective-permute-start(f32[512,128]{1,0:T(8,128)S(1)} %get-tuple-element.16), channel_id=1, source_target_pairs={{0,1},{1,0},{2,3},{3,2},{4,5},{5,4},{6,7},{7,6},{8,9},{9,8},{10,11... | collective-permute-start | bytes 786440 | tf_op jit(solution)/shard_map/ppermute | solution.py:309
  9.5 10.5 %collective-permute-start.3 = (f32[512,128]{1,0:T(8,128)S(1)}, f32[512,128]{1,0:T(8,128)S(1)}, u32[]{:S(2)}, u32[]{:S(2)}) collective-permute-start(f32[512,128]{1,0:T(8,128)S(1)} %get-tuple-element.17), channel_id=1, source_target_pairs={{1,2},{2,1},{5,6},{6,5},{9,10},{10,9},{13,14},{14,13},{17,18},{18,... | collective-permute-start | bytes 786440 | tf_op jit(solution)/shard_map/ppermute | solution.py:309
  11.5 0.7 copy-start.4
  12.1 0.7 copy-start.8
  12.8 18.0 %copy-start.6 = (f32[64]{0:T(128)S(1)}, f32[64]{0:T(128)}, u32[]{:S(2)}) copy-start(f32[64]{0:T(128)} %param.10) | copy-start | bytes 772
  12.8 18.0 %copy-start.7 = (f32[64]{0:T(128)S(1)}, f32[64]{0:T(128)}, u32[]{:S(2)}) copy-start(f32[64]{0:T(128)} %param.11) | copy-start | bytes 772
  14.4 20.6 %copy-start.2 = (bf16[1,1,1,7,2048,128]{5,4,3,2,1,0:T(8,128)(2,1)S(1)}, bf16[1,1,1,7,2048,128]{5,4,3,2,1,0:T(8,128)(2,1)}, u32[]{:S(2)}) copy-start(bf16[1,1,1,7,2048,128]{5,4,3,2,1,0:T(8,128)(2,1)} %param.13) | copy-start | bytes 11010052
  20.4 14.6 %copy-start.3 = (f32[4,4,128]{2,1,0:T(4,128)S(1)}, f32[4,4,128]{2,1,0:T(4,128)}, u32[]{:S(2)}) copy-start(f32[4,4,128]{2,1,0:T(4,128)} %param.9) | copy-start | bytes 24580
  20.4 14.6 %copy-start.5 = (s32[1,1,1,7,1]{3,4,2,1,0:T(1,128)S(1)}, s32[1,1,1,7,1]{3,4,2,1,0:T(1,128)}, u32[]{:S(2)}) copy-start(s32[1,1,1,7,1]{3,4,2,1,0:T(1,128)} %param.14) | copy-start | bytes 88
  20.5 11.5 %collective-permute-start.4 = (f32[128,128]{1,0:T(8,128)S(1)}, f32[128,128]{1,0:T(8,128)S(1)}, u32[]{:S(2)}, u32[]{:S(2)}) collective-permute-start(f32[128,128]{1,0:T(8,128)S(1)} %get-tuple-element.20), channel_id=1, source_target_pairs={{0,4},{4,0},{8,12},{12,8},{16,20},{20,16},{24,28},{28,24},{32,36},... | collective-permute-start | bytes 196616 | tf_op jit(solution)/shard_map/ppermute | solution.py:309
  23.9 8.3 %collective-permute-start.5 = (f32[128,128]{1,0:T(8,128)S(1)}, f32[128,128]{1,0:T(8,128)S(1)}, u32[]{:S(2)}, u32[]{:S(2)}) collective-permute-start(f32[128,128]{1,0:T(8,128)S(1)} %get-tuple-element.21), channel_id=1, source_target_pairs={{4,8},{8,4},{12,16},{16,12},{20,24},{24,20},{28,32},{32,28},{36,40... | collective-permute-start | bytes 196616 | tf_op jit(solution)/shard_map/ppermute | solution.py:309
  27.0 6.2 %collective-permute-start.6 = (f32[128,128]{1,0:T(8,128)S(1)}, f32[128,128]{1,0:T(8,128)S(1)}, u32[]{:S(2)}, u32[]{:S(2)}) collective-permute-start(f32[128,128]{1,0:T(8,128)S(1)} %get-tuple-element.22), channel_id=1, source_target_pairs={{0,1},{1,0},{2,3},{3,2},{4,5},{5,4},{6,7},{7,6},{8,9},{9,8},{10,11... | collective-permute-start | bytes 196616 | tf_op jit(solution)/shard_map/ppermute | solution.py:309
  28.9 6.2 %collective-permute-start.7 = (f32[128,128]{1,0:T(8,128)S(1)}, f32[128,128]{1,0:T(8,128)S(1)}, u32[]{:S(2)}, u32[]{:S(2)}) collective-permute-start(f32[128,128]{1,0:T(8,128)S(1)} %get-tuple-element.23), channel_id=1, source_target_pairs={{1,2},{2,1},{5,6},{6,5},{9,10},{10,9},{13,14},{14,13},{17,18},{18,... | collective-permute-start | bytes 196616 | tf_op jit(solution)/shard_map/ppermute | solution.py:309
  37.1 10.0 %copy-start.9 = (f32[96,64]{0,1:T(8,128)S(1)}, f32[96,64]{0,1:T(8,128)}, u32[]{:S(2)}) copy-start(f32[96,64]{0,1:T(8,128)} %param.12) | copy-start | bytes 73732
  37.1 34.8 %all-to-all-start = ((f32[16,1,16512]{2,1,0:T(1,128)}), f32[16,1,16512]{2,1,0:T(1,128)S(1)}, u32[]{:S(2)}, u32[]{:S(2)}) async-start(f32[16,1,16512]{2,1,0:T(1,128)} %bitcast.9), calls=%async_computation | async-start | bytes 2113536 | tf_op jit(solution)/shard_map/all_to_all | solution.py:359

commit v6 on v5

--- a/solution.py
+++ b/solution.py
@@ -139,11 +139,11 @@
 
 def stepper(diff, loss):
     top = lax.broadcasted_iota(jnp.int32, (NE, CY), 0) == NE - 1
+    keep = 1.0 - 6.0 * diff - loss
+    loss_above = jnp.where(top, 0.0, pltpu.roll(loss, NE - 1, 0))
 
     def update(c, beside):
-        flux = loss * c
-        above = jnp.where(top, 0.0, pltpu.roll(flux, NE - 1, 0))
-        return c + diff * (beside - 6.0 * c) + above - flux
+        return keep * c + diff * beside + loss_above * pltpu.roll(c, NE - 1, 0)
 
     return update
 

time: 73.8 us -> 73.8 us (level)
  no operation moved by 1% of the time
where the time goes in v6:
time: 73.8 us; the launch traced here: 73.2 us
  waiting for transfers between devices  31.9 us (43%)
  starting transfers between devices  29.9 us (41%)
  Pallas kernels  8.19 us (11%)
  local copies, waits for them, and re-layouts  2.46 us (3%)
  between operations  0.83 us (1%)
    all_to_all x1, waiting for transfers between devices, body(): lax.all_to_all(send.reshape(owners, 1, LANE * PB), 'gy', 0, 0, tiled=True)  23.7 us
    ppermute x8, starting transfers between devices, swap(): return lax.ppermute(values, axis, pairs)  19.9 us
    all_to_all x1, starting transfers between devices, body(): lax.all_to_all(send.reshape(owners, 1, LANE * PB), 'gy', 0, 0, tiled=True)  9.94 us
    ppermute x8, waiting for transfers between devices, swap(): return lax.ppermute(values, axis, pairs)  8.23 us
    unnamed x21, local copies, waits for them, and re-layouts  2.46 us
    pallas_call x1, Pallas kernels, body(): call(project, 'project', [f32(ZX * NE, CY), f32(owners * LANE, 1, PB)], [...  2.06 us
    pallas_call x1, Pallas kernels, body(): call(blank_lanes, 'blank_lanes', [f32(owners * LANE, PB)], [ANY] * 2, 1,...  1.59 us
  transfers between devices with their start and end apart: 9, of which 6 were waited for; matrix products, arithmetic and copies ran while one was open for 0% of the time, Pallas kernels for 6%

profile of v6, /device:TPU:336, one launch (start us, length us, event | category | flops | bytes accessed | tf_op | source)
XLA Modules:
  0.0 73.2 jit_solution(11351516745011672095)
XLA Ops:
  0.6 0.0 copy-start
  0.6 1.0 %copy-done = f32[64,4,4,128]{3,2,1,0:T(4,128)S(1)} copy-done((f32[64,4,4,128]{3,2,1,0:T(4,128)S(1)}, f32[64,4,4,128]{3,2,1,0:T(4,128)}, u32[]{:S(2)}) %copy-start) | copy-done | bytes 524312
  1.7 0.0 copy-start.1
  1.7 0.2 first_faces.1
  1.9 1.9 %collective-permute-start = (f32[512,128]{1,0:T(8,128)S(1)}, f32[512,128]{1,0:T(8,128)S(1)}, u32[]{:S(2)}, u32[]{:S(2)}) collective-permute-start(f32[512,128]{1,0:T(8,128)S(1)} %get-tuple-element.14), channel_id=1, source_target_pairs={{0,64},{64,0},{128,192},{192,128},{256,320},{320,256},{384,448},{4... | collective-permute-start | bytes 786440 | tf_op jit(solution)/shard_map/ppermute | solution.py:309
  3.8 2.6 %collective-permute-start.1 = (f32[512,128]{1,0:T(8,128)S(1)}, f32[512,128]{1,0:T(8,128)S(1)}, u32[]{:S(2)}, u32[]{:S(2)}) collective-permute-start(f32[512,128]{1,0:T(8,128)S(1)} %get-tuple-element.15), channel_id=1, source_target_pairs={{64,128},{128,64},{192,256},{256,192},{320,384},{384,320},{65,129}... | collective-permute-start | bytes 786440 | tf_op jit(solution)/shard_map/ppermute | solution.py:309
  6.3 3.2 %collective-permute-start.2 = (f32[512,128]{1,0:T(8,128)S(1)}, f32[512,128]{1,0:T(8,128)S(1)}, u32[]{:S(2)}, u32[]{:S(2)}) collective-permute-start(f32[512,128]{1,0:T(8,128)S(1)} %get-tuple-element.16), channel_id=1, source_target_pairs={{0,1},{1,0},{2,3},{3,2},{4,5},{5,4},{6,7},{7,6},{8,9},{9,8},{10,11... | collective-permute-start | bytes 786440 | tf_op jit(solution)/shard_map/ppermute | solution.py:309
  9.5 1.9 %collective-permute-start.3 = (f32[512,128]{1,0:T(8,128)S(1)}, f32[512,128]{1,0:T(8,128)S(1)}, u32[]{:S(2)}, u32[]{:S(2)}) collective-permute-start(f32[512,128]{1,0:T(8,128)S(1)} %get-tuple-element.17), channel_id=1, source_target_pairs={{1,2},{2,1},{5,6},{6,5},{9,10},{10,9},{13,14},{14,13},{17,18},{18,... | collective-permute-start | bytes 786440 | tf_op jit(solution)/shard_map/ppermute | solution.py:309
  11.5 0.0 copy-start.4
  11.5 0.6 copy-done.4
  12.1 0.0 copy-start.8
  12.1 0.7 copy-done.8
  12.8 0.0 copy-start.6
  12.8 0.0 copy-start.7
  12.8 1.6 %blank_lanes.1.blank_any = f32[2064,128]{1,0:T(8,128)} custom-call(s32[7]{0:T(128)S(1)} %bitcast.18, s32[7]{0:T(128)S(1)} %bitcast.24), custom_call_target="tpu_custom_call" | custom-call | bytes 3000000 | tf_op jit(solution)/shard_map/blank_lanes/pallas_call | solution.py:322
  14.4 0.0 copy-done.1
  14.4 0.0 copy-start.2
  14.4 0.6 own_columns.1
  15.0 0.0 collective-permute-done.xa
  15.0 4.6 %collective-permute-done.1.xb = f32[512,128]{1,0:T(8,128)S(1)} collective-permute-done((f32[512,128]{1,0:T(8,128)S(1)}, f32[512,128]{1,0:T(8,128)S(1)}, u32[]{:S(2)}, u32[]{:S(2)}) %collective-permute-start.1) | collective-permute-done | bytes 262176 | tf_op jit(solution)/shard_map/ppermute | solution.py:309
  19.6 0.0 collective-permute-done.2.za
  19.6 0.5 collective-permute-done.3.zb
  20.1 0.3 edge_faces.1
  20.4 0.0 copy-start.3
  20.4 0.0 copy-start.5
  20.5 3.4 %collective-permute-start.4 = (f32[128,128]{1,0:T(8,128)S(1)}, f32[128,128]{1,0:T(8,128)S(1)}, u32[]{:S(2)}, u32[]{:S(2)}) collective-permute-start(f32[128,128]{1,0:T(8,128)S(1)} %get-tuple-element.20), channel_id=1, source_target_pairs={{0,4},{4,0},{8,12},{12,8},{16,20},{20,16},{24,28},{28,24},{32,36},... | collective-permute-start | bytes 196616 | tf_op jit(solution)/shard_map/ppermute | solution.py:309
  23.9 3.1 %collective-permute-start.5 = (f32[128,128]{1,0:T(8,128)S(1)}, f32[128,128]{1,0:T(8,128)S(1)}, u32[]{:S(2)}, u32[]{:S(2)}) collective-permute-start(f32[128,128]{1,0:T(8,128)S(1)} %get-tuple-element.21), channel_id=1, source_target_pairs={{4,8},{8,4},{12,16},{16,12},{20,24},{24,20},{28,32},{32,28},{36,40... | collective-permute-start | bytes 196616 | tf_op jit(solution)/shard_map/ppermute | solution.py:309
  27.0 1.9 %collective-permute-start.6 = (f32[128,128]{1,0:T(8,128)S(1)}, f32[128,128]{1,0:T(8,128)S(1)}, u32[]{:S(2)}, u32[]{:S(2)}) collective-permute-start(f32[128,128]{1,0:T(8,128)S(1)} %get-tuple-element.22), channel_id=1, source_target_pairs={{0,1},{1,0},{2,3},{3,2},{4,5},{5,4},{6,7},{7,6},{8,9},{9,8},{10,11... | collective-permute-start | bytes 196616 | tf_op jit(solution)/shard_map/ppermute | solution.py:309
  28.9 1.9 %collective-permute-start.7 = (f32[128,128]{1,0:T(8,128)S(1)}, f32[128,128]{1,0:T(8,128)S(1)}, u32[]{:S(2)}, u32[]{:S(2)}) collective-permute-start(f32[128,128]{1,0:T(8,128)S(1)} %get-tuple-element.23), channel_id=1, source_target_pairs={{1,2},{2,1},{5,6},{6,5},{9,10},{10,9},{13,14},{14,13},{17,18},{18,... | collective-permute-start | bytes 196616 | tf_op jit(solution)/shard_map/ppermute | solution.py:309
  30.8 0.0 copy-done.6
  30.8 0.0 copy-done.7
  30.8 1.1 %inner_steps.1.inner_ref = f32[1024,128]{1,0:T(8,128)S(1)} custom-call(f32[1024,128]{1,0:T(8,128)S(1)} %bitcast.14, f32[512,128]{1,0:T(8,128)S(1)} %collective-permute-done.xa, f32[512,128]{1,0:T(8,128)S(1)} %collective-permute-done.1.xb, f32[512,128]{1,0:T(8,128)S(1)} %collective-permute-done.2.za, f32[512,128]{1,0:T(8,128)S(1)} %collective-permute-done.3.zb, ...), custom_call_target="tpu_custom_call" | custom-call | bytes 6000000 | tf_op jit(solution)/shard_map/inner_steps/pallas_call | solution.py:338
  31.9 0.0 collective-permute-done.4.ya
  31.9 0.2 collective-permute-done.5.yb
  32.1 1.0 %collective-permute-done.6.ea = f32[128,128]{1,0:T(8,128)S(1)} collective-permute-done((f32[128,128]{1,0:T(8,128)S(1)}, f32[128,128]{1,0:T(8,128)S(1)}, u32[]{:S(2)}, u32[]{:S(2)}) %collective-permute-start.6) | collective-permute-done | bytes 65568 | tf_op jit(solution)/shard_map/ppermute | solution.py:309
  33.1 1.9 %collective-permute-done.7.eb = f32[128,128]{1,0:T(8,128)S(1)} collective-permute-done((f32[128,128]{1,0:T(8,128)S(1)}, f32[128,128]{1,0:T(8,128)S(1)}, u32[]{:S(2)}, u32[]{:S(2)}) %collective-permute-start.7) | collective-permute-done | bytes 65568 | tf_op jit(solution)/shard_map/ppermute | solution.py:309
  35.0 0.0 copy-done.2
  35.0 0.0 copy-done.3
  35.0 0.0 copy-done.5
  35.1 2.1 %project.1 = (f32[1024,128]{1,0:T(8,128)S(1)}, f32[2064,1,128]{2,1,0:T(1,128)}) custom-call(s32[7]{0:T(128)S(1)} %bitcast.19, f32[2064,1,128]{2,1,0:T(1,128)} %bitcast.2.lanes_any, f32[1024,128]{1,0:T(8,128)S(1)} %inner_steps.1.inner_ref, f32[64,128]{1,0:T(8,128)S(1)} %get-tuple-element.18.low_ref, ...), custom_call_target="tpu_custom_call", output_to_operand_aliasing={{1}: (1, {})} | custom-call | bytes 6000000 | tf_op jit(solution)/shard_map/project/pallas_call | solution.py:339
  37.1 0.0 copy-start.9
  37.1 9.9 %all-to-all-start = ((f32[16,1,16512]{2,1,0:T(1,128)}), f32[16,1,16512]{2,1,0:T(1,128)S(1)}, u32[]{:S(2)}, u32[]{:S(2)}) async-start(f32[16,1,16512]{2,1,0:T(1,128)} %bitcast.9), calls=%async_computation | async-start | bytes 2113536 | tf_op jit(solution)/shard_map/all_to_all | solution.py:359
  47.1 0.0 copy-done.9
  47.1 0.1 copy.13.table_ref
  47.2 1.0 %finish_density.1 = f32[1024,128]{1,0:T(8,128)} custom-call(f32[1024,128]{1,0:T(8,128)S(1)} %get-tuple-element.24.cells_ref), custom_call_target="tpu_custom_call" | custom-call | bytes 6000000 | tf_op jit(solution)/shard_map/finish_density/pallas_call | solution.py:358
  48.2 23.7 %all-to-all-done = f32[16,1,16512]{2,1,0:T(1,128)S(1)} async-done(((f32[16,1,16512]{2,1,0:T(1,128)}), f32[16,1,16512]{2,1,0:T(1,128)S(1)}, u32[]{:S(2)}, u32[]{:S(2)}) %all-to-all-start) | async-done | bytes 1056800 | tf_op jit(solution)/shard_map/all_to_all | solution.py:359
  71.9 1.3 %gather_sky.1 = f32[384,128]{1,0:T(8,128)} custom-call(f32[2064,128]{1,0:T(8,128)S(1)} %bitcast.15, f32[96,64]{1,0:T(8,128)S(1)} %copy.13.table_ref), custom_call_target="tpu_custom_call" | custom-call | bytes 3000000 | tf_op jit(solution)/shard_map/gather_sky/pallas_call | solution.py:360
Async XLA Ops:
  0.6 1.0 %copy-start = (f32[64,4,4,128]{3,2,1,0:T(4,128)S(1)}, f32[64,4,4,128]{3,2,1,0:T(4,128)}, u32[]{:S(2)}) copy-start(f32[64,4,4,128]{3,2,1,0:T(4,128)} %param.8) | copy-start | bytes 1572868
  1.7 12.7 %copy-start.1 = (f32[64,4,4,128]{3,2,1,0:T(4,128)S(1)}, f32[64,4,4,128]{3,2,1,0:T(4,128)}, u32[]{:S(2)}) copy-start(f32[64,4,4,128]{3,2,1,0:T(4,128)} %param.8) | copy-start | bytes 1572868
  1.9 13.1 %collective-permute-start = (f32[512,128]{1,0:T(8,128)S(1)}, f32[512,128]{1,0:T(8,128)S(1)}, u32[]{:S(2)}, u32[]{:S(2)}) collective-permute-start(f32[512,128]{1,0:T(8,128)S(1)} %get-tuple-element.14), channel_id=1, source_target_pairs={{0,64},{64,0},{128,192},{192,128},{256,320},{320,256},{384,448},{4... | collective-permute-start | bytes 786440 | tf_op jit(solution)/shard_map/ppermute | solution.py:309
  3.8 15.8 %collective-permute-start.1 = (f32[512,128]{1,0:T(8,128)S(1)}, f32[512,128]{1,0:T(8,128)S(1)}, u32[]{:S(2)}, u32[]{:S(2)}) collective-permute-start(f32[512,128]{1,0:T(8,128)S(1)} %get-tuple-element.15), channel_id=1, source_target_pairs={{64,128},{128,64},{192,256},{256,192},{320,384},{384,320},{65,129}... | collective-permute-start | bytes 786440 | tf_op jit(solution)/shard_map/ppermute | solution.py:309
  6.3 13.3 %collective-permute-start.2 = (f32[512,128]{1,0:T(8,128)S(1)}, f32[512,128]{1,0:T(8,128)S(1)}, u32[]{:S(2)}, u32[]{:S(2)}) collective-permute-start(f32[512,128]{1,0:T(8,128)S(1)} %get-tuple-element.16), channel_id=1, source_target_pairs={{0,1},{1,0},{2,3},{3,2},{4,5},{5,4},{6,7},{7,6},{8,9},{9,8},{10,11... | collective-permute-start | bytes 786440 | tf_op jit(solution)/shard_map/ppermute | solution.py:309
  9.5 10.5 %collective-permute-start.3 = (f32[512,128]{1,0:T(8,128)S(1)}, f32[512,128]{1,0:T(8,128)S(1)}, u32[]{:S(2)}, u32[]{:S(2)}) collective-permute-start(f32[512,128]{1,0:T(8,128)S(1)} %get-tuple-element.17), channel_id=1, source_target_pairs={{1,2},{2,1},{5,6},{6,5},{9,10},{10,9},{13,14},{14,13},{17,18},{18,... | collective-permute-start | bytes 786440 | tf_op jit(solution)/shard_map/ppermute | solution.py:309
  11.5 0.7 copy-start.4
  12.1 0.7 copy-start.8
  12.8 18.0 %copy-start.6 = (f32[64]{0:T(128)S(1)}, f32[64]{0:T(128)}, u32[]{:S(2)}) copy-start(f32[64]{0:T(128)} %param.10) | copy-start | bytes 772
  12.8 18.0 %copy-start.7 = (f32[64]{0:T(128)S(1)}, f32[64]{0:T(128)}, u32[]{:S(2)}) copy-start(f32[64]{0:T(128)} %param.11) | copy-start | bytes 772
  14.4 20.6 %copy-start.2 = (bf16[1,1,1,7,2048,128]{5,4,3,2,1,0:T(8,128)(2,1)S(1)}, bf16[1,1,1,7,2048,128]{5,4,3,2,1,0:T(8,128)(2,1)}, u32[]{:S(2)}) copy-start(bf16[1,1,1,7,2048,128]{5,4,3,2,1,0:T(8,128)(2,1)} %param.13) | copy-start | bytes 11010052
  20.4 14.6 %copy-start.3 = (f32[4,4,128]{2,1,0:T(4,128)S(1)}, f32[4,4,128]{2,1,0:T(4,128)}, u32[]{:S(2)}) copy-start(f32[4,4,128]{2,1,0:T(4,128)} %param.9) | copy-start | bytes 24580
  20.4 14.6 %copy-start.5 = (s32[1,1,1,7,1]{3,4,2,1,0:T(1,128)S(1)}, s32[1,1,1,7,1]{3,4,2,1,0:T(1,128)}, u32[]{:S(2)}) copy-start(s32[1,1,1,7,1]{3,4,2,1,0:T(1,128)} %param.14) | copy-start | bytes 88
  20.5 11.4 %collective-permute-start.4 = (f32[128,128]{1,0:T(8,128)S(1)}, f32[128,128]{1,0:T(8,128)S(1)}, u32[]{:S(2)}, u32[]{:S(2)}) collective-permute-start(f32[128,128]{1,0:T(8,128)S(1)} %get-tuple-element.20), channel_id=1, source_target_pairs={{0,4},{4,0},{8,12},{12,8},{16,20},{20,16},{24,28},{28,24},{32,36},... | collective-permute-start | bytes 196616 | tf_op jit(solution)/shard_map/ppermute | solution.py:309
  23.9 8.3 %collective-permute-start.5 = (f32[128,128]{1,0:T(8,128)S(1)}, f32[128,128]{1,0:T(8,128)S(1)}, u32[]{:S(2)}, u32[]{:S(2)}) collective-permute-start(f32[128,128]{1,0:T(8,128)S(1)} %get-tuple-element.21), channel_id=1, source_target_pairs={{4,8},{8,4},{12,16},{16,12},{20,24},{24,20},{28,32},{32,28},{36,40... | collective-permute-start | bytes 196616 | tf_op jit(solution)/shard_map/ppermute | solution.py:309
  27.0 6.2 %collective-permute-start.6 = (f32[128,128]{1,0:T(8,128)S(1)}, f32[128,128]{1,0:T(8,128)S(1)}, u32[]{:S(2)}, u32[]{:S(2)}) collective-permute-start(f32[128,128]{1,0:T(8,128)S(1)} %get-tuple-element.22), channel_id=1, source_target_pairs={{0,1},{1,0},{2,3},{3,2},{4,5},{5,4},{6,7},{7,6},{8,9},{9,8},{10,11... | collective-permute-start | bytes 196616 | tf_op jit(solution)/shard_map/ppermute | solution.py:309
  28.9 6.2 %collective-permute-start.7 = (f32[128,128]{1,0:T(8,128)S(1)}, f32[128,128]{1,0:T(8,128)S(1)}, u32[]{:S(2)}, u32[]{:S(2)}) collective-permute-start(f32[128,128]{1,0:T(8,128)S(1)} %get-tuple-element.23), channel_id=1, source_target_pairs={{1,2},{2,1},{5,6},{6,5},{9,10},{10,9},{13,14},{14,13},{17,18},{18,... | collective-permute-start | bytes 196616 | tf_op jit(solution)/shard_map/ppermute | solution.py:309
  37.1 10.0 %copy-start.9 = (f32[96,64]{0,1:T(8,128)S(1)}, f32[96,64]{0,1:T(8,128)}, u32[]{:S(2)}) copy-start(f32[96,64]{0,1:T(8,128)} %param.12) | copy-start | bytes 73732
  37.1 34.8 %all-to-all-start = ((f32[16,1,16512]{2,1,0:T(1,128)}), f32[16,1,16512]{2,1,0:T(1,128)S(1)}, u32[]{:S(2)}, u32[]{:S(2)}) async-start(f32[16,1,16512]{2,1,0:T(1,128)} %bitcast.9), calls=%async_computation | async-start | bytes 2113536 | tf_op jit(solution)/shard_map/all_to_all | solution.py:359

commit v7 on v5

--- a/solution.py
+++ b/solution.py
@@ -261,23 +261,34 @@
         final_ref[pl.ds(zx, NE, stride=ZX), :] = tile(cells_ref, zx)
 
 
-def gather_sky(recv_ref, table_ref, sky_ref):
+def gather_sky(recv_ref, table_ref, sky_any, total_ref, sky_ref, sem):
     count = recv_ref.shape[0] // LANE
-    total = [jnp.zeros((NE, PB), jnp.float32) for _ in range(BO)]
     feeds = recv_ref[pl.ds(CAP * NE, count, stride=LANE), :]
     first = lax.broadcasted_iota(jnp.int32, (count, PB), 1) < PB // 2
     turned = pltpu.roll(feeds, PB // 2, 1)
     feeds = [jnp.where(first, feeds, turned), jnp.where(first, turned, feeds)]
-    for b in range(BO):
-        chosen = [jnp.where(rows == b, 1.0, 0.0) for rows in feeds]
+    chosen = [[jnp.where(rows == b, 1.0, 0.0) for b in range(BO)] for rows in feeds]
+    part = NE // 2
+    for at in range(0, NE, part):
+        total = [jnp.zeros((part, PB), jnp.float32) for _ in range(BO)]
         for j in range(count):
             for k in range(CAP):
-                block = recv_ref[j * LANE + k * NE:j * LANE + (k + 1) * NE, :]
-                total[b] = total[b] + block * chosen[k][j:j + 1, :]
+                row = j * LANE + k * NE + at
+                block = recv_ref[row:row + part, :]
+                for b in range(BO):
+                    total[b] = total[b] + block * chosen[k][b][j:j + 1, :]
+        for b in range(BO):
+            total_ref[b * NE + at:b * NE + at + part, :] = total[b]
+    copies = []
     for b in range(BO):
         sky_ref[b * NG:(b + 1) * NG, :] = jnp.dot(
-            table_ref[...], total[b], precision=lax.Precision.HIGHEST, preferred_element_type=jnp.float32
+            table_ref[...], tile(total_ref, b), precision=lax.Precision.HIGHEST, preferred_element_type=jnp.float32
         )
+        rows = pl.ds(b * NG, NG)
+        copies.append(pltpu.make_async_copy(sky_ref.at[rows], sky_any.at[rows], sem.at[b]))
+        copies[b].start()
+    for copy in copies:
+        copy.wait()
 
 
 def f32(*shape):
@@ -357,7 +368,17 @@
     )
     (final,) = call(finish_density, "finish_density", [f32(NE * ZX, CY)], [VMEM], 2)(cells)
     recv = lax.all_to_all(send.reshape(owners, 1, LANE * PB), "gy", 0, 0, tiled=True)
-    (sky,) = call(gather_sky, "gather_sky", [f32(BO * NG, PB)], [VMEM] * 2, 1)(
+    (sky,) = call(
+        gather_sky,
+        "gather_sky",
+        [f32(BO * NG, PB)],
+        [VMEM] * 2,
+        1,
+        out_specs=[ANY],
+        scratch=[
+            pltpu.VMEM((BO * NE, PB), jnp.float32), pltpu.VMEM((BO * NG, PB), jnp.float32), pltpu.SemaphoreType.DMA((BO,))
+        ],
+    )(
         recv.reshape(owners * LANE, PB), pi0_table
     )
     return final.reshape(cr_init.shape), sky.reshape(1, 1, BO, NG, PB)

time: 73.8 us -> 73.8 us (level)
  no operation moved by 1% of the time
where the time goes in v7:
time: 73.8 us; the launch traced here: 73.2 us
  waiting for transfers between devices  31.9 us (43%)
  starting transfers between devices  29.8 us (40%)
  Pallas kernels  8.23 us (11%)
  local copies, waits for them, and re-layouts  2.46 us (3%)
  between operations  0.84 us (1%)
    all_to_all x1, waiting for transfers between devices, body(): lax.all_to_all(send.reshape(owners, 1, LANE * PB), 'gy', 0, 0, tiled=True)  23.7 us
    ppermute x8, starting transfers between devices, swap(): return lax.ppermute(values, axis, pairs)  19.9 us
    all_to_all x1, starting transfers between devices, body(): lax.all_to_all(send.reshape(owners, 1, LANE * PB), 'gy', 0, 0, tiled=True)  9.91 us
    ppermute x8, waiting for transfers between devices, swap(): return lax.ppermute(values, axis, pairs)  8.18 us
    unnamed x21, local copies, waits for them, and re-layouts  2.46 us
    pallas_call x1, Pallas kernels, body(): call(project, 'project', [f32(ZX * NE, CY), f32(owners * LANE, 1, PB)], [...  2.06 us
    pallas_call x1, Pallas kernels, body(): call(blank_lanes, 'blank_lanes', [f32(owners * LANE, PB)], [ANY] * 2, 1,...  1.59 us
  transfers between devices with their start and end apart: 9, of which 6 were waited for; matrix products, arithmetic and copies ran while one was open for 0% of the time, Pallas kernels for 6%

profile of v7, /device:TPU:336, one launch (start us, length us, event | category | flops | bytes accessed | tf_op | source)
XLA Modules:
  0.0 73.2 jit_solution(10542930149956389604)
XLA Ops:
  0.6 0.0 copy-start
  0.6 1.0 %copy-done = f32[64,4,4,128]{3,2,1,0:T(4,128)S(1)} copy-done((f32[64,4,4,128]{3,2,1,0:T(4,128)S(1)}, f32[64,4,4,128]{3,2,1,0:T(4,128)}, u32[]{:S(2)}) %copy-start) | copy-done | bytes 524312
  1.7 0.0 copy-start.1
  1.7 0.2 first_faces.1
  1.9 1.9 %collective-permute-start = (f32[512,128]{1,0:T(8,128)S(1)}, f32[512,128]{1,0:T(8,128)S(1)}, u32[]{:S(2)}, u32[]{:S(2)}) collective-permute-start(f32[512,128]{1,0:T(8,128)S(1)} %get-tuple-element.14), channel_id=1, source_target_pairs={{0,64},{64,0},{128,192},{192,128},{256,320},{320,256},{384,448},{4... | collective-permute-start | bytes 786440 | tf_op jit(solution)/shard_map/ppermute | solution.py:320
  3.8 2.6 %collective-permute-start.1 = (f32[512,128]{1,0:T(8,128)S(1)}, f32[512,128]{1,0:T(8,128)S(1)}, u32[]{:S(2)}, u32[]{:S(2)}) collective-permute-start(f32[512,128]{1,0:T(8,128)S(1)} %get-tuple-element.15), channel_id=1, source_target_pairs={{64,128},{128,64},{192,256},{256,192},{320,384},{384,320},{65,129}... | collective-permute-start | bytes 786440 | tf_op jit(solution)/shard_map/ppermute | solution.py:320
  6.3 3.2 %collective-permute-start.2 = (f32[512,128]{1,0:T(8,128)S(1)}, f32[512,128]{1,0:T(8,128)S(1)}, u32[]{:S(2)}, u32[]{:S(2)}) collective-permute-start(f32[512,128]{1,0:T(8,128)S(1)} %get-tuple-element.16), channel_id=1, source_target_pairs={{0,1},{1,0},{2,3},{3,2},{4,5},{5,4},{6,7},{7,6},{8,9},{9,8},{10,11... | collective-permute-start | bytes 786440 | tf_op jit(solution)/shard_map/ppermute | solution.py:320
  9.5 1.9 %collective-permute-start.3 = (f32[512,128]{1,0:T(8,128)S(1)}, f32[512,128]{1,0:T(8,128)S(1)}, u32[]{:S(2)}, u32[]{:S(2)}) collective-permute-start(f32[512,128]{1,0:T(8,128)S(1)} %get-tuple-element.17), channel_id=1, source_target_pairs={{1,2},{2,1},{5,6},{6,5},{9,10},{10,9},{13,14},{14,13},{17,18},{18,... | collective-permute-start | bytes 786440 | tf_op jit(solution)/shard_map/ppermute | solution.py:320
  11.5 0.0 copy-start.4
  11.5 0.6 copy-done.4
  12.1 0.0 copy-start.8
  12.1 0.7 copy-done.8
  12.8 0.0 copy-start.6
  12.8 0.0 copy-start.7
  12.8 1.6 %blank_lanes.1.blank_any = f32[2064,128]{1,0:T(8,128)} custom-call(s32[7]{0:T(128)S(1)} %bitcast.18, s32[7]{0:T(128)S(1)} %bitcast.24), custom_call_target="tpu_custom_call" | custom-call | bytes 3000000 | tf_op jit(solution)/shard_map/blank_lanes/pallas_call | solution.py:333
  14.4 0.0 copy-done.1
  14.4 0.0 copy-start.2
  14.4 0.6 own_columns.1
  15.0 0.0 collective-permute-done.xa
  15.0 4.6 %collective-permute-done.1.xb = f32[512,128]{1,0:T(8,128)S(1)} collective-permute-done((f32[512,128]{1,0:T(8,128)S(1)}, f32[512,128]{1,0:T(8,128)S(1)}, u32[]{:S(2)}, u32[]{:S(2)}) %collective-permute-start.1) | collective-permute-done | bytes 262176 | tf_op jit(solution)/shard_map/ppermute | solution.py:320
  19.6 0.0 collective-permute-done.2.za
  19.6 0.5 collective-permute-done.3.zb
  20.1 0.3 edge_faces.1
  20.4 0.0 copy-start.3
  20.4 0.0 copy-start.5
  20.5 3.4 %collective-permute-start.4 = (f32[128,128]{1,0:T(8,128)S(1)}, f32[128,128]{1,0:T(8,128)S(1)}, u32[]{:S(2)}, u32[]{:S(2)}) collective-permute-start(f32[128,128]{1,0:T(8,128)S(1)} %get-tuple-element.20), channel_id=1, source_target_pairs={{0,4},{4,0},{8,12},{12,8},{16,20},{20,16},{24,28},{28,24},{32,36},... | collective-permute-start | bytes 196616 | tf_op jit(solution)/shard_map/ppermute | solution.py:320
  23.9 3.1 %collective-permute-start.5 = (f32[128,128]{1,0:T(8,128)S(1)}, f32[128,128]{1,0:T(8,128)S(1)}, u32[]{:S(2)}, u32[]{:S(2)}) collective-permute-start(f32[128,128]{1,0:T(8,128)S(1)} %get-tuple-element.21), channel_id=1, source_target_pairs={{4,8},{8,4},{12,16},{16,12},{20,24},{24,20},{28,32},{32,28},{36,40... | collective-permute-start | bytes 196616 | tf_op jit(solution)/shard_map/ppermute | solution.py:320
  27.0 1.9 %collective-permute-start.6 = (f32[128,128]{1,0:T(8,128)S(1)}, f32[128,128]{1,0:T(8,128)S(1)}, u32[]{:S(2)}, u32[]{:S(2)}) collective-permute-start(f32[128,128]{1,0:T(8,128)S(1)} %get-tuple-element.22), channel_id=1, source_target_pairs={{0,1},{1,0},{2,3},{3,2},{4,5},{5,4},{6,7},{7,6},{8,9},{9,8},{10,11... | collective-permute-start | bytes 196616 | tf_op jit(solution)/shard_map/ppermute | solution.py:320
  28.9 1.9 %collective-permute-start.7 = (f32[128,128]{1,0:T(8,128)S(1)}, f32[128,128]{1,0:T(8,128)S(1)}, u32[]{:S(2)}, u32[]{:S(2)}) collective-permute-start(f32[128,128]{1,0:T(8,128)S(1)} %get-tuple-element.23), channel_id=1, source_target_pairs={{1,2},{2,1},{5,6},{6,5},{9,10},{10,9},{13,14},{14,13},{17,18},{18,... | collective-permute-start | bytes 196616 | tf_op jit(solution)/shard_map/ppermute | solution.py:320
  30.8 0.0 copy-done.6
  30.8 0.0 copy-done.7
  30.8 1.1 %inner_steps.1.inner_ref = f32[1024,128]{1,0:T(8,128)S(1)} custom-call(f32[1024,128]{1,0:T(8,128)S(1)} %bitcast.14, f32[512,128]{1,0:T(8,128)S(1)} %collective-permute-done.xa, f32[512,128]{1,0:T(8,128)S(1)} %collective-permute-done.1.xb, f32[512,128]{1,0:T(8,128)S(1)} %collective-permute-done.2.za, f32[512,128]{1,0:T(8,128)S(1)} %collective-permute-done.3.zb, ...), custom_call_target="tpu_custom_call" | custom-call | bytes 6000000 | tf_op jit(solution)/shard_map/inner_steps/pallas_call | solution.py:349
  31.9 0.0 collective-permute-done.4.ya
  32.0 0.2 collective-permute-done.5.yb
  32.1 1.0 %collective-permute-done.6.ea = f32[128,128]{1,0:T(8,128)S(1)} collective-permute-done((f32[128,128]{1,0:T(8,128)S(1)}, f32[128,128]{1,0:T(8,128)S(1)}, u32[]{:S(2)}, u32[]{:S(2)}) %collective-permute-start.6) | collective-permute-done | bytes 65568 | tf_op jit(solution)/shard_map/ppermute | solution.py:320
  33.1 1.9 %collective-permute-done.7.eb = f32[128,128]{1,0:T(8,128)S(1)} collective-permute-done((f32[128,128]{1,0:T(8,128)S(1)}, f32[128,128]{1,0:T(8,128)S(1)}, u32[]{:S(2)}, u32[]{:S(2)}) %collective-permute-start.7) | collective-permute-done | bytes 65568 | tf_op jit(solution)/shard_map/ppermute | solution.py:320
  35.0 0.0 copy-done.2
  35.0 0.0 copy-done.3
  35.0 0.0 copy-done.5
  35.1 2.1 %project.1 = (f32[1024,128]{1,0:T(8,128)S(1)}, f32[2064,1,128]{2,1,0:T(1,128)}) custom-call(s32[7]{0:T(128)S(1)} %bitcast.19, f32[2064,1,128]{2,1,0:T(1,128)} %bitcast.2.lanes_any, f32[1024,128]{1,0:T(8,128)S(1)} %inner_steps.1.inner_ref, f32[64,128]{1,0:T(8,128)S(1)} %get-tuple-element.18.low_ref, ...), custom_call_target="tpu_custom_call", output_to_operand_aliasing={{1}: (1, {})} | custom-call | bytes 6000000 | tf_op jit(solution)/shard_map/project/pallas_call | solution.py:350
  37.1 0.0 copy-start.9
  37.1 9.9 %all-to-all-start = ((f32[16,1,16512]{2,1,0:T(1,128)}), f32[16,1,16512]{2,1,0:T(1,128)S(1)}, u32[]{:S(2)}, u32[]{:S(2)}) async-start(f32[16,1,16512]{2,1,0:T(1,128)} %bitcast.9), calls=%async_computation | async-start | bytes 2113536 | tf_op jit(solution)/shard_map/all_to_all | solution.py:370
  47.0 0.0 copy-done.9
  47.0 0.1 copy.13.table_ref
  47.1 1.0 %finish_density.1 = f32[1024,128]{1,0:T(8,128)} custom-call(f32[1024,128]{1,0:T(8,128)S(1)} %get-tuple-element.24.cells_ref), custom_call_target="tpu_custom_call" | custom-call | bytes 6000000 | tf_op jit(solution)/shard_map/finish_density/pallas_call | solution.py:369
  48.2 23.7 %all-to-all-done = f32[16,1,16512]{2,1,0:T(1,128)S(1)} async-done(((f32[16,1,16512]{2,1,0:T(1,128)}), f32[16,1,16512]{2,1,0:T(1,128)S(1)}, u32[]{:S(2)}, u32[]{:S(2)}) %all-to-all-start) | async-done | bytes 1056800 | tf_op jit(solution)/shard_map/all_to_all | solution.py:370
  71.9 1.3 %gather_sky.1 = f32[384,128]{1,0:T(8,128)} custom-call(f32[2064,128]{1,0:T(8,128)S(1)} %bitcast.15, f32[96,64]{1,0:T(8,128)S(1)} %copy.13.table_ref), custom_call_target="tpu_custom_call" | custom-call | bytes 3000000 | tf_op jit(solution)/shard_map/gather_sky/pallas_call | solution.py:371
Async XLA Ops:
  0.6 1.0 %copy-start = (f32[64,4,4,128]{3,2,1,0:T(4,128)S(1)}, f32[64,4,4,128]{3,2,1,0:T(4,128)}, u32[]{:S(2)}) copy-start(f32[64,4,4,128]{3,2,1,0:T(4,128)} %param.8) | copy-start | bytes 1572868
  1.7 12.7 %copy-start.1 = (f32[64,4,4,128]{3,2,1,0:T(4,128)S(1)}, f32[64,4,4,128]{3,2,1,0:T(4,128)}, u32[]{:S(2)}) copy-start(f32[64,4,4,128]{3,2,1,0:T(4,128)} %param.8) | copy-start | bytes 1572868
  1.9 13.1 %collective-permute-start = (f32[512,128]{1,0:T(8,128)S(1)}, f32[512,128]{1,0:T(8,128)S(1)}, u32[]{:S(2)}, u32[]{:S(2)}) collective-permute-start(f32[512,128]{1,0:T(8,128)S(1)} %get-tuple-element.14), channel_id=1, source_target_pairs={{0,64},{64,0},{128,192},{192,128},{256,320},{320,256},{384,448},{4... | collective-permute-start | bytes 786440 | tf_op jit(solution)/shard_map/ppermute | solution.py:320
  3.8 15.8 %collective-permute-start.1 = (f32[512,128]{1,0:T(8,128)S(1)}, f32[512,128]{1,0:T(8,128)S(1)}, u32[]{:S(2)}, u32[]{:S(2)}) collective-permute-start(f32[512,128]{1,0:T(8,128)S(1)} %get-tuple-element.15), channel_id=1, source_target_pairs={{64,128},{128,64},{192,256},{256,192},{320,384},{384,320},{65,129}... | collective-permute-start | bytes 786440 | tf_op jit(solution)/shard_map/ppermute | solution.py:320
  6.3 13.3 %collective-permute-start.2 = (f32[512,128]{1,0:T(8,128)S(1)}, f32[512,128]{1,0:T(8,128)S(1)}, u32[]{:S(2)}, u32[]{:S(2)}) collective-permute-start(f32[512,128]{1,0:T(8,128)S(1)} %get-tuple-element.16), channel_id=1, source_target_pairs={{0,1},{1,0},{2,3},{3,2},{4,5},{5,4},{6,7},{7,6},{8,9},{9,8},{10,11... | collective-permute-start | bytes 786440 | tf_op jit(solution)/shard_map/ppermute | solution.py:320
  9.5 10.5 %collective-permute-start.3 = (f32[512,128]{1,0:T(8,128)S(1)}, f32[512,128]{1,0:T(8,128)S(1)}, u32[]{:S(2)}, u32[]{:S(2)}) collective-permute-start(f32[512,128]{1,0:T(8,128)S(1)} %get-tuple-element.17), channel_id=1, source_target_pairs={{1,2},{2,1},{5,6},{6,5},{9,10},{10,9},{13,14},{14,13},{17,18},{18,... | collective-permute-start | bytes 786440 | tf_op jit(solution)/shard_map/ppermute | solution.py:320
  11.5 0.7 copy-start.4
  12.1 0.7 copy-start.8
  12.8 18.0 %copy-start.6 = (f32[64]{0:T(128)S(1)}, f32[64]{0:T(128)}, u32[]{:S(2)}) copy-start(f32[64]{0:T(128)} %param.10) | copy-start | bytes 772
  12.8 18.0 %copy-start.7 = (f32[64]{0:T(128)S(1)}, f32[64]{0:T(128)}, u32[]{:S(2)}) copy-start(f32[64]{0:T(128)} %param.11) | copy-start | bytes 772
  14.4 20.6 %copy-start.2 = (bf16[1,1,1,7,2048,128]{5,4,3,2,1,0:T(8,128)(2,1)S(1)}, bf16[1,1,1,7,2048,128]{5,4,3,2,1,0:T(8,128)(2,1)}, u32[]{:S(2)}) copy-start(bf16[1,1,1,7,2048,128]{5,4,3,2,1,0:T(8,128)(2,1)} %param.13) | copy-start | bytes 11010052
  20.4 14.6 %copy-start.3 = (f32[4,4,128]{2,1,0:T(4,128)S(1)}, f32[4,4,128]{2,1,0:T(4,128)}, u32[]{:S(2)}) copy-start(f32[4,4,128]{2,1,0:T(4,128)} %param.9) | copy-start | bytes 24580
  20.4 14.6 %copy-start.5 = (s32[1,1,1,7,1]{3,4,2,1,0:T(1,128)S(1)}, s32[1,1,1,7,1]{3,4,2,1,0:T(1,128)}, u32[]{:S(2)}) copy-start(s32[1,1,1,7,1]{3,4,2,1,0:T(1,128)} %param.14) | copy-start | bytes 88
  20.5 11.5 %collective-permute-start.4 = (f32[128,128]{1,0:T(8,128)S(1)}, f32[128,128]{1,0:T(8,128)S(1)}, u32[]{:S(2)}, u32[]{:S(2)}) collective-permute-start(f32[128,128]{1,0:T(8,128)S(1)} %get-tuple-element.20), channel_id=1, source_target_pairs={{0,4},{4,0},{8,12},{12,8},{16,20},{20,16},{24,28},{28,24},{32,36},... | collective-permute-start | bytes 196616 | tf_op jit(solution)/shard_map/ppermute | solution.py:320
  23.9 8.3 %collective-permute-start.5 = (f32[128,128]{1,0:T(8,128)S(1)}, f32[128,128]{1,0:T(8,128)S(1)}, u32[]{:S(2)}, u32[]{:S(2)}) collective-permute-start(f32[128,128]{1,0:T(8,128)S(1)} %get-tuple-element.21), channel_id=1, source_target_pairs={{4,8},{8,4},{12,16},{16,12},{20,24},{24,20},{28,32},{32,28},{36,40... | collective-permute-start | bytes 196616 | tf_op jit(solution)/shard_map/ppermute | solution.py:320
  27.0 6.2 %collective-permute-start.6 = (f32[128,128]{1,0:T(8,128)S(1)}, f32[128,128]{1,0:T(8,128)S(1)}, u32[]{:S(2)}, u32[]{:S(2)}) collective-permute-start(f32[128,128]{1,0:T(8,128)S(1)} %get-tuple-element.22), channel_id=1, source_target_pairs={{0,1},{1,0},{2,3},{3,2},{4,5},{5,4},{6,7},{7,6},{8,9},{9,8},{10,11... | collective-permute-start | bytes 196616 | tf_op jit(solution)/shard_map/ppermute | solution.py:320
  28.9 6.2 %collective-permute-start.7 = (f32[128,128]{1,0:T(8,128)S(1)}, f32[128,128]{1,0:T(8,128)S(1)}, u32[]{:S(2)}, u32[]{:S(2)}) collective-permute-start(f32[128,128]{1,0:T(8,128)S(1)} %get-tuple-element.23), channel_id=1, source_target_pairs={{1,2},{2,1},{5,6},{6,5},{9,10},{10,9},{13,14},{14,13},{17,18},{18,... | collective-permute-start | bytes 196616 | tf_op jit(solution)/shard_map/ppermute | solution.py:320
  37.1 9.9 %copy-start.9 = (f32[96,64]{0,1:T(8,128)S(1)}, f32[96,64]{0,1:T(8,128)}, u32[]{:S(2)}) copy-start(f32[96,64]{0,1:T(8,128)} %param.12) | copy-start | bytes 73732
  37.1 34.8 %all-to-all-start = ((f32[16,1,16512]{2,1,0:T(1,128)}), f32[16,1,16512]{2,1,0:T(1,128)S(1)}, u32[]{:S(2)}, u32[]{:S(2)}) async-start(f32[16,1,16512]{2,1,0:T(1,128)} %bitcast.9), calls=%async_computation | async-start | bytes 2113536 | tf_op jit(solution)/shard_map/all_to_all | solution.py:370
